TPU v7x, 768 devices: a whole 4x8x12 slice. The times are simulated.
768 devices in a mesh: replica: 24 (over z, y_lo), shard: 4 (over x), tensor: 8 (over y_hi, core).
Axes of the slice: x: 4, y: 8 (y_hi: 4, y_lo: 2; y = y_hi * 2 + y_lo), z: 12, core: 2. Of those that a mesh axis runs over, the one named last changes fastest.
Arguments:
- inputs: bfloat16 [12288, 8192], P(('replica', 'shard')), may hold values from -0.59765625 to 0.59765625
- gain: bfloat16 [8192], replicated, may hold values from 0.099609375 to 1.8984375
- value_weight: bfloat16 [8192, 2048], P('shard', 'tensor'), may hold values from -0.0625 to 0.0625
- value_cot: bfloat16 [12288, 2048], P(('replica', 'shard'), 'tensor'), may hold values from -0.5 to 0.5
- pseudo_grad: float32 [24, 2048, 3072], P('replica', ('shard', 'tensor')), may hold values from -6 to 6
- global_params: float32 [2048, 3072], P(('shard', 'tensor'), 'replica'), may hold values from -6 to 6
- momentum: float32 [2048, 3072], P(('shard', 'tensor'), 'replica'), may hold values from -3 to 3
Outputs:
- values: bfloat16 [12288, 2048], P(('replica', 'shard'), 'tensor')
- weight_grad: bfloat16 [24, 8192, 2048], P('replica', 'shard', 'tensor')
- input_grad: bfloat16 [12288, 8192], P(('replica', 'shard', 'tensor'))
- new_global: float32 [2048, 3072], P(('shard', 'tensor'), 'replica')
- new_momentum: float32 [2048, 3072], P(('shard', 'tensor'), 'replica')
All inputs are finite; a program needn't handle non-finite values.
Results may differ from a plain program's by a relative error of at most 0.014.
Values may be sent and summed in bfloat16 or wider, within the bound.
No kernel may reach another device: no remote copies, remote signals or barrier semaphores. Data moves between devices by JAX's collectives and lax.ppermute only.
A program may use at most 64 MiB of HBM per device.

v0:
```python
import jax
import jax.numpy as jnp
from jax import lax
from jax.sharding import PartitionSpec as P

norm_epsilon = 1e-05
outer_rate = 0.7
outer_beta = 0.9


def body(inputs, gain, value_weight, value_cot, pseudo_grad, global_params, momentum):
    wide_inputs = inputs.astype(jnp.float32)
    inv_scale = lax.rsqrt(jnp.mean(wide_inputs * wide_inputs, axis=1, keepdims=True) + norm_epsilon)
    gain_wide = gain.astype(jnp.float32)
    normed = (wide_inputs * inv_scale * gain_wide).astype(jnp.bfloat16)
    tokens, model_width = normed.shape
    tensor_count = lax.axis_size("tensor")
    share_rows = tokens // tensor_count
    first_row = lax.axis_index("tensor") * share_rows
    weight_piece = lax.all_gather(value_weight, "shard", axis=0, tiled=True)
    segment = normed
    partial_values = jnp.dot(segment, weight_piece, preferred_element_type=jnp.float32)
    product = lax.dot_general(
        value_cot, weight_piece, (((1,), (1,)), ((), ())), preferred_element_type=jnp.float32
    )
    hidden = product
    values, hidden = (partial_values, hidden)
    summed = lax.psum_scatter(
        hidden.astype(jnp.bfloat16), "tensor", scatter_dimension=0, tiled=True
    ).astype(jnp.float32)
    segment = normed
    weight_grad = lax.psum_scatter(
        lax.dot_general(
            segment, value_cot, (((0,), (0,)), ((), ())), preferred_element_type=jnp.float32
        ).astype(jnp.bfloat16),
        "shard",
        scatter_dimension=0,
        tiled=True,
    )[None]
    input_rows = lax.dynamic_slice_in_dim(wide_inputs, first_row, share_rows, 0)
    scale_rows = lax.dynamic_slice_in_dim(inv_scale, first_row, share_rows, 0)
    scaled = gain_wide * summed
    inner_mean = jnp.mean(input_rows * scaled, axis=1, keepdims=True)
    cubed = scale_rows * scale_rows * scale_rows
    input_grad = (scale_rows * scaled - input_rows * cubed * inner_mean).astype(jnp.bfloat16)
    local_grad = pseudo_grad[0]
    replicas = lax.axis_size("replica")
    summed_grad = lax.psum(local_grad.astype(jnp.bfloat16), "replica").astype(jnp.float32)
    own_cols = momentum.shape[1]
    summed_grad = lax.dynamic_slice_in_dim(
        summed_grad, lax.axis_index("replica") * own_cols, own_cols, 1
    )
    average = summed_grad / replicas
    new_momentum = outer_beta * momentum + average
    new_global = global_params - outer_rate * (average + outer_beta * new_momentum)
    return (values.astype(jnp.bfloat16), weight_grad, input_grad, new_global, new_momentum)


def solution(mesh):
    placed = (
        P(("replica", "shard"), None),
        P(),
        P("shard", "tensor"),
        P(("replica", "shard"), "tensor"),
        P("replica", ("shard", "tensor"), None),
        P(("shard", "tensor"), "replica"),
        P(("shard", "tensor"), "replica"),
    )
    return jax.shard_map(
        body,
        mesh=mesh,
        in_specs=placed,
        out_specs=(
            P(("replica", "shard"), "tensor"),
            P("replica", "shard", "tensor"),
            P(("replica", "shard", "tensor"), None),
            P(("shard", "tensor"), "replica"),
            P(("shard", "tensor"), "replica"),
        ),
        check_vma=False,
    )
```

profile of v0, /device:TPU:2, one launch (start us, length us, event | category | flops | bytes accessed | tf_op | source)
XLA Modules:
  0.0 245.0 jit_solution(15060938265644887843)
XLA Ops:
  8.0 0.0 copy-start
  8.0 0.0 all-gather.2.cloned.1.call-start
  8.1 0.7 all-gather.2.cloned.1.call-update
  8.7 0.0 all-reduce.2.cloned.1.call-start
  8.8 1.9 convert_bitcast_fusion
  10.7 0.0 all-reduce.2.cloned.1.call-update
  10.8 0.0 copy-start.4
  10.8 0.0 copy-start.1
  10.8 0.0 reduce-scatter.5.cloned.1.call-start
  10.8 62.8 %all-gather.2.cloned.1.call-done = bf16[8192,256]{1,0:T(8,128)(2,1)} async-done(((bf16[2048,256]{1,0:T(8,128)(2,1)}), bf16[8192,256]{1,0:T(8,128)(2,1)}) %all-gather.2.cloned.1.call-update) | async-done | bytes 4194320 | tf_op jit(solution)/shard_map/all_gather | solution.py:20
  73.6 0.0 copy-done
  73.6 5.0 %convolution_convert_fusion.1 = bf16[128,8192]{1,0:T(8,128)(2,1)} fusion(bf16[128,256]{1,0:T(8,128)(2,1)S(1)} %copy-done, bf16[8192,256]{1,0:T(8,128)(2,1)} %all-gather.2.cloned.1.call-done), kind=kOutput, calls=%fused_computation.1 | convolution fusion | flops 537919488 | bytes 6356992 | tf_op jit(solution)/shard_map/dot_general | solution.py:23
  78.6 0.0 reduce-scatter.5.cloned.1.call-update
  78.7 0.0 reduce-scatter.3.cloned.1.call-start
  78.7 0.0 copy-done.4
  78.7 0.0 copy-done.1
  78.7 0.5 multiply_reduce_fusion
  79.2 3.4 %convolution_convert_fusion = bf16[8192,256]{1,0:T(8,128)(2,1)} fusion(bf16[128,256]{1,0:T(8,128)(2,1)S(1)} %copy-done, f32[8192]{0:T(1024)S(1)} %convert_element_type.34, f32[128]{0:T(128)S(1)} %add_rsqrt_fusion, bf16[128,8192]{1,0:T(8,128)(2,1)S(1)} %copy-done.1), kind=kOutput, calls=%fused_computation | convolution fusion | flops 543162368 | bytes 6390272 | tf_op jit(solution)/shard_map/dot_general | solution.py:33
  82.6 0.0 reduce-scatter.3.cloned.1.call-update
  82.7 0.0 copy-start.2
  82.7 0.0 copy-start.3
  82.7 2.4 convert_element_type.33
  85.1 0.1 fusion
  85.1 144.5 %all-reduce.2.cloned.1.call-done = bf16[64,3072]{1,0:T(8,128)(2,1)} async-done(((bf16[64,3072]{1,0:T(8,128)(2,1)}), bf16[64,3072]{1,0:T(8,128)(2,1)}) %all-reduce.2.cloned.1.call-update) | async-done | bytes 393232 | tf_op jit(solution)/shard_map/psum | solution.py:48
  229.6 0.0 copy-done.2
  229.6 0.0 copy-done.3
  229.6 1.4 multiply_subtract_fusion
  230.9 3.6 %convolution_convert_fusion.2 = bf16[128,256]{1,0:T(8,128)(2,1)} fusion(bf16[8192,256]{1,0:T(8,128)(2,1)} %all-gather.2.cloned.1.call-done, f32[8192]{0:T(1024)S(1)} %convert_element_type.34, f32[128]{0:T(128)S(1)} %add_rsqrt_fusion, bf16[128,8192]{1,0:T(8,128)(2,1)S(1)} %copy-done.1), kind=kOutput, calls=%fused_computation.4 | convolution fusion | flops 541097984 | bytes 6390272 | tf_op jit(solution)/shard_map/dot_general | solution.py:22
  234.5 0.0 reduce-scatter.5.cloned.1.call-done
  234.5 1.3 multiply_reduce_fusion.1
  235.8 2.0 subtract_convert_fusion
  237.8 0.0 reduce-scatter.3.cloned.1.call-done
  (3 shorter events, 0.0 us)
Async XLA Ops:
  8.0 65.6 %copy-start = (bf16[128,256]{1,0:T(8,128)(2,1)S(1)}, bf16[128,256]{1,0:T(8,128)(2,1)}, u32[]{:S(2)}) copy-start(bf16[128,256]{1,0:T(8,128)(2,1)} %param.10) | copy-start | bytes 196612
  8.0 65.6 %all-gather.2.cloned.1.call-start = ((), (), s32[]{:S(2)}) async-start(), calls=%async_computation.2 | async-start | bytes 5242880 | tf_op jit(solution)/shard_map/all_gather | solution.py:20
  8.7 220.8 %all-reduce.2.cloned.1.call-start = ((), (), s32[]{:S(2)}) async-start(), calls=%async_computation.5 | async-start | bytes 786432 | tf_op jit(solution)/shard_map/psum | solution.py:48
  10.8 67.9 %copy-start.4 = (bf16[8192]{0:T(1024)(128)(2,1)S(1)}, bf16[8192]{0:T(1024)(128)(2,1)}, u32[]{:S(2)}) copy-start(bf16[8192]{0:T(1024)(128)(2,1)} %param.8) | copy-start | bytes 49156
  10.8 68.0 %copy-start.1 = (bf16[128,8192]{1,0:T(8,128)(2,1)S(1)}, bf16[128,8192]{1,0:T(8,128)(2,1)}, u32[]{:S(2)}) copy-start(bf16[128,8192]{1,0:T(8,128)(2,1)} %param.7) | copy-start | bytes 6291460
  10.8 223.8 %reduce-scatter.5.cloned.1.call-start = ((), (), s32[]{:S(2)}) async-start(), calls=%async_computation.4 | async-start | bytes 2359296 | tf_op jit(solution)/shard_map/reduce_scatter | solution.py:28
  78.7 159.2 %reduce-scatter.3.cloned.1.call-start = ((), (), s32[]{:S(2)}) async-start(), calls=%async_computation.3 | async-start | bytes 5242880 | tf_op jit(solution)/shard_map/reduce_scatter | solution.py:32
  82.7 146.9 %copy-start.2 = (f32[64,128]{1,0:T(8,128)S(1)}, f32[64,128]{1,0:T(8,128)}, u32[]{:S(2)}) copy-start(f32[64,128]{1,0:T(8,128)} %param.12) | copy-start | bytes 98308
  82.7 146.9 %copy-start.3 = (f32[64,128]{1,0:T(8,128)S(1)}, f32[64,128]{1,0:T(8,128)}, u32[]{:S(2)}) copy-start(f32[64,128]{1,0:T(8,128)} %param.13) | copy-start | bytes 98308
Sparse Core Ops, SparseCore 0:
  11.2 62.3 all-gather.1
  78.8 50.6 reduce-scatter.4
  133.2 53.9 reduce-scatter.2
Sparse Core Ops, SparseCore 1:
  12.4 217.1 all-reduce.1
where the time goes:
time: 245 us
  waiting for transfers between devices  208 us (85%)
  between operations  15.3 us (6%)
  matrix products  12 us (5%)
  other arithmetic  9.52 us (4%)
    psum x1, waiting for transfers between devices, body(): lax.psum(local_grad.astype(jnp.bfloat16), 'replica').astype(jnp.float32)  144 us
    all_gather x1, waiting for transfers between devices, body(): weight_piece = lax.all_gather(value_weight, 'shard', axis=0, tiled=True)  62.8 us
    dot_general x1, matrix products, body(): lax.dot_general(value_cot, weight_piece, (((1,), (1,)), ((), ())), prefer...  5.03 us
  transfers between devices with their start and end apart: 4, of which 2 were waited for; matrix products, arithmetic and copies ran while one was open for 9% of the time, Pallas kernels for 0%

commit v1 on v0

v1 whole, which is shorter than its diff:
```python
import jax
import jax.numpy as jnp
from jax import lax
from jax.sharding import PartitionSpec as P

norm_epsilon = 1e-05
outer_rate = 0.7
outer_beta = 0.9
CORES = 2


def body(inputs, gain, value_weight, value_cot, pseudo_grad, global_params, momentum):
    shards = lax.axis_size("shard")
    tensors = lax.axis_size("tensor")
    replicas = lax.axis_size("replica")
    tokens, width = inputs.shape
    block_rows, block_cols = value_weight.shape
    half = block_rows // CORES
    tensor = lax.axis_index("tensor")
    core = tensor % CORES
    swap = [(i, i ^ 1) for i in range(tensors)]
    near = [
        [s * tensors + h * CORES + c for s in range(shards) for c in range(CORES)]
        for h in range(tensors // CORES)
    ]
    group = ("shard", "tensor")
    fan = shards * CORES

    halves = value_weight.reshape(CORES, half, block_cols)
    kept = lax.dynamic_index_in_dim(halves, core, 0, keepdims=False)
    given = lax.dynamic_index_in_dim(halves, 1 - core, 0, keepdims=False)
    with jax.named_scope("wswap"):
        taken = lax.ppermute(given, "tensor", swap)
    weight = jnp.where(
        core == 0,
        jnp.concatenate([kept, taken], axis=1),
        jnp.concatenate([taken, kept], axis=1),
    )

    with jax.named_scope("cotgather"):
        cots = lax.all_to_all(
            jnp.broadcast_to(value_cot, (fan, tokens, block_cols)),
            group, 0, 0, axis_index_groups=near, tiled=True,
        )
    cot = cots.reshape(shards, CORES, tokens, block_cols).transpose(0, 2, 1, 3)
    cot = cot.reshape(shards * tokens, CORES * block_cols)

    wide_inputs = inputs.astype(jnp.float32)
    inv_scale = lax.rsqrt(jnp.mean(wide_inputs * wide_inputs, axis=1, keepdims=True) + norm_epsilon)
    gain_wide = gain.astype(jnp.float32)
    normed = (wide_inputs * inv_scale * gain_wide).astype(jnp.bfloat16)
    parts = lax.dynamic_index_in_dim(
        normed.reshape(tokens, shards, CORES, half), core, 2, keepdims=False
    ).transpose(1, 0, 2)
    with jax.named_scope("normed"):
        block = lax.all_to_all(parts, "shard", 0, 0, tiled=True)
    block = block.reshape(shards * tokens, half)

    hidden = lax.dot_general(
        cot, weight, (((1,), (1,)), ((), ())), preferred_element_type=jnp.float32
    ).astype(jnp.bfloat16)
    rows = tokens // tensors
    with jax.named_scope("hidden"):
        pieces = lax.all_to_all(
            hidden.reshape(shards * tensors, rows, half), group, 0, 0, tiled=True
        )

    local_grad = pseudo_grad[0].astype(jnp.bfloat16)
    frows, fcols = local_grad.shape
    own_cols = fcols // replicas
    with jax.named_scope("outer"):
        grads = lax.all_to_all(
            local_grad.reshape(frows, replicas, own_cols).transpose(1, 0, 2),
            "replica", 0, 0, tiled=True,
        )

    partial_values = jnp.dot(block, weight, preferred_element_type=jnp.float32).astype(jnp.bfloat16)
    sent = partial_values.reshape(shards, tokens, CORES, block_cols).transpose(0, 2, 1, 3)
    with jax.named_scope("values"):
        got = lax.all_to_all(
            sent.reshape(fan, tokens, block_cols), group, 0, 0, axis_index_groups=near, tiled=True
        )
    values = jnp.sum(got.astype(jnp.float32), axis=0).astype(jnp.bfloat16)

    wgrad = lax.dot_general(
        block, cot, (((0,), (0,)), ((), ())), preferred_element_type=jnp.float32
    ).astype(jnp.bfloat16)
    wgrad = wgrad.reshape(half, CORES, block_cols)
    mine = lax.dynamic_index_in_dim(wgrad, core, 1, keepdims=False)
    other = lax.dynamic_index_in_dim(wgrad, 1 - core, 1, keepdims=False)
    with jax.named_scope("gswap"):
        back = lax.ppermute(other, "tensor", swap)
    weight_grad = jnp.where(
        core == 0, jnp.stack([mine, back]), jnp.stack([back, mine])
    ).reshape(1, block_rows, block_cols)

    summed = jnp.sum(
        pieces.reshape(shards, tensors // CORES, CORES, rows, half).astype(jnp.float32), axis=1
    )
    summed = summed.transpose(2, 0, 1, 3).reshape(rows, width)
    first_row = tensor * rows
    input_rows = lax.dynamic_slice_in_dim(inputs, first_row, rows, 0).astype(jnp.float32)
    scale_rows = lax.dynamic_slice_in_dim(inv_scale, first_row, rows, 0)
    scaled = gain_wide * summed
    inner_mean = jnp.mean(input_rows * scaled, axis=1, keepdims=True)
    cubed = scale_rows * scale_rows * scale_rows
    input_grad = (scale_rows * scaled - input_rows * cubed * inner_mean).astype(jnp.bfloat16)

    average = jnp.sum(grads.reshape(replicas, frows, own_cols).astype(jnp.float32), axis=0) / replicas
    new_momentum = outer_beta * momentum + average
    new_global = global_params - outer_rate * (average + outer_beta * new_momentum)
    return (values, weight_grad, input_grad, new_global, new_momentum)


def solution(mesh):
    placed = (
        P(("replica", "shard"), None),
        P(),
        P("shard", "tensor"),
        P(("replica", "shard"), "tensor"),
        P("replica", ("shard", "tensor"), None),
        P(("shard", "tensor"), "replica"),
        P(("shard", "tensor"), "replica"),
    )
    return jax.shard_map(
        body,
        mesh=mesh,
        in_specs=placed,
        out_specs=(
            P(("replica", "shard"), "tensor"),
            P("replica", "shard", "tensor"),
            P(("replica", "shard", "tensor"), None),
            P(("shard", "tensor"), "replica"),
            P(("shard", "tensor"), "replica"),
        ),
        check_vma=False,
    )
```

time: 245 us -> 130 us (0.53)
  the two profiles are of different devices: /device:TPU:2 before, /device:TPU:9 now
where the time goes in v1:
time: 130 us; the launch traced here: 129 us
  waiting for transfers between devices  50.8 us (39%)
  starting transfers between devices  46.8 us (36%)
  local copies, waits for them, and re-layouts  13.8 us (11%)
  other arithmetic  13.3 us (10%)
  matrix products  3.2 us (2%)
    all_to_all x1, waiting for transfers between devices, body(): lax.all_to_all(hidden.reshape(shards * tensors, rows, half), group, 0, 0,...  22.1 us
    all_to_all x1, starting transfers between devices, body(): lax.all_to_all(local_grad.reshape(frows, replicas, own_cols).transpose(1,...  16.1 us
    all_to_all x1, waiting for transfers between devices, body(): block = lax.all_to_all(parts, 'shard', 0, 0, tiled=True)  12.3 us
    all_to_all x1, starting transfers between devices, body(): lax.all_to_all(hidden.reshape(shards * tensors, rows, half), group, 0, 0,...  7.91 us
    all_to_all x1, starting transfers between devices, body(): lax.all_to_all(sent.reshape(fan, tokens, block_cols), group, 0, 0, axis_i...  7.61 us
    all_to_all x1, waiting for transfers between devices, body(): lax.all_to_all(local_grad.reshape(frows, replicas, own_cols).transpose(1,...  7.59 us
    all_to_all x1, waiting for transfers between devices, body(): lax.all_to_all(sent.reshape(fan, tokens, block_cols), group, 0, 0, axis_i...  7.01 us
    unnamed x17, local copies, waits for them, and re-layouts  5.38 us
  transfers between devices with their start and end apart: 7, of which 5 were waited for; matrix products, arithmetic and copies ran while one was open for 18% of the time, Pallas kernels for 0%

profile of v1, /device:TPU:9, one launch (start us, length us, event | category | flops | bytes accessed | tf_op | source)
XLA Modules:
  0.0 128.8 jit_solution(15906014544977018327)
XLA Ops:
  0.6 1.7 %broadcast_in_dim.2 = bf16[8,128,256]{2,1,0:T(8,128)(2,1)} broadcast(bf16[128,256]{1,0:T(8,128)(2,1)} %param.10), dimensions={1,2} | broadcast | bytes 589824 | tf_op jit(solution)/shard_map/cotgather/broadcast_in_dim | solution.py:42
  2.3 5.0 %all-to-all-start.2 = ((bf16[8,128,256]{2,1,0:T(8,128)(2,1)}), bf16[8,128,256]{2,1,0:T(8,128)(2,1)S(1)}, u32[]{:S(2)}, u32[]{:S(2)}) async-start(bf16[8,128,256]{2,1,0:T(8,128)(2,1)} %broadcast_in_dim.2), calls=%async_computation.2 | async-start | bytes 1048576 | tf_op jit(solution)/shard_map/cotgather/all_to_all | solution.py:41
  7.3 3.2 %copy.27 = bf16[128,8192]{0,1:T(8,128)(2,1)S(1)} copy(bf16[128,8192]{1,0:T(8,128)(2,1)} %param.7) | data formatting | bytes 4194304 | tf_op args[0]
  10.5 0.0 copy-done.3
  10.5 0.0 copy-start.1
  10.5 1.1 fusion
  11.7 4.3 %fusion.2 = bf16[128,8192]{0,1:T(8,128)(2,1)} fusion(bf16[128,8192]{0,1:T(8,128)(2,1)S(1)} %copy.27, f32[8192]{0:T(1024)S(1)} %convert_element_type.46, f32[128]{0:T(128)S(1)} %add_rsqrt_fusion), kind=kLoop, calls=%fused_computation.4 | loop fusion | flops 4194304 | bytes 4227584 | tf_op jit(solution)/shard_map/convert_element_type | solution.py:51
  16.0 0.0 copy-done.1
  16.0 1.3 %constant_dynamic-slice_fusion.2 = bf16[128,4,1,1024]{0,3,2,1:T(8,128)(2,1)S(1)} fusion(bf16[128,4,2,1024]{0,3,2,1:T(8,128)(2,1)} %bitcast.44, s32[]{:T(128)S(6)} %select_n.50), kind=kLoop, calls=%fused_computation.25 | loop fusion | bytes 2097156 | tf_op jit(solution)/shard_map/jit(dynamic_index_in_dim)/dynamic_slice | solution.py:52
  17.3 1.3 %copy.28 = bf16[128,4,1,1024]{3,0,2,1:T(8,128)(2,1)} copy(bf16[128,4,1,1024]{0,3,2,1:T(8,128)(2,1)S(1)} %constant_dynamic-slice_fusion.2) | data formatting | bytes 2097152 | tf_op jit(solution)/shard_map/jit(dynamic_index_in_dim)/dynamic_slice | solution.py:52
  18.6 0.0 all-to-all-done.2
  18.6 4.1 %all-to-all-start = ((bf16[4,128,1024]{2,1,0:T(8,128)(2,1)}), bf16[4,128,1024]{2,1,0:T(8,128)(2,1)S(1)}, u32[]{:S(2)}, u32[]{:S(2)}) async-start(bf16[4,128,1024]{2,1,0:T(8,128)(2,1)} %bitcast.2), calls=%async_computation | async-start | bytes 2097152 | tf_op jit(solution)/shard_map/normed/all_to_all | solution.py:56
  22.8 1.3 convert_bitcast_fusion
  24.0 0.1 copy.38
  24.1 0.8 copy.34
  24.9 12.3 %all-to-all-done = bf16[4,128,1024]{2,1,0:T(8,128)(2,1)S(1)} async-done(((bf16[4,128,1024]{2,1,0:T(8,128)(2,1)}), bf16[4,128,1024]{2,1,0:T(8,128)(2,1)S(1)}, u32[]{:S(2)}, u32[]{:S(2)}) %all-to-all-start) | async-done | bytes 1048608 | tf_op jit(solution)/shard_map/normed/all_to_all | solution.py:56
  37.3 16.1 %all-to-all-start.4 = ((bf16[24,64,128]{2,1,0:T(8,128)(2,1)}), bf16[24,64,128]{2,1,0:T(8,128)(2,1)S(1)}, u32[]{:S(2)}, u32[]{:S(2)}) async-start(bf16[24,64,128]{2,1,0:T(8,128)(2,1)} %copy.34), calls=%async_computation.4 | async-start | bytes 786432 | tf_op jit(solution)/shard_map/outer/all_to_all | solution.py:72
  53.4 0.9 dynamic-slice_bitcast_fusion.1
  54.3 4.0 %collective-permute-start = (bf16[1024,256]{1,0:T(8,128)(2,1)}, bf16[1024,256]{1,0:T(8,128)(2,1)S(1)}, u32[]{:S(2)}, u32[]{:S(2)}) collective-permute-start(bf16[1024,256]{1,0:T(8,128)(2,1)} %get-tuple-element.12), channel_id=1, source_target_pairs={{0,1},{1,0},{2,3},{3,2},{4,5},{5,4},{6,7},{7,6},{8,9},{9,8},{10,11... | collective-permute-start | bytes 1572872 | tf_op jit(solution)/shard_map/wswap/ppermute | solution.py:33
  58.3 1.7 %collective-permute-done = bf16[1024,256]{1,0:T(8,128)(2,1)S(1)} collective-permute-done((bf16[1024,256]{1,0:T(8,128)(2,1)}, bf16[1024,256]{1,0:T(8,128)(2,1)S(1)}, u32[]{:S(2)}, u32[]{:S(2)}) %collective-permute-start) | collective-permute-done | bytes 524320 | tf_op jit(solution)/shard_map/wswap/ppermute | solution.py:33
  60.0 0.8 copy-done.4
  60.8 0.7 convolution_convert_fusion.2
  61.5 0.1 reshape.98
  61.6 0.9 copy.29
  62.5 7.6 %all-to-all-done.4 = bf16[24,64,128]{2,1,0:T(8,128)(2,1)S(1)} async-done(((bf16[24,64,128]{2,1,0:T(8,128)(2,1)}), bf16[24,64,128]{2,1,0:T(8,128)(2,1)S(1)}, u32[]{:S(2)}, u32[]{:S(2)}) %all-to-all-start.4) | async-done | bytes 393248 | tf_op jit(solution)/shard_map/outer/all_to_all | solution.py:72
  70.1 7.6 %all-to-all-start.1 = ((bf16[8,128,256]{2,1,0:T(8,128)(2,1)}), bf16[8,128,256]{2,1,0:T(8,128)(2,1)S(1)}, u32[]{:S(2)}, u32[]{:S(2)}) async-start(bf16[8,128,256]{2,1,0:T(8,128)(2,1)} %bitcast.8), calls=%async_computation.1 | async-start | bytes 1048576 | tf_op jit(solution)/shard_map/values/all_to_all | solution.py:80
  77.7 0.5 copy.30
  78.3 0.1 copy.37
  78.4 1.7 %convolution_convert_fusion = bf16[1024,512]{0,1:T(8,128)(2,1)} fusion(bf16[512,512]{1,0:T(8,128)(2,1)S(1)} %bitcast.59, bf16[1024,256]{1,0:T(8,128)(2,1)S(1)} %copy-done.5, bf16[1024,256]{1,0:T(8,128)(2,1)S(1)} %get-tuple-element.11, pred[]{:T(512)S(6)} %eq.6), kind=kOutput, calls=%fused_computation.6 | convolution fusion | flops 542113792 | bytes 2621441 | tf_op jit(solution)/shard_map/dot_general | solution.py:59
  80.1 7.0 %all-to-all-done.1 = bf16[8,128,256]{2,1,0:T(8,128)(2,1)S(1)} async-done(((bf16[8,128,256]{2,1,0:T(8,128)(2,1)}), bf16[8,128,256]{2,1,0:T(8,128)(2,1)S(1)}, u32[]{:S(2)}, u32[]{:S(2)}) %all-to-all-start.1) | async-done | bytes 524320 | tf_op jit(solution)/shard_map/values/all_to_all | solution.py:80
  87.1 7.9 %all-to-all-start.3 = ((bf16[32,16,1024]{2,1,0:T(8,128)(2,1)}), bf16[32,16,1024]{2,1,0:T(8,128)(2,1)S(1)}, u32[]{:S(2)}, u32[]{:S(2)}) async-start(bf16[32,16,1024]{2,1,0:T(8,128)(2,1)} %bitcast.54), calls=%async_computation.3 | async-start | bytes 2097152 | tf_op jit(solution)/shard_map/hidden/all_to_all | solution.py:64
  95.0 0.8 convolution_convert_fusion.1
  95.8 0.1 constant_dynamic-slice_fusion.1
  95.9 1.0 copy.36
  96.9 2.1 %collective-permute-start.1 = (bf16[1024,256]{1,0:T(8,128)(2,1)}, bf16[1024,256]{1,0:T(8,128)(2,1)S(1)}, u32[]{:S(2)}, u32[]{:S(2)}) collective-permute-start(bf16[1024,256]{1,0:T(8,128)(2,1)} %bitcast.58), channel_id=1, source_target_pairs={{0,1},{1,0},{2,3},{3,2},{4,5},{5,4},{6,7},{7,6},{8,9},{9,8},{10,11... | collective-permute-start | bytes 1572872 | tf_op jit(solution)/shard_map/gswap/ppermute | solution.py:92
  99.0 0.1 fusion.7
  99.1 0.2 copy.35
  99.3 0.1 convert_reduce_fusion.1
  99.4 1.4 %multiply_subtract_fusion = (f32[64,128]{1,0:T(8,128)}, f32[64,128]{1,0:T(8,128)}) fusion(f32[64,128]{1,0:T(8,128)} %param.12, f32[64,128]{1,0:T(8,128)S(1)} %convert_reduce_fusion.1, f32[64,128]{1,0:T(8,128)} %param.13), kind=kLoop, calls=%fused_computation.21 | loop fusion | flops 57344 | bytes 163840 | tf_op jit(solution)/shard_map/sub | solution.py:111
  100.8 0.7 reduce_sum.49
  101.5 0.0 collective-permute-done.1
  101.5 1.1 maximum_select_fusion.1
  102.6 22.1 %all-to-all-done.3 = bf16[32,16,1024]{2,1,0:T(8,128)(2,1)S(1)} async-done(((bf16[32,16,1024]{2,1,0:T(8,128)(2,1)}), bf16[32,16,1024]{2,1,0:T(8,128)(2,1)S(1)}, u32[]{:S(2)}, u32[]{:S(2)}) %all-to-all-start.3) | async-done | bytes 1048608 | tf_op jit(solution)/shard_map/hidden/all_to_all | solution.py:64
  124.8 0.2 convert_reduce_fusion
  124.9 0.4 copy.33
  125.4 0.5 reshape.104
  125.8 1.1 fusion.6
  127.0 1.8 %fusion.5 = bf16[16,8192]{1,0:T(8,128)(2,1)} fusion(f32[16,8192]{1,0:T(8,128)S(1)} %reshape.104, f32[16]{0:T(128)S(1)} %broadcast_multiply_fusion, f32[16]{0:T(128)S(1)} %get-tuple-element.7, f32[8192]{0:T(1024)S(1)} %copy-done.2, f32[16]{0:T(128)S(1)} %get-tuple-element.8, bf16[128,8192]{1,0:T(8,128)(2,1)} %param.7, s32[]{:T(128)S(6)} %select_n.57), kind=kLoop, calls=%fused_computation.16 | loop fusion | flops 917504 | bytes 1081540 | tf_op jit(solution)/shard_map/convert_element_type | solution.py:107
  (11 shorter events, 0.0 us)
Async XLA Ops:
  2.3 16.3 %all-to-all-start.2 = ((bf16[8,128,256]{2,1,0:T(8,128)(2,1)}), bf16[8,128,256]{2,1,0:T(8,128)(2,1)S(1)}, u32[]{:S(2)}, u32[]{:S(2)}) async-start(bf16[8,128,256]{2,1,0:T(8,128)(2,1)} %broadcast_in_dim.2), calls=%async_computation.2 | async-start | bytes 1048576 | tf_op jit(solution)/shard_map/cotgather/all_to_all | solution.py:41
  7.3 3.2 %copy-start.3 = (bf16[8192]{0:T(1024)(128)(2,1)S(1)}, bf16[8192]{0:T(1024)(128)(2,1)}, u32[]{:S(2)}) copy-start(bf16[8192]{0:T(1024)(128)(2,1)} %param.8) | copy-start | bytes 49156
  10.5 5.5 %copy-start.1 = (f32[8192]{0:T(1024)}, f32[8192]{0:T(1024)S(1)}, u32[]{:S(2)}) copy-start(f32[8192]{0:T(1024)S(1)} %convert_element_type.46) | copy-start | bytes 98308
  18.6 18.6 %all-to-all-start = ((bf16[4,128,1024]{2,1,0:T(8,128)(2,1)}), bf16[4,128,1024]{2,1,0:T(8,128)(2,1)S(1)}, u32[]{:S(2)}, u32[]{:S(2)}) async-start(bf16[4,128,1024]{2,1,0:T(8,128)(2,1)} %bitcast.2), calls=%async_computation | async-start | bytes 2097152 | tf_op jit(solution)/shard_map/normed/all_to_all | solution.py:56
  22.8 30.6 %copy-start = (bf16[2048,256]{1,0:T(8,128)(2,1)S(1)}, bf16[2048,256]{1,0:T(8,128)(2,1)}, u32[]{:S(2)}) copy-start(bf16[2048,256]{1,0:T(8,128)(2,1)} %param.9) | copy-start | bytes 3145732
  37.3 32.8 %all-to-all-start.4 = ((bf16[24,64,128]{2,1,0:T(8,128)(2,1)}), bf16[24,64,128]{2,1,0:T(8,128)(2,1)S(1)}, u32[]{:S(2)}, u32[]{:S(2)}) async-start(bf16[24,64,128]{2,1,0:T(8,128)(2,1)} %copy.34), calls=%async_computation.4 | async-start | bytes 786432 | tf_op jit(solution)/shard_map/outer/all_to_all | solution.py:72
  54.3 5.7 %collective-permute-start = (bf16[1024,256]{1,0:T(8,128)(2,1)}, bf16[1024,256]{1,0:T(8,128)(2,1)S(1)}, u32[]{:S(2)}, u32[]{:S(2)}) collective-permute-start(bf16[1024,256]{1,0:T(8,128)(2,1)} %get-tuple-element.12), channel_id=1, source_target_pairs={{0,1},{1,0},{2,3},{3,2},{4,5},{5,4},{6,7},{7,6},{8,9},{9,8},{10,11... | collective-permute-start | bytes 1572872 | tf_op jit(solution)/shard_map/wswap/ppermute | solution.py:33
  60.0 0.8 copy-start.4
  61.6 16.7 %copy-start.5 = (bf16[1024,256]{1,0:T(8,128)(2,1)S(1)}, bf16[1024,256]{1,0:T(8,128)(2,1)}, u32[]{:S(2)}) copy-start(bf16[1024,256]{1,0:T(8,128)(2,1)} %copy-done.4) | copy-start | bytes 1572868
  70.1 17.0 %all-to-all-start.1 = ((bf16[8,128,256]{2,1,0:T(8,128)(2,1)}), bf16[8,128,256]{2,1,0:T(8,128)(2,1)S(1)}, u32[]{:S(2)}, u32[]{:S(2)}) async-start(bf16[8,128,256]{2,1,0:T(8,128)(2,1)} %bitcast.8), calls=%async_computation.1 | async-start | bytes 1048576 | tf_op jit(solution)/shard_map/values/all_to_all | solution.py:80
  87.1 37.7 %all-to-all-start.3 = ((bf16[32,16,1024]{2,1,0:T(8,128)(2,1)}), bf16[32,16,1024]{2,1,0:T(8,128)(2,1)S(1)}, u32[]{:S(2)}, u32[]{:S(2)}) async-start(bf16[32,16,1024]{2,1,0:T(8,128)(2,1)} %bitcast.54), calls=%async_computation.3 | async-start | bytes 2097152 | tf_op jit(solution)/shard_map/hidden/all_to_all | solution.py:64
  96.9 4.6 %collective-permute-start.1 = (bf16[1024,256]{1,0:T(8,128)(2,1)}, bf16[1024,256]{1,0:T(8,128)(2,1)S(1)}, u32[]{:S(2)}, u32[]{:S(2)}) collective-permute-start(bf16[1024,256]{1,0:T(8,128)(2,1)} %bitcast.58), channel_id=1, source_target_pairs={{0,1},{1,0},{2,3},{3,2},{4,5},{5,4},{6,7},{7,6},{8,9},{9,8},{10,11... | collective-permute-start | bytes 1572872 | tf_op jit(solution)/shard_map/gswap/ppermute | solution.py:92
  102.6 23.2 %copy-start.2 = (f32[8192]{0:T(1024)S(1)}, f32[8192]{0:T(1024)}, u32[]{:S(2)}) copy-start(f32[8192]{0:T(1024)} %copy-done.1) | copy-start | bytes 98308

commit v2 on v0

v2 whole, which is shorter than its diff:
```python
import functools

import jax
import jax.numpy as jnp
from jax import lax
from jax.experimental import pallas as pl
from jax.experimental.pallas import tpu as pltpu
from jax.sharding import PartitionSpec as P

norm_epsilon = 1e-05
outer_rate = 0.7
outer_beta = 0.9
CORES = 2
SHARDS = 4
CHIPS = 4
F32 = jnp.float32
BF16 = jnp.bfloat16


def cost(flops, moved):
    return pl.CostEstimate(flops=flops, bytes_accessed=moved, transcendentals=0)


def whole(shape):
    return pl.BlockSpec(shape, lambda *_: (0,) * len(shape))


def spread_kernel(x_ref, o_ref):
    for i in range(o_ref.shape[0]):
        o_ref[i] = x_ref[...]


def pack_kernel(idx, x_ref, g_ref, o0, o1, o2, o3, inv_ref):
    width = x_ref.shape[1]
    part = width // SHARDS
    chunk = 1024
    total = jnp.zeros((x_ref.shape[0], chunk), F32)
    for q in range(width // chunk):
        wide = x_ref[:, q * chunk:(q + 1) * chunk].astype(F32)
        total += wide * wide
    inv = lax.rsqrt(jnp.sum(total, axis=1, keepdims=True) / width + norm_epsilon)
    inv_ref[...] = jnp.broadcast_to(inv, inv_ref.shape)
    for k, out in enumerate((o0, o1, o2, o3)):
        begin = pl.multiple_of(lax.rem(idx[2] + k, SHARDS) * part, part)
        for q in range(part // chunk):
            at = pl.ds(begin + q * chunk, chunk)
            wide = x_ref[:, at].astype(F32)
            out[:, q * chunk:(q + 1) * chunk] = (wide * inv * g_ref[:, at]).astype(BF16)


def hidden_kernel(idx, cots, w_ref, v_ref, o0, o1, o2, o3, own, oth):
    core, chip = idx[0], idx[1]

    @pl.when(pl.program_id(0) == 0)
    def _():
        for j in range(CHIPS):
            row = pl.multiple_of((CORES * lax.rem(chip + j, CHIPS) + core) * 16, 16)
            for s in range(SHARDS):
                to = pl.ds(j * 64 + s * 16, 16)
                own[to, :] = cots[CORES * s + core, pl.ds(row, 16), :]
                oth[to, :] = cots[CORES * s + 1 - core, pl.ds(row, 16), :]

    dims = (((1,), (1,)), ((), ()))
    product = lax.dot_general(own[...], w_ref[...], dims, preferred_element_type=F32)
    product += lax.dot_general(oth[...], v_ref[...], dims, preferred_element_type=F32)
    for j, out in enumerate((o0, o1, o2, o3)):
        out[...] = product[j * 64:(j + 1) * 64].astype(BF16)


def values_kernel(n0, n1, n2, n3, w_ref, o0, o1, o2, o3, acc):
    step = pl.program_id(0)

    @pl.when(step == 0)
    def _():
        acc[...] = jnp.zeros_like(acc)

    for k, block in enumerate((n0, n1, n2, n3)):
        acc[k] += jnp.dot(block[...], w_ref[...], preferred_element_type=F32)

    @pl.when(step == pl.num_programs(0) - 1)
    def _():
        for k, out in enumerate((o0, o1, o2, o3)):
            out[...] = acc[k].astype(out.dtype)


def wgrad_kernel(idx, n0, n1, n2, n3, cots, o_ref):
    total = None
    for k, block in enumerate((n0, n1, n2, n3)):
        owner = lax.rem(idx[2] + SHARDS - k, SHARDS)
        term = lax.dot_general(
            block[...], cots[CORES * owner + idx[0]], (((0,), (0,)), ((), ())),
            preferred_element_type=F32,
        )
        total = term if total is None else total + term
    o_ref[0] = total.astype(BF16)


def merge_kernel(idx, h0, r1, r2, r3, v1, v2, v3, keep, m1, m2, m3):
    cols = m1.shape[1]
    tokens = v1.shape[0]
    for k, out in enumerate((keep, m1, m2, m3)):
        at = pl.ds(pl.multiple_of(lax.rem(idx[2] + k, SHARDS) * 16, 16), 16)
        for q in range(h0.shape[1] // cols):
            lanes = slice(q * cols, (q + 1) * cols)
            total = h0[at, lanes].astype(F32) + r1[at, lanes].astype(F32)
            total += r2[at, lanes].astype(F32) + r3[at, lanes].astype(F32)
            if k == 0:
                out[:, lanes] = total
            else:
                out[q * 16:(q + 1) * 16, :] = total.astype(BF16)
    for k, out, val in ((1, m1, v3), (2, m2, v2), (3, m3, v1)):
        out[tokens:, :] = val[...]


def final_kernel(idx, keep, m1, m2, m3, v0, x_ref, inv_ref, g_ref, o_ref, val_ref):
    part = keep.shape[1]
    tokens, cols = v0.shape
    width = x_ref.shape[1]
    inv = inv_ref[:, :1]
    places = []
    for k, got in enumerate((keep, m1, m2, m3)):
        begin = pl.multiple_of(lax.rem(idx[2] + SHARDS - k, SHARDS) * part, part)
        for q in range(part // cols):
            places.append((k, got, q, pl.ds(begin + q * cols, cols)))

    def scaled(k, got, q, at):
        if k == 0:
            term = got[:, q * cols:(q + 1) * cols]
        else:
            term = got[q * 16:(q + 1) * 16, :].astype(F32)
        return g_ref[:, at] * term

    total = jnp.zeros((16, cols), F32)
    for place in places:
        total += x_ref[:, place[3]].astype(F32) * scaled(*place)
    mean = jnp.sum(total, axis=1, keepdims=True) / width
    factor = inv * inv * inv * mean
    for place in places:
        at = place[3]
        o_ref[:, at] = (inv * scaled(*place) - x_ref[:, at].astype(F32) * factor).astype(BF16)
    summed = v0[...]
    for got in (m1, m2, m3):
        summed += got[tokens:, :].astype(F32)
    val_ref[...] = summed.astype(BF16)


def outer_pack_kernel(x_ref, o_ref):
    cols = o_ref.shape[2]
    for r in range(o_ref.shape[0]):
        o_ref[r] = x_ref[0, :, r * cols:(r + 1) * cols].astype(BF16)


def outer_kernel(g_ref, p_ref, m_ref, new_p, new_m):
    replicas = g_ref.shape[0]
    total = g_ref[0].astype(F32)
    for r in range(1, replicas):
        total += g_ref[r].astype(F32)
    average = total / replicas
    momentum = outer_beta * m_ref[...] + average
    new_m[...] = momentum
    new_p[...] = p_ref[...] - outer_rate * (average + outer_beta * momentum)


def body(inputs, gain, value_weight, value_cot, pseudo_grad, global_params, momentum):
    tensors = lax.axis_size("tensor")
    replicas = lax.axis_size("replica")
    tokens, width = inputs.shape
    rows, cols = value_weight.shape
    tensor = lax.axis_index("tensor")
    shard = lax.axis_index("shard")
    idx = jnp.stack([tensor % CORES, tensor // CORES, shard, tensor]).astype(jnp.int32)
    swap = [(i, i ^ 1) for i in range(tensors)]
    chip_shift = lambda j: [
        (t, (t // CORES + j) % CHIPS * CORES + t % CORES) for t in range(tensors)
    ]
    shard_shift = lambda k: [(s, (s + k) % SHARDS) for s in range(SHARDS)]
    near = [
        [s * tensors + h * CORES + c for s in range(SHARDS) for c in range(CORES)]
        for h in range(CHIPS)
    ]
    fan = SHARDS * CORES
    spec = jax.ShapeDtypeStruct
    rest = (1, 3, 2)

    spread = pl.pallas_call(
        spread_kernel, out_shape=spec((fan, tokens, cols), BF16),
        cost_estimate=cost(0, 600_000), name="spread",
    )(value_cot)
    with jax.named_scope("cotgather"):
        cots = lax.all_to_all(
            spread, ("shard", "tensor"), 0, 0, axis_index_groups=near, tiled=True
        )
    with jax.named_scope("wswap"):
        other_weight = lax.ppermute(value_weight, "tensor", swap)

    gain_row = gain.astype(F32).reshape(1, width)
    part = width // SHARDS
    *sent, inv_scale = pl.pallas_call(
        pack_kernel,
        grid_spec=pltpu.PrefetchScalarGridSpec(
            num_scalar_prefetch=1, grid=(tokens // 16,),
            in_specs=[pl.BlockSpec((16, width), lambda i, _: (i, 0)), whole((1, width))],
            out_specs=[pl.BlockSpec((16, part), lambda i, _: (i, 0))] * SHARDS
            + [pl.BlockSpec((16, 128), lambda i, _: (i, 0))],
        ),
        out_shape=[spec((tokens, part), BF16)] * SHARDS + [spec((tokens, 128), F32)],
        cost_estimate=cost(6_000_000, 4_300_000), name="pack",
    )(idx, inputs, gain_row)
    normed = [sent[0], None, None, None]
    for k in rest:
        with jax.named_scope(f"normed{k}"):
            normed[k] = lax.ppermute(sent[k], "shard", shard_shift(k))

    step = 512
    outs = pl.pallas_call(
        hidden_kernel,
        grid_spec=pltpu.PrefetchScalarGridSpec(
            num_scalar_prefetch=1, grid=(rows // step,),
            in_specs=[whole((fan, tokens, cols))]
            + [pl.BlockSpec((step, cols), lambda i, _: (i, 0))] * 2,
            out_specs=[pl.BlockSpec((64, step), lambda i, _: (0, i))] * CHIPS,
            scratch_shapes=[pltpu.VMEM((256, cols), BF16)] * 2,
        ),
        out_shape=[spec((64, rows), BF16)] * CHIPS,
        cost_estimate=cost(540_000_000, 3_700_000), name="hiddenmm",
    )(idx, cots, value_weight, other_weight)
    hidden = [outs[0], None, None, None]
    for j in rest:
        with jax.named_scope(f"hidden{j}"):
            hidden[j] = lax.ppermute(outs[j], "tensor", chip_shift(j))

    frows, fcols = pseudo_grad.shape[1:]
    own_cols = fcols // replicas
    packed = pl.pallas_call(
        outer_pack_kernel, grid=(3,),
        in_specs=[pl.BlockSpec((1, frows, fcols // 3), lambda i: (0, 0, i))],
        out_specs=pl.BlockSpec((replicas // 3, frows, own_cols), lambda i: (i, 0, 0)),
        out_shape=spec((replicas, frows, own_cols), BF16),
        cost_estimate=cost(0, 1_200_000), name="outerpack",
    )(pseudo_grad)
    packed, _ = lax.optimization_barrier((packed, outs[0]))
    with jax.named_scope("outer"):
        grads = lax.all_to_all(packed, "replica", 0, 0, tiled=True)

    partial_values = pl.pallas_call(
        values_kernel,
        grid_spec=pltpu.PrefetchScalarGridSpec(
            num_scalar_prefetch=0, grid=(rows // step,),
            in_specs=[pl.BlockSpec((tokens, step), lambda i: (0, i))] * SHARDS
            + [pl.BlockSpec((step, cols), lambda i: (i, 0))],
            out_specs=[whole((tokens, cols))] * SHARDS,
            scratch_shapes=[pltpu.VMEM((SHARDS, tokens, cols), F32)],
        ),
        out_shape=[spec((tokens, cols), F32)] + [spec((tokens, cols), BF16)] * 3,
        cost_estimate=cost(540_000_000, 3_300_000), name="valuesmm",
    )(*normed, value_weight)

    weight_grad = pl.pallas_call(
        wgrad_kernel,
        grid_spec=pltpu.PrefetchScalarGridSpec(
            num_scalar_prefetch=1, grid=(rows // step,),
            in_specs=[pl.BlockSpec((tokens, step), lambda i, _: (0, i))] * SHARDS
            + [whole((fan, tokens, cols))],
            out_specs=pl.BlockSpec((1, step, cols), lambda i, _: (0, i, 0)),
        ),
        out_shape=spec((1, rows, cols), BF16),
        cost_estimate=cost(540_000_000, 3_600_000), name="wgradmm",
    )(idx, *normed, cots)

    keep, *merged = pl.pallas_call(
        merge_kernel,
        grid_spec=pltpu.PrefetchScalarGridSpec(
            num_scalar_prefetch=1, grid=(1,),
            in_specs=[whole((64, rows))] * CHIPS + [whole((tokens, cols))] * 3,
            out_specs=[whole((16, rows))] + [whole((2 * tokens, cols))] * 3,
        ),
        out_shape=[spec((16, rows), F32)] + [spec((2 * tokens, cols), BF16)] * 3,
        cost_estimate=cost(1_000_000, 1_700_000), name="merge",
    )(idx, *hidden, *partial_values[1:])
    got = [None] * SHARDS
    for k in rest:
        with jax.named_scope(f"last{k}"):
            got[k] = lax.ppermute(merged[k - 1], "shard", shard_shift(k))

    input_grad, values = pl.pallas_call(
        final_kernel,
        grid_spec=pltpu.PrefetchScalarGridSpec(
            num_scalar_prefetch=1, grid=(1,),
            in_specs=[whole((16, rows))] + [whole((2 * tokens, cols))] * 3
            + [
                whole((tokens, cols)),
                pl.BlockSpec((16, width), lambda i, at: (at[3], 0)),
                pl.BlockSpec((16, 128), lambda i, at: (at[3], 0)),
                whole((1, width)),
            ],
            out_specs=[whole((16, width)), whole((tokens, cols))],
        ),
        out_shape=[spec((16, width), BF16), spec((tokens, cols), BF16)],
        cost_estimate=cost(2_000_000, 1_500_000), name="final",
    )(idx, keep, *got[1:], partial_values[0], inputs, inv_scale, gain_row)

    new_global, new_momentum = pl.pallas_call(
        outer_kernel, out_shape=[spec(momentum.shape, F32)] * 2,
        cost_estimate=cost(500_000, 600_000), name="outerstep",
    )(grads, global_params, momentum)
    return (values, weight_grad, input_grad, new_global, new_momentum)


def solution(mesh):
    placed = (
        P(("replica", "shard"), None),
        P(),
        P("shard", "tensor"),
        P(("replica", "shard"), "tensor"),
        P("replica", ("shard", "tensor"), None),
        P(("shard", "tensor"), "replica"),
        P(("shard", "tensor"), "replica"),
    )
    return jax.shard_map(
        body,
        mesh=mesh,
        in_specs=placed,
        out_specs=(
            P(("replica", "shard"), "tensor"),
            P("replica", "shard", "tensor"),
            P(("replica", "shard", "tensor"), None),
            P(("shard", "tensor"), "replica"),
            P(("shard", "tensor"), "replica"),
        ),
        check_vma=False,
    )
```

time: 245 us -> 119 us (0.49)
  the two profiles are of different devices: /device:TPU:2 before, /device:TPU:1 now
where the time goes in v2:
time: 119 us; the launch traced here: 117 us
  starting transfers between devices  58.6 us (49%)
  Pallas kernels  33 us (28%)
  waiting for transfers between devices  19.1 us (16%)
  local copies, waits for them, and re-layouts  4.74 us (4%)
  other arithmetic  1.21 us (1%)
    ppermute x3, starting transfers between devices, body(): hidden[j] = lax.ppermute(outs[j], 'tensor', chip_shift(j))  13.9 us
    ppermute x1, starting transfers between devices, body(): other_weight = lax.ppermute(value_weight, 'tensor', swap)  12.4 us
    ppermute x3, starting transfers between devices, body(): got[k] = lax.ppermute(merged[k - 1], 'shard', shard_shift(k))  12.2 us
    ppermute x3, starting transfers between devices, body(): normed[k] = lax.ppermute(sent[k], 'shard', shard_shift(k))  8.4 us
    all_to_all x1, starting transfers between devices, body(): grads = lax.all_to_all(packed, 'replica', 0, 0, tiled=True)  8.24 us
    ppermute x3, waiting for transfers between devices, body(): normed[k] = lax.ppermute(sent[k], 'shard', shard_shift(k))  7.52 us
    pallas_call x1, Pallas kernels, body(): pl.pallas_call(pack_kernel, grid_spec=pltpu.PrefetchScalarGridSpec(num_sc...  6.67 us
    all_to_all x1, waiting for transfers between devices, body(): lax.all_to_all(spread, ('shard', 'tensor'), 0, 0, axis_index_groups=near,...  6 us
  transfers between devices with their start and end apart: 12, of which 4 were waited for; matrix products, arithmetic and copies ran while one was open for 1% of the time, Pallas kernels for 22%

profile of v2, /device:TPU:1, one launch (start us, length us, event | category | flops | bytes accessed | tf_op | source)
XLA Modules:
  0.0 117.5 jit_solution(9808086145295175094)
XLA Ops:
  0.6 12.4 %collective-permute-start = (bf16[2048,256]{1,0:T(8,128)(2,1)}, bf16[2048,256]{1,0:T(8,128)(2,1)S(1)}, u32[]{:S(2)}, u32[]{:S(2)}) collective-permute-start(bf16[2048,256]{1,0:T(8,128)(2,1)} %w_ref.3), channel_id=1, source_target_pairs={{0,1},{1,0},{2,3},{3,2},{4,5},{5,4},{6,7},{7,6},{8,9},{9,8},{10,11... | collective-permute-start | bytes 3145736 | tf_op jit(solution)/shard_map/wswap/ppermute | solution.py:194
  13.0 1.7 %spread.1 = bf16[8,128,256]{2,1,0:T(8,128)(2,1)} custom-call(bf16[128,256]{1,0:T(8,128)(2,1)} %x_ref.4), custom_call_target="tpu_custom_call" | custom-call | bytes 600000 | tf_op jit(solution)/shard_map/spread/pallas_call | solution.py:185
  14.7 3.4 %all-to-all-start = ((bf16[8,128,256]{2,1,0:T(8,128)(2,1)}), bf16[8,128,256]{2,1,0:T(8,128)(2,1)S(1)}, u32[]{:S(2)}, u32[]{:S(2)}) async-start(bf16[8,128,256]{2,1,0:T(8,128)(2,1)} %spread.1), calls=%async_computation | async-start | bytes 1048576 | tf_op jit(solution)/shard_map/cotgather/all_to_all | solution.py:190
  18.2 0.0 copy-start.12
  18.2 2.7 %outerpack.1 = bf16[24,64,128]{2,1,0:T(8,128)(2,1)} custom-call(f32[1,64,3072]{2,1,0:T(8,128)} %x_ref.7), custom_call_target="tpu_custom_call" | custom-call | bytes 1200000 | tf_op jit(solution)/shard_map/outerpack/pallas_call | solution.py:234
  20.9 0.6 pad_add_fusion.idx
  21.5 6.0 %all-to-all-done.cots = bf16[8,128,256]{2,1,0:T(8,128)(2,1)S(1)} async-done(((bf16[8,128,256]{2,1,0:T(8,128)(2,1)}), bf16[8,128,256]{2,1,0:T(8,128)(2,1)S(1)}, u32[]{:S(2)}, u32[]{:S(2)}) %all-to-all-start) | async-done | bytes 524320 | tf_op jit(solution)/shard_map/cotgather/all_to_all | solution.py:190
  27.5 0.0 collective-permute-done.v_ref
  27.5 0.8 copy-done
  28.3 1.0 copy-done.5
  29.2 4.9 %hiddenmm.1 = (bf16[64,2048]{1,0:T(8,128)(2,1)}, bf16[64,2048]{1,0:T(8,128)(2,1)}, bf16[64,2048]{1,0:T(8,128)(2,1)}, bf16[64,2048]{1,0:T(8,128)(2,1)}) custom-call(s32[4]{0:T(128)} %pad_add_fusion.idx, bf16[8,128,256]{2,1,0:T(8,128)(2,1)} %copy-done, bf16[2048,256]{1,0:T(8,128)(2,1)} %w_ref.3, bf16[2048,256]{1,0:T(8,128)(2,1)} %copy-done.5), custom_call_target="tpu_custom_call" | custom-call | flops 540000000 | bytes 3700000 | tf_op jit(solution)/shard_map/hiddenmm/pallas_call | solution.py:215
  34.2 8.2 %all-to-all-start.1 = ((bf16[24,64,128]{2,1,0:T(8,128)(2,1)}), bf16[24,64,128]{2,1,0:T(8,128)(2,1)S(1)}, u32[]{:S(2)}, u32[]{:S(2)}) async-start(bf16[24,64,128]{2,1,0:T(8,128)(2,1)} %outerpack.1), calls=%async_computation.1 | async-start | bytes 786432 | tf_op jit(solution)/shard_map/outer/all_to_all | solution.py:243
  42.4 0.6 reshape.17
  43.1 6.7 %pack.1 = (bf16[128,2048]{1,0:T(8,128)(2,1)}, bf16[128,2048]{1,0:T(8,128)(2,1)}, bf16[128,2048]{1,0:T(8,128)(2,1)}, bf16[128,2048]{1,0:T(8,128)(2,1)}, f32[128,128]{1,0:T(8,128)}) custom-call(s32[4]{0:T(128)} %pad_add_fusion.idx, bf16[128,8192]{1,0:T(8,128)(2,1)} %x_ref.6, f32[1,8192]{1,0:T(1,128)} %bitcast.5), custom_call_target="tpu_custom_call" | custom-call | flops 6000000 | bytes 4300000 | tf_op jit(solution)/shard_map/pack/pallas_call | solution.py:198
  49.7 2.2 %collective-permute-start.4 = (bf16[128,2048]{1,0:T(8,128)(2,1)}, bf16[128,2048]{1,0:T(8,128)(2,1)S(1)}, u32[]{:S(2)}, u32[]{:S(2)}) collective-permute-start(bf16[128,2048]{1,0:T(8,128)(2,1)} %get-tuple-element.32), channel_id=1, source_target_pairs={{0,8},{8,16},{16,24},{24,0},{1,9},{9,17},{17,25},{25,1},{2,10},{10... | collective-permute-start | bytes 1572872 | tf_op jit(solution)/shard_map/normed1/ppermute | solution.py:212
  51.9 3.7 %collective-permute-start.5 = (bf16[128,2048]{1,0:T(8,128)(2,1)}, bf16[128,2048]{1,0:T(8,128)(2,1)S(1)}, u32[]{:S(2)}, u32[]{:S(2)}) collective-permute-start(bf16[128,2048]{1,0:T(8,128)(2,1)} %get-tuple-element.33), channel_id=1, source_target_pairs={{0,16},{8,24},{16,0},{24,8},{1,17},{9,25},{17,1},{25,9},{2,18},{10... | collective-permute-start | bytes 1572872 | tf_op jit(solution)/shard_map/normed2/ppermute | solution.py:212
  55.6 2.5 %collective-permute-start.6 = (bf16[128,2048]{1,0:T(8,128)(2,1)}, bf16[128,2048]{1,0:T(8,128)(2,1)S(1)}, u32[]{:S(2)}, u32[]{:S(2)}) collective-permute-start(bf16[128,2048]{1,0:T(8,128)(2,1)} %get-tuple-element.34), channel_id=1, source_target_pairs={{0,24},{8,0},{16,8},{24,16},{1,25},{9,1},{17,9},{25,17},{2,26},{10... | collective-permute-start | bytes 1572872 | tf_op jit(solution)/shard_map/normed3/ppermute | solution.py:212
  58.2 4.2 %collective-permute-start.1 = (bf16[64,2048]{1,0:T(8,128)(2,1)S(1)}, bf16[64,2048]{1,0:T(8,128)(2,1)S(1)}, u32[]{:S(2)}, u32[]{:S(2)}) collective-permute-start(bf16[64,2048]{1,0:T(8,128)(2,1)S(1)} %copy-done.15), channel_id=1, source_target_pairs={{0,2},{1,3},{2,4},{3,5},{4,6},{5,7},{6,0},{7,1},{8,10},{9,11},{10,... | collective-permute-start | bytes 786440 | tf_op jit(solution)/shard_map/hidden1/ppermute | solution.py:230
  62.4 4.8 %collective-permute-start.2 = (bf16[64,2048]{1,0:T(8,128)(2,1)S(1)}, bf16[64,2048]{1,0:T(8,128)(2,1)S(1)}, u32[]{:S(2)}, u32[]{:S(2)}) collective-permute-start(bf16[64,2048]{1,0:T(8,128)(2,1)S(1)} %copy-done.14), channel_id=1, source_target_pairs={{0,4},{1,5},{2,6},{3,7},{4,0},{5,1},{6,2},{7,3},{8,12},{9,13},{10,... | collective-permute-start | bytes 786440 | tf_op jit(solution)/shard_map/hidden2/ppermute | solution.py:230
  67.2 0.0 collective-permute-done.4.n1
  67.2 0.0 copy-start.1
  67.2 0.0 copy-done.13
  67.2 5.0 %collective-permute-start.3 = (bf16[64,2048]{1,0:T(8,128)(2,1)S(1)}, bf16[64,2048]{1,0:T(8,128)(2,1)S(1)}, u32[]{:S(2)}, u32[]{:S(2)}) collective-permute-start(bf16[64,2048]{1,0:T(8,128)(2,1)S(1)} %copy-done.13), channel_id=1, source_target_pairs={{0,6},{1,7},{2,0},{3,1},{4,2},{5,3},{6,4},{7,5},{8,14},{9,15},{10,... | collective-permute-start | bytes 786440 | tf_op jit(solution)/shard_map/hidden3/ppermute | solution.py:230
  72.2 3.8 %collective-permute-done.5.n2 = bf16[128,2048]{1,0:T(8,128)(2,1)S(1)} collective-permute-done((bf16[128,2048]{1,0:T(8,128)(2,1)}, bf16[128,2048]{1,0:T(8,128)(2,1)S(1)}, u32[]{:S(2)}, u32[]{:S(2)}) %collective-permute-start.5) | collective-permute-done | bytes 524320 | tf_op jit(solution)/shard_map/normed2/ppermute | solution.py:212
  76.0 3.8 %collective-permute-done.6.n3 = bf16[128,2048]{1,0:T(8,128)(2,1)S(1)} collective-permute-done((bf16[128,2048]{1,0:T(8,128)(2,1)}, bf16[128,2048]{1,0:T(8,128)(2,1)S(1)}, u32[]{:S(2)}, u32[]{:S(2)}) %collective-permute-start.6) | collective-permute-done | bytes 524320 | tf_op jit(solution)/shard_map/normed3/ppermute | solution.py:212
  79.7 0.8 copy-done.3
  80.5 4.2 %valuesmm.1 = (f32[128,256]{1,0:T(8,128)}, bf16[128,256]{1,0:T(8,128)(2,1)}, bf16[128,256]{1,0:T(8,128)(2,1)}, bf16[128,256]{1,0:T(8,128)(2,1)}) custom-call(bf16[128,2048]{1,0:T(8,128)(2,1)} %get-tuple-element.31.n0, bf16[128,2048]{1,0:T(8,128)(2,1)} %copy-done.1, bf16[128,2048]{1,0:T(8,128)(2,1)} %copy-done.2, bf16[128,2048]{1,0:T(8,128)(2,1)} %copy-done.3, ...), custom_call_target="tpu_custom_call" | custom-call | flops 540000000 | bytes 3300000 | tf_op jit(solution)/shard_map/valuesmm/pallas_call | solution.py:245
  84.7 0.0 collective-permute-done.1.r1
  84.7 0.0 collective-permute-done.2.r2
  84.7 0.0 copy-start.7
  84.7 5.6 %collective-permute-done.3.r3 = bf16[64,2048]{1,0:T(8,128)(2,1)S(1)} collective-permute-done((bf16[64,2048]{1,0:T(8,128)(2,1)S(1)}, bf16[64,2048]{1,0:T(8,128)(2,1)S(1)}, u32[]{:S(2)}, u32[]{:S(2)}) %collective-permute-start.3) | collective-permute-done | bytes 262176 | tf_op jit(solution)/shard_map/hidden3/ppermute | solution.py:230
  90.3 0.0 copy-done.6
  90.3 0.7 copy-done.8
  91.0 2.7 %merge.1 = (f32[16,2048]{1,0:T(8,128)}, bf16[256,256]{1,0:T(8,128)(2,1)}, bf16[256,256]{1,0:T(8,128)(2,1)}, bf16[256,256]{1,0:T(8,128)(2,1)}) custom-call(s32[4]{0:T(128)} %pad_add_fusion.idx, bf16[64,2048]{1,0:T(8,128)(2,1)} %get-tuple-element.27.h0, bf16[64,2048]{1,0:T(8,128)(2,1)} %copy-done.6, bf16[64,2048]{1,0:T(8,128)(2,1)} %copy-done.7, ...), custom_call_target="tpu_custom_call" | custom-call | flops 1000000 | bytes 1700000 | tf_op jit(solution)/shard_map/merge/pallas_call | solution.py:270
  93.7 4.8 %collective-permute-start.7 = (bf16[256,256]{1,0:T(8,128)(2,1)}, bf16[256,256]{1,0:T(8,128)(2,1)S(1)}, u32[]{:S(2)}, u32[]{:S(2)}) collective-permute-start(bf16[256,256]{1,0:T(8,128)(2,1)} %get-tuple-element.39), channel_id=1, source_target_pairs={{0,8},{8,16},{16,24},{24,0},{1,9},{9,17},{17,25},{25,1},{2,10},{10... | collective-permute-start | bytes 393224 | tf_op jit(solution)/shard_map/last1/ppermute | solution.py:283
  98.5 3.4 %collective-permute-start.8 = (bf16[256,256]{1,0:T(8,128)(2,1)}, bf16[256,256]{1,0:T(8,128)(2,1)S(1)}, u32[]{:S(2)}, u32[]{:S(2)}) collective-permute-start(bf16[256,256]{1,0:T(8,128)(2,1)} %get-tuple-element.40), channel_id=1, source_target_pairs={{0,16},{8,24},{16,0},{24,8},{1,17},{9,25},{17,1},{25,9},{2,18},{10... | collective-permute-start | bytes 393224 | tf_op jit(solution)/shard_map/last2/ppermute | solution.py:283
  101.9 4.0 %collective-permute-start.9 = (bf16[256,256]{1,0:T(8,128)(2,1)}, bf16[256,256]{1,0:T(8,128)(2,1)S(1)}, u32[]{:S(2)}, u32[]{:S(2)}) collective-permute-start(bf16[256,256]{1,0:T(8,128)(2,1)} %get-tuple-element.41), channel_id=1, source_target_pairs={{0,24},{8,0},{16,8},{24,16},{1,25},{9,1},{17,9},{25,17},{2,26},{10... | collective-permute-start | bytes 393224 | tf_op jit(solution)/shard_map/last3/ppermute | solution.py:283
  105.9 5.5 %wgradmm.1 = bf16[1,2048,256]{2,1,0:T(8,128)(2,1)} custom-call(s32[4]{0:T(128)} %pad_add_fusion.idx, bf16[128,2048]{1,0:T(8,128)(2,1)} %get-tuple-element.31.n0, bf16[128,2048]{1,0:T(8,128)(2,1)} %copy-done.1, bf16[128,2048]{1,0:T(8,128)(2,1)} %copy-done.2, bf16[128,2048]{1,0:T(8,128)(2,1)} %copy-done.3, bf16[8,128,256]{2,1,0:T(8,128)(2,1)} %copy-done), custom_call_target="tpu_custom_call" | custom-call | flops 540000000 | bytes 3600000 | tf_op jit(solution)/shard_map/wgradmm/pallas_call | solution.py:258
  111.4 0.0 collective-permute-done.7.m1
  111.4 0.0 collective-permute-done.8.m2
  111.4 0.0 collective-permute-done.9.m3
  111.4 0.6 copy-done.9
  112.0 0.1 copy-done.10
  112.1 0.0 copy-done.11
  112.1 2.9 %final.1 = (bf16[16,8192]{1,0:T(8,128)(2,1)}, bf16[128,256]{1,0:T(8,128)(2,1)}) custom-call(s32[4]{0:T(128)} %pad_add_fusion.idx, f32[16,2048]{1,0:T(8,128)} %get-tuple-element.38.keep, bf16[256,256]{1,0:T(8,128)(2,1)} %copy-done.9, bf16[256,256]{1,0:T(8,128)(2,1)} %copy-done.10, bf16[256,256]{1,0:T(8,128)(2,1)} %copy-done.11, ...), custom_call_target="tpu_custom_call" | custom-call | flops 2000000 | bytes 1500000 | tf_op jit(solution)/shard_map/final/pallas_call | solution.py:285
  115.0 0.0 all-to-all-done.1.g_ref
  115.0 0.7 copy-done.4
  115.8 1.7 %outerstep.1 = (f32[64,128]{1,0:T(8,128)}, f32[64,128]{1,0:T(8,128)}) custom-call(bf16[24,64,128]{2,1,0:T(8,128)(2,1)} %copy-done.4, f32[64,128]{1,0:T(8,128)} %p_ref.1, f32[64,128]{1,0:T(8,128)} %m_ref.1), custom_call_target="tpu_custom_call" | custom-call | flops 500000 | bytes 600000 | tf_op jit(solution)/shard_map/outerstep/pallas_call | solution.py:302
  (19 shorter events, 0.0 us)
Async XLA Ops:
  0.6 26.9 %collective-permute-start = (bf16[2048,256]{1,0:T(8,128)(2,1)}, bf16[2048,256]{1,0:T(8,128)(2,1)S(1)}, u32[]{:S(2)}, u32[]{:S(2)}) collective-permute-start(bf16[2048,256]{1,0:T(8,128)(2,1)} %w_ref.3), channel_id=1, source_target_pairs={{0,1},{1,0},{2,3},{3,2},{4,5},{5,4},{6,7},{7,6},{8,9},{9,8},{10,11... | collective-permute-start | bytes 3145736 | tf_op jit(solution)/shard_map/wswap/ppermute | solution.py:194
  14.7 12.8 %all-to-all-start = ((bf16[8,128,256]{2,1,0:T(8,128)(2,1)}), bf16[8,128,256]{2,1,0:T(8,128)(2,1)S(1)}, u32[]{:S(2)}, u32[]{:S(2)}) async-start(bf16[8,128,256]{2,1,0:T(8,128)(2,1)} %spread.1), calls=%async_computation | async-start | bytes 1048576 | tf_op jit(solution)/shard_map/cotgather/all_to_all | solution.py:190
  18.2 24.3 %copy-start.12 = (bf16[8192]{0:T(1024)(128)(2,1)S(1)}, bf16[8192]{0:T(1024)(128)(2,1)}, u32[]{:S(2)}) copy-start(bf16[8192]{0:T(1024)(128)(2,1)} %param.8) | copy-start | bytes 49156
  27.5 0.8 copy-start
  28.3 1.0 copy-start.5
  34.2 24.0 %copy-start.15 = (bf16[64,2048]{1,0:T(8,128)(2,1)S(1)}, bf16[64,2048]{1,0:T(8,128)(2,1)}, u32[]{:S(2)}) copy-start(bf16[64,2048]{1,0:T(8,128)(2,1)} %get-tuple-element.28) | copy-start | bytes 786436
  34.2 28.2 %copy-start.14 = (bf16[64,2048]{1,0:T(8,128)(2,1)S(1)}, bf16[64,2048]{1,0:T(8,128)(2,1)}, u32[]{:S(2)}) copy-start(bf16[64,2048]{1,0:T(8,128)(2,1)} %get-tuple-element.29) | copy-start | bytes 786436
  34.2 33.0 %copy-start.13 = (bf16[64,2048]{1,0:T(8,128)(2,1)S(1)}, bf16[64,2048]{1,0:T(8,128)(2,1)}, u32[]{:S(2)}) copy-start(bf16[64,2048]{1,0:T(8,128)(2,1)} %get-tuple-element.30) | copy-start | bytes 786436
  34.2 80.8 %all-to-all-start.1 = ((bf16[24,64,128]{2,1,0:T(8,128)(2,1)}), bf16[24,64,128]{2,1,0:T(8,128)(2,1)S(1)}, u32[]{:S(2)}, u32[]{:S(2)}) async-start(bf16[24,64,128]{2,1,0:T(8,128)(2,1)} %outerpack.1), calls=%async_computation.1 | async-start | bytes 786432 | tf_op jit(solution)/shard_map/outer/all_to_all | solution.py:243
  49.7 17.4 %collective-permute-start.4 = (bf16[128,2048]{1,0:T(8,128)(2,1)}, bf16[128,2048]{1,0:T(8,128)(2,1)S(1)}, u32[]{:S(2)}, u32[]{:S(2)}) collective-permute-start(bf16[128,2048]{1,0:T(8,128)(2,1)} %get-tuple-element.32), channel_id=1, source_target_pairs={{0,8},{8,16},{16,24},{24,0},{1,9},{9,17},{17,25},{25,1},{2,10},{10... | collective-permute-start | bytes 1572872 | tf_op jit(solution)/shard_map/normed1/ppermute | solution.py:212
  51.9 24.0 %collective-permute-start.5 = (bf16[128,2048]{1,0:T(8,128)(2,1)}, bf16[128,2048]{1,0:T(8,128)(2,1)S(1)}, u32[]{:S(2)}, u32[]{:S(2)}) collective-permute-start(bf16[128,2048]{1,0:T(8,128)(2,1)} %get-tuple-element.33), channel_id=1, source_target_pairs={{0,16},{8,24},{16,0},{24,8},{1,17},{9,25},{17,1},{25,9},{2,18},{10... | collective-permute-start | bytes 1572872 | tf_op jit(solution)/shard_map/normed2/ppermute | solution.py:212
  55.6 24.1 %collective-permute-start.6 = (bf16[128,2048]{1,0:T(8,128)(2,1)}, bf16[128,2048]{1,0:T(8,128)(2,1)S(1)}, u32[]{:S(2)}, u32[]{:S(2)}) collective-permute-start(bf16[128,2048]{1,0:T(8,128)(2,1)} %get-tuple-element.34), channel_id=1, source_target_pairs={{0,24},{8,0},{16,8},{24,16},{1,25},{9,1},{17,9},{25,17},{2,26},{10... | collective-permute-start | bytes 1572872 | tf_op jit(solution)/shard_map/normed3/ppermute | solution.py:212
  58.2 26.5 %collective-permute-start.1 = (bf16[64,2048]{1,0:T(8,128)(2,1)S(1)}, bf16[64,2048]{1,0:T(8,128)(2,1)S(1)}, u32[]{:S(2)}, u32[]{:S(2)}) collective-permute-start(bf16[64,2048]{1,0:T(8,128)(2,1)S(1)} %copy-done.15), channel_id=1, source_target_pairs={{0,2},{1,3},{2,4},{3,5},{4,6},{5,7},{6,0},{7,1},{8,10},{9,11},{10,... | collective-permute-start | bytes 786440 | tf_op jit(solution)/shard_map/hidden1/ppermute | solution.py:230
  62.4 22.3 %collective-permute-start.2 = (bf16[64,2048]{1,0:T(8,128)(2,1)S(1)}, bf16[64,2048]{1,0:T(8,128)(2,1)S(1)}, u32[]{:S(2)}, u32[]{:S(2)}) collective-permute-start(bf16[64,2048]{1,0:T(8,128)(2,1)S(1)} %copy-done.14), channel_id=1, source_target_pairs={{0,4},{1,5},{2,6},{3,7},{4,0},{5,1},{6,2},{7,3},{8,12},{9,13},{10,... | collective-permute-start | bytes 786440 | tf_op jit(solution)/shard_map/hidden2/ppermute | solution.py:230
  67.2 12.5 %copy-start.1 = (bf16[128,2048]{1,0:T(8,128)(2,1)}, bf16[128,2048]{1,0:T(8,128)(2,1)S(1)}, u32[]{:S(2)}) copy-start(bf16[128,2048]{1,0:T(8,128)(2,1)S(1)} %collective-permute-done.4.n1) | copy-start | bytes 1572868
  67.2 23.1 %collective-permute-start.3 = (bf16[64,2048]{1,0:T(8,128)(2,1)S(1)}, bf16[64,2048]{1,0:T(8,128)(2,1)S(1)}, u32[]{:S(2)}, u32[]{:S(2)}) collective-permute-start(bf16[64,2048]{1,0:T(8,128)(2,1)S(1)} %copy-done.13), channel_id=1, source_target_pairs={{0,6},{1,7},{2,0},{3,1},{4,2},{5,3},{6,4},{7,5},{8,14},{9,15},{10,... | collective-permute-start | bytes 786440 | tf_op jit(solution)/shard_map/hidden3/ppermute | solution.py:230
  76.0 3.8 %copy-start.2 = (bf16[128,2048]{1,0:T(8,128)(2,1)}, bf16[128,2048]{1,0:T(8,128)(2,1)S(1)}, u32[]{:S(2)}) copy-start(bf16[128,2048]{1,0:T(8,128)(2,1)S(1)} %collective-permute-done.5.n2) | copy-start | bytes 1572868
  79.7 0.8 copy-start.3
  84.7 5.6 %copy-start.6 = (bf16[64,2048]{1,0:T(8,128)(2,1)}, bf16[64,2048]{1,0:T(8,128)(2,1)S(1)}, u32[]{:S(2)}) copy-start(bf16[64,2048]{1,0:T(8,128)(2,1)S(1)} %collective-permute-done.1.r1) | copy-start | bytes 786436
  84.7 5.6 %copy-start.7 = (bf16[64,2048]{1,0:T(8,128)(2,1)}, bf16[64,2048]{1,0:T(8,128)(2,1)S(1)}, u32[]{:S(2)}) copy-start(bf16[64,2048]{1,0:T(8,128)(2,1)S(1)} %collective-permute-done.2.r2) | copy-start | bytes 786436
  90.3 0.7 copy-start.8
  93.7 17.6 %collective-permute-start.7 = (bf16[256,256]{1,0:T(8,128)(2,1)}, bf16[256,256]{1,0:T(8,128)(2,1)S(1)}, u32[]{:S(2)}, u32[]{:S(2)}) collective-permute-start(bf16[256,256]{1,0:T(8,128)(2,1)} %get-tuple-element.39), channel_id=1, source_target_pairs={{0,8},{8,16},{16,24},{24,0},{1,9},{9,17},{17,25},{25,1},{2,10},{10... | collective-permute-start | bytes 393224 | tf_op jit(solution)/shard_map/last1/ppermute | solution.py:283
  98.5 12.9 %collective-permute-start.8 = (bf16[256,256]{1,0:T(8,128)(2,1)}, bf16[256,256]{1,0:T(8,128)(2,1)S(1)}, u32[]{:S(2)}, u32[]{:S(2)}) collective-permute-start(bf16[256,256]{1,0:T(8,128)(2,1)} %get-tuple-element.40), channel_id=1, source_target_pairs={{0,16},{8,24},{16,0},{24,8},{1,17},{9,25},{17,1},{25,9},{2,18},{10... | collective-permute-start | bytes 393224 | tf_op jit(solution)/shard_map/last2/ppermute | solution.py:283
  101.9 9.5 %collective-permute-start.9 = (bf16[256,256]{1,0:T(8,128)(2,1)}, bf16[256,256]{1,0:T(8,128)(2,1)S(1)}, u32[]{:S(2)}, u32[]{:S(2)}) collective-permute-start(bf16[256,256]{1,0:T(8,128)(2,1)} %get-tuple-element.41), channel_id=1, source_target_pairs={{0,24},{8,0},{16,8},{24,16},{1,25},{9,1},{17,9},{25,17},{2,26},{10... | collective-permute-start | bytes 393224 | tf_op jit(solution)/shard_map/last3/ppermute | solution.py:283
  111.4 0.6 copy-start.9
  111.4 0.7 copy-start.10
  111.4 0.7 copy-start.11
  115.0 0.7 copy-start.4

commit v3 on v2

v3 whole, which is shorter than its diff:
```python
import jax
import jax.numpy as jnp
from jax import lax
from jax.experimental import pallas as pl
from jax.experimental.pallas import tpu as pltpu
from jax.sharding import PartitionSpec as P


norm_epsilon = 1e-05
outer_rate = 0.7
outer_beta = 0.9
CORES = 2
SHARDS = 4
CHIPS = 4
F32 = jnp.float32
BF16 = jnp.bfloat16


def cost(flops, moved):
    return pl.CostEstimate(flops=flops, bytes_accessed=moved, transcendentals=0)


def whole(shape):
    return pl.BlockSpec(shape, lambda *_: (0,) * len(shape))


def spread_kernel(x_ref, o_ref, sems):
    copies = [pltpu.make_async_copy(x_ref, o_ref.at[i], sems.at[i]) for i in range(o_ref.shape[0])]
    for copy in copies:
        copy.start()
    for copy in copies:
        copy.wait()


def pack_kernel(idx, x_ref, g_ref, o0, o1, o2, o3, inv_ref):
    width = x_ref.shape[1]
    part = width // SHARDS
    chunk = 512
    total = jnp.zeros((x_ref.shape[0], chunk), F32)
    for q in range(width // chunk):
        wide = x_ref[:, q * chunk:(q + 1) * chunk].astype(F32)
        total += wide * wide
    inv = lax.rsqrt(jnp.sum(total, axis=1, keepdims=True) / width + norm_epsilon)
    inv_ref[...] = jnp.broadcast_to(inv, inv_ref.shape)
    for k, out in enumerate((o0, o1, o2, o3)):
        begin = (idx[2] ^ k) * part
        for q in range(part // chunk):
            at = pl.ds(pl.multiple_of(begin + q * chunk, chunk), chunk)
            wide = x_ref[:, at].astype(F32)
            out[:, q * chunk:(q + 1) * chunk] = (wide * inv * g_ref[:, at]).astype(BF16)


def rows_kernel(idx, cots, own, oth):
    core, chip = idx[0], idx[1]
    for j in range(CHIPS):
        row = pl.multiple_of((CORES * (chip ^ j) + core) * 16, 16)
        for s in range(SHARDS):
            to = slice(j * 64 + s * 16, j * 64 + (s + 1) * 16)
            own[to, :] = cots[CORES * s + core, pl.ds(row, 16), :]
            oth[to, :] = cots[CORES * s + 1 - core, pl.ds(row, 16), :]


def merge_kernel(idx, h0, r1, r2, r3, v1, v2, v3, keep, m1, m2, m3):
    cols = m1.shape[1]
    tokens = v1.shape[0]
    for k, out in enumerate((keep, m1, m2, m3)):
        at = pl.ds(pl.multiple_of((idx[2] ^ k) * 16, 16), 16)
        for q in range(h0.shape[1] // cols):
            lanes = slice(q * cols, (q + 1) * cols)
            total = h0[at, lanes].astype(F32) + r1[at, lanes].astype(F32)
            total += r2[at, lanes].astype(F32) + r3[at, lanes].astype(F32)
            if k == 0:
                out[:, lanes] = total
            else:
                out[q * 16:(q + 1) * 16, :] = total.astype(BF16)
    for out, val in ((m1, v1), (m2, v2), (m3, v3)):
        out[tokens:, :] = val[...]


def final_kernel(idx, keep, m1, m2, m3, v0, x_ref, inv_ref, g_ref, o_ref, val_ref):
    part = keep.shape[1]
    tokens, cols = v0.shape
    width = x_ref.shape[1]
    inv = inv_ref[:, :1]
    places = []
    for k, got in enumerate((keep, m1, m2, m3)):
        begin = (idx[2] ^ k) * part
        for q in range(part // cols):
            at = pl.ds(pl.multiple_of(begin + q * cols, cols), cols)
            places.append((k, got, q, at))

    def scaled(k, got, q, at):
        if k == 0:
            term = got[:, q * cols:(q + 1) * cols]
        else:
            term = got[q * 16:(q + 1) * 16, :].astype(F32)
        return g_ref[:, at] * term

    total = jnp.zeros((16, cols), F32)
    for place in places:
        total += x_ref[:, place[3]].astype(F32) * scaled(*place)
    mean = jnp.sum(total, axis=1, keepdims=True) / width
    factor = inv * inv * inv * mean
    for place in places:
        at = place[3]
        o_ref[:, at] = (inv * scaled(*place) - x_ref[:, at].astype(F32) * factor).astype(BF16)
    summed = v0[...]
    for got in (m1, m2, m3):
        summed += got[tokens:, :].astype(F32)
    val_ref[...] = summed.astype(BF16)


def outer_pack_kernel(x_ref, o_ref):
    cols = o_ref.shape[2]
    for r in range(o_ref.shape[0]):
        o_ref[r] = x_ref[0, :, r * cols:(r + 1) * cols].astype(BF16)


def outer_kernel(g_ref, p_ref, m_ref, new_p, new_m):
    replicas = g_ref.shape[0]
    total = g_ref[0].astype(F32)
    for r in range(1, replicas):
        total += g_ref[r].astype(F32)
    average = total / replicas
    momentum = outer_beta * m_ref[...] + average
    new_m[...] = momentum
    new_p[...] = p_ref[...] - outer_rate * (average + outer_beta * momentum)


def body(inputs, gain, value_weight, value_cot, pseudo_grad, global_params, momentum):
    tensors = lax.axis_size("tensor")
    replicas = lax.axis_size("replica")
    tokens, width = inputs.shape
    rows, cols = value_weight.shape
    tensor = lax.axis_index("tensor")
    shard = lax.axis_index("shard")
    idx = jnp.stack([tensor % CORES, tensor // CORES, shard, tensor]).astype(jnp.int32)
    swap = [(i, i ^ 1) for i in range(tensors)]
    chip_shift = lambda j: [
        (t, (t // CORES ^ j) * CORES + t % CORES) for t in range(tensors)
    ]
    shard_shift = lambda k: [(s, s ^ k) for s in range(SHARDS)]
    near = [
        [s * tensors + h * CORES + c for s in range(SHARDS) for c in range(CORES)]
        for h in range(CHIPS)
    ]
    fan = SHARDS * CORES
    spec = jax.ShapeDtypeStruct
    rest = (1, 3, 2)

    spread = pl.pallas_call(
        spread_kernel, out_shape=spec((fan, tokens, cols), BF16),
        in_specs=[pl.BlockSpec(memory_space=pltpu.VMEM)],
        out_specs=pl.BlockSpec(memory_space=pl.ANY),
        scratch_shapes=[pltpu.SemaphoreType.DMA((fan,))],
        cost_estimate=cost(0, 600_000), name="spread",
    )(value_cot)
    cots = lax.all_to_all(
        spread, ("shard", "tensor"), 0, 0, axis_index_groups=near, tiled=True
    )
    other_weight = lax.ppermute(value_weight, "tensor", swap)

    gain_row = gain.astype(F32).reshape(1, width)
    part = width // SHARDS
    packing = pl.pallas_call(
        pack_kernel,
        grid_spec=pltpu.PrefetchScalarGridSpec(
            num_scalar_prefetch=1, grid=(tokens // 16,),
            in_specs=[pl.BlockSpec((16, width), lambda i, _: (i, 0)), whole((1, width))],
            out_specs=[pl.BlockSpec((16, part), lambda i, _: (i, 0))] * SHARDS
            + [pl.BlockSpec((16, 128), lambda i, _: (i, 0))],
        ),
        out_shape=[spec((tokens, part), BF16)] * SHARDS + [spec((tokens, 128), F32)],
        cost_estimate=cost(6_000_000, 4_300_000), name="pack",
    )
    *sent, inv_scale = packing(idx, inputs, gain_row)
    normed = [sent[0], None, None, None]
    for k in rest:
        normed[k] = lax.ppermute(sent[k], "shard", shard_shift(k))

    own_rows, other_rows = pl.pallas_call(
        rows_kernel,
        grid_spec=pltpu.PrefetchScalarGridSpec(
            num_scalar_prefetch=1, grid=(1,),
            in_specs=[whole((fan, tokens, cols))],
            out_specs=[whole((256, cols))] * 2,
        ),
        out_shape=[spec((256, cols), BF16)] * 2,
        cost_estimate=cost(0, 800_000), name="rows",
    )(idx, cots)
    last_dims = (((1,), (1,)), ((), ()))
    product = lax.dot_general(own_rows, value_weight, last_dims, preferred_element_type=F32)
    product += lax.dot_general(other_rows, other_weight, last_dims, preferred_element_type=F32)
    product = product.astype(BF16)
    outs = [product[j * 64:(j + 1) * 64] for j in range(CHIPS)]
    hidden = [outs[0], None, None, None]
    for j in rest:
        hidden[j] = lax.ppermute(outs[j], "tensor", chip_shift(j))

    frows, fcols = pseudo_grad.shape[1:]
    own_cols = fcols // replicas
    outer_packing = pl.pallas_call(
        outer_pack_kernel, grid=(3,),
        in_specs=[pl.BlockSpec((1, frows, fcols // 3), lambda i: (0, 0, i))],
        out_specs=pl.BlockSpec((replicas // 3, frows, own_cols), lambda i: (i, 0, 0)),
        out_shape=spec((replicas, frows, own_cols), BF16),
        cost_estimate=cost(0, 1_200_000), name="outerpack",
    )
    packed = outer_packing(pseudo_grad)
    grads = lax.all_to_all(packed, "replica", 0, 0, tiled=True)

    partial_values = [
        jnp.dot(block, value_weight, preferred_element_type=F32) for block in normed
    ]
    partial_values[1:] = [part.astype(BF16) for part in partial_values[1:]]

    own_cots = [
        lax.dynamic_index_in_dim(cots, CORES * (shard ^ k) + tensor % CORES, 0, keepdims=False)
        for k in range(SHARDS)
    ]
    weight_grad = lax.dot_general(
        jnp.concatenate(normed, axis=0), jnp.concatenate(own_cots, axis=0),
        (((0,), (0,)), ((), ())), preferred_element_type=F32,
    ).astype(BF16)[None]

    keep, *merged = pl.pallas_call(
        merge_kernel,
        grid_spec=pltpu.PrefetchScalarGridSpec(
            num_scalar_prefetch=1, grid=(1,),
            in_specs=[whole((64, rows))] * CHIPS + [whole((tokens, cols))] * 3,
            out_specs=[whole((16, rows))] + [whole((2 * tokens, cols))] * 3,
        ),
        out_shape=[spec((16, rows), F32)] + [spec((2 * tokens, cols), BF16)] * 3,
        cost_estimate=cost(1_000_000, 1_700_000), name="merge",
    )(idx, *hidden, *partial_values[1:])
    got = [None] * SHARDS
    for k in rest:
        got[k] = lax.ppermute(merged[k - 1], "shard", shard_shift(k))

    input_grad, values = pl.pallas_call(
        final_kernel,
        grid_spec=pltpu.PrefetchScalarGridSpec(
            num_scalar_prefetch=1, grid=(1,),
            in_specs=[whole((16, rows))] + [whole((2 * tokens, cols))] * 3
            + [
                whole((tokens, cols)),
                pl.BlockSpec((16, width), lambda i, at: (at[3], 0)),
                pl.BlockSpec((16, 128), lambda i, at: (at[3], 0)),
                whole((1, width)),
            ],
            out_specs=[whole((16, width)), whole((tokens, cols))],
        ),
        out_shape=[spec((16, width), BF16), spec((tokens, cols), BF16)],
        cost_estimate=cost(2_000_000, 1_500_000), name="final",
    )(idx, keep, *got[1:], partial_values[0], inputs, inv_scale, gain_row)

    new_global, new_momentum = pl.pallas_call(
        outer_kernel, out_shape=[spec(momentum.shape, F32)] * 2,
        cost_estimate=cost(500_000, 600_000), name="outerstep",
    )(grads, global_params, momentum)
    return (values, weight_grad, input_grad, new_global, new_momentum)


def solution(mesh):
    placed = (
        P(("replica", "shard"), None),
        P(),
        P("shard", "tensor"),
        P(("replica", "shard"), "tensor"),
        P("replica", ("shard", "tensor"), None),
        P(("shard", "tensor"), "replica"),
        P(("shard", "tensor"), "replica"),
    )
    return jax.shard_map(
        body,
        mesh=mesh,
        in_specs=placed,
        out_specs=(
            P(("replica", "shard"), "tensor"),
            P("replica", "shard", "tensor"),
            P(("replica", "shard", "tensor"), None),
            P(("shard", "tensor"), "replica"),
            P(("shard", "tensor"), "replica"),
        ),
        check_vma=False,
    )
```

time: 119 us -> 117 us (0.983)
  the two profiles are of different devices: /device:TPU:1 before, /device:TPU:16 now
where the time goes in v3:
time: 117 us; the launch traced here: 116 us
  starting transfers between devices  56.1 us (48%)
  Pallas kernels  20.9 us (18%)
  waiting for transfers between devices  20.1 us (17%)
  matrix products  11.7 us (10%)
  local copies, waits for them, and re-layouts  4.56 us (4%)
  other arithmetic  1.98 us (2%)
    ppermute x3, waiting for transfers between devices, body(): hidden[j] = lax.ppermute(outs[j], 'tensor', chip_shift(j))  19.4 us
    all_to_all x1, starting transfers between devices, body(): grads = lax.all_to_all(packed, 'replica', 0, 0, tiled=True)  16.4 us
    ppermute x3, starting transfers between devices, body(): hidden[j] = lax.ppermute(outs[j], 'tensor', chip_shift(j))  12.2 us
    ppermute x3, starting transfers between devices, body(): normed[k] = lax.ppermute(sent[k], 'shard', shard_shift(k))  10.4 us
    ppermute x3, starting transfers between devices, body(): got[k] = lax.ppermute(merged[k - 1], 'shard', shard_shift(k))  10.4 us
    dot_general x4, matrix products, body(): jnp.dot(block, value_weight, preferred_element_type=F32)  6.91 us
    pallas_call x1, Pallas kernels, body(): *sent, inv_scale = packing(idx, inputs, gain_row)  6.7 us
    all_to_all x1, starting transfers between devices, body(): lax.all_to_all(spread, ('shard', 'tensor'), 0, 0, axis_index_groups=near,...  4.31 us
  transfers between devices with their start and end apart: 12, of which 3 were waited for; matrix products, arithmetic and copies ran while one was open for 14% of the time, Pallas kernels for 14%

profile of v3, /device:TPU:16, one launch (start us, length us, event | category | flops | bytes accessed | tf_op | source)
XLA Modules:
  0.0 116.2 jit_solution(11256010280113032467)
XLA Ops:
  0.6 0.0 copy-start
  0.6 1.8 %spread.1 = bf16[8,128,256]{2,1,0:T(8,128)(2,1)} custom-call(bf16[128,256]{1,0:T(8,128)(2,1)} %x_ref.4), custom_call_target="tpu_custom_call" | custom-call | bytes 600000 | tf_op jit(solution)/shard_map/spread/pallas_call | solution.py:151
  2.4 4.3 %all-to-all-start = ((bf16[8,128,256]{2,1,0:T(8,128)(2,1)}), bf16[8,128,256]{2,1,0:T(8,128)(2,1)S(1)}, u32[]{:S(2)}, u32[]{:S(2)}) async-start(bf16[8,128,256]{2,1,0:T(8,128)(2,1)} %spread.1), calls=%async_computation | async-start | bytes 1048576 | tf_op jit(solution)/shard_map/all_to_all | solution.py:158
  6.7 2.4 %collective-permute-start = (bf16[2048,256]{1,0:T(8,128)(2,1)}, bf16[2048,256]{1,0:T(8,128)(2,1)S(1)}, u32[]{:S(2)}, u32[]{:S(2)}) collective-permute-start(bf16[2048,256]{1,0:T(8,128)(2,1)} %param.9), channel_id=1, source_target_pairs={{0,1},{1,0},{2,3},{3,2},{4,5},{5,4},{6,7},{7,6},{8,9},{9,8},{10,11... | collective-permute-start | bytes 3145736 | tf_op jit(solution)/shard_map/ppermute | solution.py:161
  9.2 1.3 %reshape.17 = f32[8192]{0:T(1024)} convert(bf16[8192]{0:T(1024)(128)(2,1)} %param.8) | non-fusion elementwise | flops 8192 | bytes 49152 | tf_op jit(solution)/shard_map/reshape | solution.py:163
  10.5 0.7 pad_add_fusion.idx
  11.1 6.7 %pack.1 = (bf16[128,2048]{1,0:T(8,128)(2,1)}, bf16[128,2048]{1,0:T(8,128)(2,1)}, bf16[128,2048]{1,0:T(8,128)(2,1)}, bf16[128,2048]{1,0:T(8,128)(2,1)}, f32[128,128]{1,0:T(8,128)}) custom-call(s32[4]{0:T(128)} %pad_add_fusion.idx, bf16[128,8192]{1,0:T(8,128)(2,1)} %x_ref.6, f32[1,8192]{1,0:T(1,128)} %bitcast.27), custom_call_target="tpu_custom_call" | custom-call | flops 6000000 | bytes 4300000 | tf_op jit(solution)/shard_map/pack/pallas_call | solution.py:176
  17.8 3.5 %collective-permute-start.4 = (bf16[128,2048]{1,0:T(8,128)(2,1)}, bf16[128,2048]{1,0:T(8,128)(2,1)S(1)}, u32[]{:S(2)}, u32[]{:S(2)}) collective-permute-start(bf16[128,2048]{1,0:T(8,128)(2,1)} %get-tuple-element.22), channel_id=1, source_target_pairs={{0,8},{8,0},{16,24},{24,16},{1,9},{9,1},{17,25},{25,17},{2,10},{10... | collective-permute-start | bytes 1572872 | tf_op jit(solution)/shard_map/ppermute | solution.py:179
  21.4 4.6 %collective-permute-start.5 = (bf16[128,2048]{1,0:T(8,128)(2,1)}, bf16[128,2048]{1,0:T(8,128)(2,1)}, u32[]{:S(2)}, u32[]{:S(2)}) collective-permute-start(bf16[128,2048]{1,0:T(8,128)(2,1)} %get-tuple-element.23), channel_id=1, source_target_pairs={{0,16},{8,24},{16,0},{24,8},{1,17},{9,25},{17,1},{25,9},{2,18},{10... | collective-permute-start | bytes 1572872 | tf_op jit(solution)/shard_map/ppermute | solution.py:179
  26.0 2.3 %collective-permute-start.6 = (bf16[128,2048]{1,0:T(8,128)(2,1)}, bf16[128,2048]{1,0:T(8,128)(2,1)}, u32[]{:S(2)}, u32[]{:S(2)}) collective-permute-start(bf16[128,2048]{1,0:T(8,128)(2,1)} %get-tuple-element.24), channel_id=1, source_target_pairs={{0,24},{8,16},{16,8},{24,0},{1,25},{9,17},{17,9},{25,1},{2,26},{10... | collective-permute-start | bytes 1572872 | tf_op jit(solution)/shard_map/ppermute | solution.py:179
  28.3 2.0 %fusion.19.v0 = f32[128,256]{1,0:T(8,128)} fusion(bf16[128,2048]{1,0:T(8,128)(2,1)} %get-tuple-element.29, bf16[2048,256]{1,0:T(8,128)(2,1)S(1)} %copy-done), kind=kOutput, calls=%fused_computation.29 | convolution fusion | flops 134217728 | bytes 1703936 | tf_op jit(solution)/shard_map/dot_general | solution.py:213
  30.3 2.7 %outerpack.1 = bf16[24,64,128]{2,1,0:T(8,128)(2,1)} custom-call(f32[1,64,3072]{2,1,0:T(8,128)} %x_ref.7), custom_call_target="tpu_custom_call" | custom-call | bytes 1200000 | tf_op jit(solution)/shard_map/outerpack/pallas_call | solution.py:209
  33.0 0.0 all-to-all-done.cots
  33.0 16.4 %all-to-all-start.1 = ((bf16[24,64,128]{2,1,0:T(8,128)(2,1)}), bf16[24,64,128]{2,1,0:T(8,128)(2,1)S(1)}, u32[]{:S(2)}, u32[]{:S(2)}) async-start(bf16[24,64,128]{2,1,0:T(8,128)(2,1)} %outerpack.1), calls=%async_computation.1 | async-start | bytes 786432 | tf_op jit(solution)/shard_map/all_to_all | solution.py:210
  49.4 2.4 %rows.1 = (bf16[256,256]{1,0:T(8,128)(2,1)}, bf16[256,256]{1,0:T(8,128)(2,1)}) custom-call(s32[4]{0:T(128)} %pad_add_fusion.idx, bf16[8,128,256]{2,1,0:T(8,128)(2,1)} %copy-done.1), custom_call_target="tpu_custom_call" | custom-call | bytes 800000 | tf_op jit(solution)/shard_map/rows/pallas_call | solution.py:181
  51.8 1.7 %dynamic-slice_bitcast_fusion.3 = (bf16[128,256]{1,0:T(8,128)(2,1)}, bf16[128,256]{1,0:T(8,128)(2,1)}, bf16[128,256]{1,0:T(8,128)(2,1)}, bf16[128,256]{1,0:T(8,128)(2,1)}) fusion(bf16[8,128,256]{2,1,0:T(8,128)(2,1)} %copy-done.1, s32[]{:T(128)S(6)} %select_n.34, s32[]{:T(128)S(6)} %select_n.37, s32[]{:T(128)S(6)} %select_n.36, s32[]{:T(128)S(6)} %select_n.35), kind=kLoop, calls=%fused_computation.24 | loop fusion | bytes 524304 | tf_op jit(solution)/shard_map/jit(dynamic_index_in_dim)/squeeze | solution.py:218
  53.5 1.4 %fusion.18 = f32[256,2048]{1,0:T(8,128)S(1)} fusion(bf16[256,256]{1,0:T(8,128)(2,1)} %get-tuple-element.20, bf16[2048,256]{1,0:T(8,128)(2,1)S(1)} %copy-done), kind=kOutput, calls=%fused_computation.28 | convolution fusion | flops 268435456 | bytes 3276800 | tf_op jit(solution)/shard_map/dot_general | solution.py:192
  54.8 0.0 collective-permute-done.4
  54.8 0.9 convolution_convert_fusion.3.v1
  55.8 0.0 collective-permute-done.5
  55.8 2.0 %convolution_convert_fusion.2.v2 = bf16[128,256]{1,0:T(8,128)(2,1)} fusion(bf16[128,2048]{1,0:T(8,128)(2,1)} %collective-permute-done.5, bf16[2048,256]{1,0:T(8,128)(2,1)S(1)} %copy-done), kind=kOutput, calls=%fused_computation.12 | convolution fusion | flops 134250496 | bytes 1638400 | tf_op jit(solution)/shard_map/dot_general | solution.py:213
  57.8 0.0 collective-permute-done
  57.8 0.5 fusion
  58.3 0.8 fusion.17
  59.1 2.4 %collective-permute-start.1 = (bf16[64,2048]{1,0:T(8,128)(2,1)S(1)}, bf16[64,2048]{1,0:T(8,128)(2,1)S(1)}, u32[]{:S(2)}, u32[]{:S(2)}) collective-permute-start(bf16[64,2048]{1,0:T(8,128)(2,1)S(1)} %get-tuple-element.37), channel_id=1, source_target_pairs={{0,2},{1,3},{2,0},{3,1},{4,6},{5,7},{6,4},{7,5},{8,10},{9,11},{10,... | collective-permute-start | bytes 786440 | tf_op jit(solution)/shard_map/ppermute | solution.py:198
  61.5 6.6 %collective-permute-start.2 = (bf16[64,2048]{1,0:T(8,128)(2,1)S(1)}, bf16[64,2048]{1,0:T(8,128)(2,1)S(1)}, u32[]{:S(2)}, u32[]{:S(2)}) collective-permute-start(bf16[64,2048]{1,0:T(8,128)(2,1)S(1)} %get-tuple-element.36), channel_id=1, source_target_pairs={{0,4},{1,5},{2,6},{3,7},{4,0},{5,1},{6,2},{7,3},{8,12},{9,13},{10,... | collective-permute-start | bytes 786440 | tf_op jit(solution)/shard_map/ppermute | solution.py:198
  68.1 3.1 %collective-permute-start.3 = (bf16[64,2048]{1,0:T(8,128)(2,1)S(1)}, bf16[64,2048]{1,0:T(8,128)(2,1)S(1)}, u32[]{:S(2)}, u32[]{:S(2)}) collective-permute-start(bf16[64,2048]{1,0:T(8,128)(2,1)S(1)} %get-tuple-element.35), channel_id=1, source_target_pairs={{0,6},{1,7},{2,4},{3,5},{4,2},{5,3},{6,0},{7,1},{8,14},{9,15},{10,... | collective-permute-start | bytes 786440 | tf_op jit(solution)/shard_map/ppermute | solution.py:198
  71.3 0.0 collective-permute-done.6
  71.3 2.0 %convolution_convert_fusion.1.v3 = bf16[128,256]{1,0:T(8,128)(2,1)} fusion(bf16[128,2048]{1,0:T(8,128)(2,1)} %collective-permute-done.6, bf16[2048,256]{1,0:T(8,128)(2,1)S(1)} %copy-done), kind=kOutput, calls=%fused_computation.11 | convolution fusion | flops 134250496 | bytes 1638400 | tf_op jit(solution)/shard_map/dot_general | solution.py:213
  73.3 10.2 %collective-permute-done.1.r1 = bf16[64,2048]{1,0:T(8,128)(2,1)S(1)} collective-permute-done((bf16[64,2048]{1,0:T(8,128)(2,1)S(1)}, bf16[64,2048]{1,0:T(8,128)(2,1)S(1)}, u32[]{:S(2)}, u32[]{:S(2)}) %collective-permute-start.1) | collective-permute-done | bytes 262176 | tf_op jit(solution)/shard_map/ppermute | solution.py:198
  83.5 0.0 collective-permute-done.2.r2
  83.5 9.1 %collective-permute-done.3.r3 = bf16[64,2048]{1,0:T(8,128)(2,1)S(1)} collective-permute-done((bf16[64,2048]{1,0:T(8,128)(2,1)S(1)}, bf16[64,2048]{1,0:T(8,128)(2,1)S(1)}, u32[]{:S(2)}, u32[]{:S(2)}) %collective-permute-start.3) | collective-permute-done | bytes 262176 | tf_op jit(solution)/shard_map/ppermute | solution.py:198
  92.7 0.7 copy-done.6
  93.4 2.8 %merge.1 = (f32[16,2048]{1,0:T(8,128)}, bf16[256,256]{1,0:T(8,128)(2,1)}, bf16[256,256]{1,0:T(8,128)(2,1)}, bf16[256,256]{1,0:T(8,128)(2,1)}) custom-call(s32[4]{0:T(128)} %pad_add_fusion.idx, bf16[64,2048]{1,0:T(8,128)(2,1)} %get-tuple-element.38.h0, bf16[64,2048]{1,0:T(8,128)(2,1)} %copy-done.4, bf16[64,2048]{1,0:T(8,128)(2,1)} %copy-done.5, ...), custom_call_target="tpu_custom_call" | custom-call | flops 1000000 | bytes 1700000 | tf_op jit(solution)/shard_map/merge/pallas_call | solution.py:226
  96.1 2.5 %collective-permute-start.7 = (bf16[256,256]{1,0:T(8,128)(2,1)}, bf16[256,256]{1,0:T(8,128)(2,1)S(1)}, u32[]{:S(2)}, u32[]{:S(2)}) collective-permute-start(bf16[256,256]{1,0:T(8,128)(2,1)} %get-tuple-element.26), channel_id=1, source_target_pairs={{0,8},{8,0},{16,24},{24,16},{1,9},{9,1},{17,25},{25,17},{2,10},{10... | collective-permute-start | bytes 393224 | tf_op jit(solution)/shard_map/ppermute | solution.py:238
  98.6 5.8 %collective-permute-start.8 = (bf16[256,256]{1,0:T(8,128)(2,1)}, bf16[256,256]{1,0:T(8,128)(2,1)S(1)}, u32[]{:S(2)}, u32[]{:S(2)}) collective-permute-start(bf16[256,256]{1,0:T(8,128)(2,1)} %get-tuple-element.27), channel_id=1, source_target_pairs={{0,16},{8,24},{16,0},{24,8},{1,17},{9,25},{17,1},{25,9},{2,18},{10... | collective-permute-start | bytes 393224 | tf_op jit(solution)/shard_map/ppermute | solution.py:238
  104.4 2.2 %collective-permute-start.9 = (bf16[256,256]{1,0:T(8,128)(2,1)}, bf16[256,256]{1,0:T(8,128)(2,1)S(1)}, u32[]{:S(2)}, u32[]{:S(2)}) collective-permute-start(bf16[256,256]{1,0:T(8,128)(2,1)} %get-tuple-element.28), channel_id=1, source_target_pairs={{0,24},{8,16},{16,8},{24,0},{1,25},{9,17},{17,9},{25,1},{2,26},{10... | collective-permute-start | bytes 393224 | tf_op jit(solution)/shard_map/ppermute | solution.py:238
  106.6 2.9 %fusion.1 = bf16[1,2048,256]{2,1,0:T(8,128)(2,1)} fusion(bf16[128,2048]{1,0:T(8,128)(2,1)} %collective-permute-done.6, bf16[128,2048]{1,0:T(8,128)(2,1)} %collective-permute-done.5, bf16[128,2048]{1,0:T(8,128)(2,1)S(1)} %collective-permute-done.4, bf16[128,2048]{1,0:T(8,128)(2,1)S(1)} %copy-done.3, bf16[128,256]{1,0:T(8,128)(2,1)} %get-tuple-element.40, ...), kind=kOutput, calls=%fused_computation.3 | convolution fusion | flops 546832384 | bytes 3407872 | tf_op jit(solution)/shard_map/dot_general | solution.py:221
  109.5 0.0 all-to-all-done.1.g_ref
  109.5 0.8 copy-done.2
  110.3 1.7 %outerstep.1 = (f32[64,128]{1,0:T(8,128)}, f32[64,128]{1,0:T(8,128)}) custom-call(bf16[24,64,128]{2,1,0:T(8,128)(2,1)} %copy-done.2, f32[64,128]{1,0:T(8,128)} %p_ref.1, f32[64,128]{1,0:T(8,128)} %m_ref.1), custom_call_target="tpu_custom_call" | custom-call | flops 500000 | bytes 600000 | tf_op jit(solution)/shard_map/outerstep/pallas_call | solution.py:257
  112.0 0.0 collective-permute-done.7.m1
  112.0 0.0 collective-permute-done.8.m2
  112.0 0.0 copy-start.8
  112.0 0.7 collective-permute-done.9.m3
  112.7 0.0 copy-done.8
  112.7 0.6 copy-done.9
  113.3 2.9 %final.1 = (bf16[16,8192]{1,0:T(8,128)(2,1)}, bf16[128,256]{1,0:T(8,128)(2,1)}) custom-call(s32[4]{0:T(128)} %pad_add_fusion.idx, f32[16,2048]{1,0:T(8,128)} %get-tuple-element.25.keep, bf16[256,256]{1,0:T(8,128)(2,1)} %copy-done.7, bf16[256,256]{1,0:T(8,128)(2,1)} %copy-done.8, bf16[256,256]{1,0:T(8,128)(2,1)} %copy-done.9, f32[128,256]{1,0:T(8,128)} %fusion.19.v0, ...), custom_call_target="tpu_custom_call" | custom-call | flops 2000000 | bytes 1500000 | tf_op jit(solution)/shard_map/final/pallas_call | solution.py:240
  (16 shorter events, 0.0 us)
Async XLA Ops:
  0.6 27.7 %copy-start = (bf16[2048,256]{1,0:T(8,128)(2,1)S(1)}, bf16[2048,256]{1,0:T(8,128)(2,1)}, u32[]{:S(2)}) copy-start(bf16[2048,256]{1,0:T(8,128)(2,1)} %param.9) | copy-start | bytes 3145732
  2.4 30.6 %all-to-all-start = ((bf16[8,128,256]{2,1,0:T(8,128)(2,1)}), bf16[8,128,256]{2,1,0:T(8,128)(2,1)S(1)}, u32[]{:S(2)}, u32[]{:S(2)}) async-start(bf16[8,128,256]{2,1,0:T(8,128)(2,1)} %spread.1), calls=%async_computation | async-start | bytes 1048576 | tf_op jit(solution)/shard_map/all_to_all | solution.py:158
  6.7 51.0 %collective-permute-start = (bf16[2048,256]{1,0:T(8,128)(2,1)}, bf16[2048,256]{1,0:T(8,128)(2,1)S(1)}, u32[]{:S(2)}, u32[]{:S(2)}) collective-permute-start(bf16[2048,256]{1,0:T(8,128)(2,1)} %param.9), channel_id=1, source_target_pairs={{0,1},{1,0},{2,3},{3,2},{4,5},{5,4},{6,7},{7,6},{8,9},{9,8},{10,11... | collective-permute-start | bytes 3145736 | tf_op jit(solution)/shard_map/ppermute | solution.py:161
  17.8 37.0 %collective-permute-start.4 = (bf16[128,2048]{1,0:T(8,128)(2,1)}, bf16[128,2048]{1,0:T(8,128)(2,1)S(1)}, u32[]{:S(2)}, u32[]{:S(2)}) collective-permute-start(bf16[128,2048]{1,0:T(8,128)(2,1)} %get-tuple-element.22), channel_id=1, source_target_pairs={{0,8},{8,0},{16,24},{24,16},{1,9},{9,1},{17,25},{25,17},{2,10},{10... | collective-permute-start | bytes 1572872 | tf_op jit(solution)/shard_map/ppermute | solution.py:179
  21.4 34.4 %collective-permute-start.5 = (bf16[128,2048]{1,0:T(8,128)(2,1)}, bf16[128,2048]{1,0:T(8,128)(2,1)}, u32[]{:S(2)}, u32[]{:S(2)}) collective-permute-start(bf16[128,2048]{1,0:T(8,128)(2,1)} %get-tuple-element.23), channel_id=1, source_target_pairs={{0,16},{8,24},{16,0},{24,8},{1,17},{9,25},{17,1},{25,9},{2,18},{10... | collective-permute-start | bytes 1572872 | tf_op jit(solution)/shard_map/ppermute | solution.py:179
  26.0 45.3 %collective-permute-start.6 = (bf16[128,2048]{1,0:T(8,128)(2,1)}, bf16[128,2048]{1,0:T(8,128)(2,1)}, u32[]{:S(2)}, u32[]{:S(2)}) collective-permute-start(bf16[128,2048]{1,0:T(8,128)(2,1)} %get-tuple-element.24), channel_id=1, source_target_pairs={{0,24},{8,16},{16,8},{24,0},{1,25},{9,17},{17,9},{25,1},{2,26},{10... | collective-permute-start | bytes 1572872 | tf_op jit(solution)/shard_map/ppermute | solution.py:179
  33.0 16.4 %copy-start.1 = (bf16[8,128,256]{2,1,0:T(8,128)(2,1)}, bf16[8,128,256]{2,1,0:T(8,128)(2,1)S(1)}, u32[]{:S(2)}) copy-start(bf16[8,128,256]{2,1,0:T(8,128)(2,1)S(1)} %all-to-all-done.cots) | copy-start | bytes 1572868
  33.0 76.5 %all-to-all-start.1 = ((bf16[24,64,128]{2,1,0:T(8,128)(2,1)}), bf16[24,64,128]{2,1,0:T(8,128)(2,1)S(1)}, u32[]{:S(2)}, u32[]{:S(2)}) async-start(bf16[24,64,128]{2,1,0:T(8,128)(2,1)} %outerpack.1), calls=%async_computation.1 | async-start | bytes 786432 | tf_op jit(solution)/shard_map/all_to_all | solution.py:210
  54.8 2.9 %copy-start.10 = (bf16[256,256]{1,0:T(8,128)(2,1)S(1)}, bf16[256,256]{1,0:T(8,128)(2,1)}, u32[]{:S(2)}) copy-start(bf16[256,256]{1,0:T(8,128)(2,1)} %get-tuple-element.21) | copy-start | bytes 393220
  58.3 48.3 %copy-start.3 = (bf16[128,2048]{1,0:T(8,128)(2,1)S(1)}, bf16[128,2048]{1,0:T(8,128)(2,1)}, u32[]{:S(2)}) copy-start(bf16[128,2048]{1,0:T(8,128)(2,1)} %get-tuple-element.29) | copy-start | bytes 1572868
  59.1 24.5 %collective-permute-start.1 = (bf16[64,2048]{1,0:T(8,128)(2,1)S(1)}, bf16[64,2048]{1,0:T(8,128)(2,1)S(1)}, u32[]{:S(2)}, u32[]{:S(2)}) collective-permute-start(bf16[64,2048]{1,0:T(8,128)(2,1)S(1)} %get-tuple-element.37), channel_id=1, source_target_pairs={{0,2},{1,3},{2,0},{3,1},{4,6},{5,7},{6,4},{7,5},{8,10},{9,11},{10,... | collective-permute-start | bytes 786440 | tf_op jit(solution)/shard_map/ppermute | solution.py:198
  61.5 22.0 %collective-permute-start.2 = (bf16[64,2048]{1,0:T(8,128)(2,1)S(1)}, bf16[64,2048]{1,0:T(8,128)(2,1)S(1)}, u32[]{:S(2)}, u32[]{:S(2)}) collective-permute-start(bf16[64,2048]{1,0:T(8,128)(2,1)S(1)} %get-tuple-element.36), channel_id=1, source_target_pairs={{0,4},{1,5},{2,6},{3,7},{4,0},{5,1},{6,2},{7,3},{8,12},{9,13},{10,... | collective-permute-start | bytes 786440 | tf_op jit(solution)/shard_map/ppermute | solution.py:198
  68.1 24.5 %collective-permute-start.3 = (bf16[64,2048]{1,0:T(8,128)(2,1)S(1)}, bf16[64,2048]{1,0:T(8,128)(2,1)S(1)}, u32[]{:S(2)}, u32[]{:S(2)}) collective-permute-start(bf16[64,2048]{1,0:T(8,128)(2,1)S(1)} %get-tuple-element.35), channel_id=1, source_target_pairs={{0,6},{1,7},{2,4},{3,5},{4,2},{5,3},{6,0},{7,1},{8,14},{9,15},{10,... | collective-permute-start | bytes 786440 | tf_op jit(solution)/shard_map/ppermute | solution.py:198
  83.5 9.2 %copy-start.4 = (bf16[64,2048]{1,0:T(8,128)(2,1)}, bf16[64,2048]{1,0:T(8,128)(2,1)S(1)}, u32[]{:S(2)}) copy-start(bf16[64,2048]{1,0:T(8,128)(2,1)S(1)} %collective-permute-done.1.r1) | copy-start | bytes 786436
  83.5 9.2 %copy-start.5 = (bf16[64,2048]{1,0:T(8,128)(2,1)}, bf16[64,2048]{1,0:T(8,128)(2,1)S(1)}, u32[]{:S(2)}) copy-start(bf16[64,2048]{1,0:T(8,128)(2,1)S(1)} %collective-permute-done.2.r2) | copy-start | bytes 786436
  92.7 0.7 copy-start.6
  96.1 15.9 %collective-permute-start.7 = (bf16[256,256]{1,0:T(8,128)(2,1)}, bf16[256,256]{1,0:T(8,128)(2,1)S(1)}, u32[]{:S(2)}, u32[]{:S(2)}) collective-permute-start(bf16[256,256]{1,0:T(8,128)(2,1)} %get-tuple-element.26), channel_id=1, source_target_pairs={{0,8},{8,0},{16,24},{24,16},{1,9},{9,1},{17,25},{25,17},{2,10},{10... | collective-permute-start | bytes 393224 | tf_op jit(solution)/shard_map/ppermute | solution.py:238
  98.6 13.4 %collective-permute-start.8 = (bf16[256,256]{1,0:T(8,128)(2,1)}, bf16[256,256]{1,0:T(8,128)(2,1)S(1)}, u32[]{:S(2)}, u32[]{:S(2)}) collective-permute-start(bf16[256,256]{1,0:T(8,128)(2,1)} %get-tuple-element.27), channel_id=1, source_target_pairs={{0,16},{8,24},{16,0},{24,8},{1,17},{9,25},{17,1},{25,9},{2,18},{10... | collective-permute-start | bytes 393224 | tf_op jit(solution)/shard_map/ppermute | solution.py:238
  104.4 8.3 %collective-permute-start.9 = (bf16[256,256]{1,0:T(8,128)(2,1)}, bf16[256,256]{1,0:T(8,128)(2,1)S(1)}, u32[]{:S(2)}, u32[]{:S(2)}) collective-permute-start(bf16[256,256]{1,0:T(8,128)(2,1)} %get-tuple-element.28), channel_id=1, source_target_pairs={{0,24},{8,16},{16,8},{24,0},{1,25},{9,17},{17,9},{25,1},{2,26},{10... | collective-permute-start | bytes 393224 | tf_op jit(solution)/shard_map/ppermute | solution.py:238
  109.5 0.8 copy-start.2
  112.0 0.7 copy-start.7
  112.0 0.7 copy-start.8
  112.7 0.7 copy-start.9

commit v4 on v3

v4 whole, which is shorter than its diff:
```python
import jax
import jax.numpy as jnp
from jax import lax
from jax.experimental import pallas as pl
from jax.experimental.pallas import tpu as pltpu
from jax.sharding import PartitionSpec as P


norm_epsilon = 1e-05
outer_rate = 0.7
outer_beta = 0.9
CORES = 2
SHARDS = 4
CHIPS = 4
F32 = jnp.float32
BF16 = jnp.bfloat16


def cost(flops, moved):
    return pl.CostEstimate(flops=flops, bytes_accessed=moved, transcendentals=0)


def whole(shape):
    return pl.BlockSpec(shape, lambda *_: (0,) * len(shape))


def block_of(idx, place, flip=0):
    return CORES * (idx[1] ^ (place % CHIPS)) + (idx[0] ^ flip ^ (place // CHIPS))


def spread_kernel(idx, x_ref, o_ref, both, sems):
    fan = o_ref.shape[0]
    copies = []
    for core in range(CORES):
        for place in range(2 * CHIPS):
            block = CORES * (idx[1] ^ (place % CHIPS)) + (core ^ (place // CHIPS))
            both[core, place * 16:(place + 1) * 16, :] = x_ref[pl.ds(pl.multiple_of(block * 16, 16), 16), :]
        for s in range(fan // CORES):
            at = CORES * s + core
            copies.append(pltpu.make_async_copy(both.at[core], o_ref.at[at], sems.at[at]))
            copies[-1].start()
    for copy in copies:
        copy.wait()


def pack_kernel(idx, x_ref, g_ref, o_ref, inv_ref, gain):
    @pl.when(pl.program_id(0) == 0)
    def _():
        gain[...] = g_ref[...].astype(F32)

    rows, width = x_ref.shape
    part = width // SHARDS
    total = jnp.zeros((rows, 512), F32)
    for q in range(width // 512):
        wide = x_ref[:, q * 512:(q + 1) * 512].astype(F32)
        total += wide * wide
    inv = lax.rsqrt(jnp.sum(total, axis=1, keepdims=True) / width + norm_epsilon)
    inv = jnp.broadcast_to(inv, inv_ref.shape)
    inv_ref[...] = inv
    for q in range(width // 128):
        wide = x_ref[:, q * 128:(q + 1) * 128].astype(F32)
        d, at = q * 128 // part, q * 128 % part
        o_ref[d, :, at:at + 128] = (wide * inv * gain[q:q + 1, :]).astype(BF16)


def merge_kernel(idx, h0, r1, r2, r3, values, keep, v0, m1, m2, m3):
    tokens, cols = v0.shape
    for k, out in enumerate((keep, m1, m2, m3)):
        at = pl.ds(pl.multiple_of((idx[2] ^ k) * 16, 16), 16)
        for q in range(h0.shape[1] // cols):
            lanes = slice(q * cols, (q + 1) * cols)
            total = h0[at, lanes].astype(F32) + r1[at, lanes].astype(F32)
            total += r2[at, lanes].astype(F32) + r3[at, lanes].astype(F32)
            if k == 0:
                out[:, lanes] = total
            else:
                out[q * 16:(q + 1) * 16, :] = total.astype(BF16)
    for k, out in enumerate((v0, m1, m2, m3)):
        val = values[pl.ds(pl.multiple_of((idx[2] ^ k) * tokens, tokens), tokens), :]
        if k == 0:
            out[...] = val
        else:
            out[tokens:, :] = val


def final_kernel(
    idx, keep, m1, m2, m3, v0, x_ref, inv_ref, g_ref, grads, p_ref, q_ref,
    o_ref, val_ref, new_p, new_m, gain,
):
    gain[...] = g_ref[...].astype(F32)
    part = keep.shape[1]
    tokens, cols = v0.shape
    width = x_ref.shape[1]
    lanes = 128
    inv = inv_ref[...]
    places = []
    for k, got in enumerate((keep, m1, m2, m3)):
        first = (idx[2] ^ k) * (part // lanes)
        for q in range(part // lanes):
            at = pl.ds(pl.multiple_of((first + q) * lanes, lanes), lanes)
            places.append((k, got, q, first + q, at))

    def scaled(k, got, q, row, at):
        if k == 0:
            term = got[:, q * lanes:(q + 1) * lanes]
        else:
            r, l = q * lanes // cols * 16, q * lanes % cols
            term = got[r:r + 16, l:l + lanes].astype(F32)
        return gain[pl.ds(row, 1), :] * term

    total = jnp.zeros((16, lanes), F32)
    for place in places:
        total += x_ref[:, place[4]].astype(F32) * scaled(*place)
    mean = jnp.sum(total, axis=1, keepdims=True) / width
    factor = inv * inv * inv * mean
    for place in places:
        at = place[4]
        o_ref[:, at] = (inv * scaled(*place) - x_ref[:, at].astype(F32) * factor).astype(BF16)
    for place in range(2 * CHIPS):
        rows = slice(place * 16, (place + 1) * 16)
        summed = v0[rows, :].astype(F32)
        for got in (m1, m2, m3):
            summed += got[tokens + place * 16:tokens + (place + 1) * 16, :].astype(F32)
        to = pl.ds(pl.multiple_of(block_of(idx, place) * 16, 16), 16)
        val_ref[to, :] = summed.astype(BF16)

    replicas = grads.shape[0]
    outer = grads[0].astype(F32)
    for r in range(1, replicas):
        outer += grads[r].astype(F32)
    average = outer / replicas
    momentum = outer_beta * q_ref[...] + average
    new_m[...] = momentum
    new_p[...] = p_ref[...] - outer_rate * (average + outer_beta * momentum)


def outer_pack_kernel(x_ref, o_ref):
    cols = o_ref.shape[2]
    for r in range(o_ref.shape[0]):
        o_ref[r] = x_ref[0, :, r * cols:(r + 1) * cols].astype(BF16)


def body(inputs, gain, value_weight, value_cot, pseudo_grad, global_params, momentum):
    tensors = lax.axis_size("tensor")
    replicas = lax.axis_size("replica")
    tokens, width = inputs.shape
    rows, cols = value_weight.shape
    tensor = lax.axis_index("tensor")
    shard = lax.axis_index("shard")
    idx = jnp.stack([tensor % CORES, tensor // CORES, shard, tensor]).astype(jnp.int32)
    swap = [(i, i ^ 1) for i in range(tensors)]
    chip_shift = lambda j: [
        (t, (t // CORES ^ j) * CORES + t % CORES) for t in range(tensors)
    ]
    shard_shift = lambda k: [(s, s ^ k) for s in range(SHARDS)]
    near = [
        [s * tensors + h * CORES + c for s in range(SHARDS) for c in range(CORES)]
        for h in range(CHIPS)
    ]
    fan = SHARDS * CORES
    spec = jax.ShapeDtypeStruct
    rest = (1, 3, 2)

    spread = pl.pallas_call(
        spread_kernel,
        grid_spec=pltpu.PrefetchScalarGridSpec(
            num_scalar_prefetch=1, grid=(1,),
            in_specs=[whole((tokens, cols))],
            out_specs=pl.BlockSpec(memory_space=pl.ANY),
            scratch_shapes=[pltpu.VMEM((CORES, tokens, cols), BF16), pltpu.SemaphoreType.DMA((fan,))],
        ),
        out_shape=spec((fan, tokens, cols), BF16),
        cost_estimate=cost(0, 600_000), name="spread",
    )(idx, value_cot)
    cots = lax.all_to_all(
        spread, ("shard", "tensor"), 0, 0, axis_index_groups=near, tiled=True
    )
    other_weight = lax.ppermute(value_weight, "tensor", swap)

    gains = gain.reshape(width // 128, 128)
    part = width // SHARDS
    packing = pl.pallas_call(
        pack_kernel,
        grid_spec=pltpu.PrefetchScalarGridSpec(
            num_scalar_prefetch=1, grid=(tokens // 16,),
            in_specs=[pl.BlockSpec((16, width), lambda i, _: (i, 0)), whole(gains.shape)],
            out_specs=[
                pl.BlockSpec(
                    (SHARDS, 16, part),
                    lambda i, at: (0, ((i // CORES) ^ at[1]) + CHIPS * ((i % CORES) ^ at[0]), 0),
                ),
                pl.BlockSpec((16, 128), lambda i, _: (i, 0)),
            ],
            scratch_shapes=[pltpu.VMEM(gains.shape, F32)],
        ),
        out_shape=[spec((SHARDS, tokens, part), BF16), spec((tokens, 128), F32)],
        cost_estimate=cost(6_000_000, 4_300_000), name="pack",
    )
    sent, inv_scale = packing(idx, inputs, gains)
    normed = lax.all_to_all(sent, "shard", 0, 0, tiled=True).reshape(SHARDS * tokens, part)

    pairs = cots.reshape(SHARDS, CORES, tokens, cols)
    own_cots = lax.dynamic_index_in_dim(pairs, tensor % CORES, 1, keepdims=False)
    other_cots = lax.dynamic_index_in_dim(pairs, 1 - tensor % CORES, 1, keepdims=False)
    share = tokens // CORES
    own_rows = own_cots[:, :share].reshape(SHARDS * share, cols)
    other_rows = other_cots[:, :share].reshape(SHARDS * share, cols)
    last_dims = (((1,), (1,)), ((), ()))
    product = lax.dot_general(own_rows, value_weight, last_dims, preferred_element_type=F32)
    product += lax.dot_general(other_rows, other_weight, last_dims, preferred_element_type=F32)
    product = product.astype(BF16).reshape(SHARDS, CHIPS, 16, rows)
    outs = [product[:, j].reshape(SHARDS * 16, rows) for j in range(CHIPS)]
    hidden = [outs[0], None, None, None]
    for j in rest:
        hidden[j] = lax.ppermute(outs[j], "tensor", chip_shift(j))

    frows, fcols = pseudo_grad.shape[1:]
    own_cols = fcols // replicas
    outer_packing = pl.pallas_call(
        outer_pack_kernel, grid=(3,),
        in_specs=[pl.BlockSpec((1, frows, fcols // 3), lambda i: (0, 0, i))],
        out_specs=pl.BlockSpec((replicas // 3, frows, own_cols), lambda i: (i, 0, 0)),
        out_shape=spec((replicas, frows, own_cols), BF16),
        cost_estimate=cost(0, 1_200_000), name="outerpack",
    )
    packed = outer_packing(pseudo_grad)
    grads = lax.all_to_all(packed, "replica", 0, 0, tiled=True)

    partial_values = jnp.dot(normed, value_weight, preferred_element_type=F32).astype(BF16)
    weight_grad = lax.dot_general(
        normed, own_cots.reshape(SHARDS * tokens, cols),
        (((0,), (0,)), ((), ())), preferred_element_type=F32,
    ).astype(BF16)[None]

    keep, own_values, *merged = pl.pallas_call(
        merge_kernel,
        grid_spec=pltpu.PrefetchScalarGridSpec(
            num_scalar_prefetch=1, grid=(1,),
            in_specs=[whole((64, rows))] * CHIPS + [whole((SHARDS * tokens, cols))],
            out_specs=[whole((16, rows)), whole((tokens, cols))] + [whole((2 * tokens, cols))] * 3,
        ),
        out_shape=[spec((16, rows), F32), spec((tokens, cols), BF16)]
        + [spec((2 * tokens, cols), BF16)] * 3,
        cost_estimate=cost(1_000_000, 1_700_000), name="merge",
    )(idx, *hidden, partial_values)
    got = [None] * SHARDS
    for k in rest:
        got[k] = lax.ppermute(merged[k - 1], "shard", shard_shift(k))

    input_grad, values, new_global, new_momentum = pl.pallas_call(
        final_kernel,
        grid_spec=pltpu.PrefetchScalarGridSpec(
            num_scalar_prefetch=1, grid=(1,),
            in_specs=[whole((16, rows))] + [whole((2 * tokens, cols))] * 3
            + [
                whole((tokens, cols)),
                pl.BlockSpec((16, width), lambda i, at: (at[3], 0)),
                pl.BlockSpec((16, 128), lambda i, at: (at[3], 0)),
                whole(gains.shape),
                whole(grads.shape),
                whole(momentum.shape),
                whole(momentum.shape),
            ],
            out_specs=[
                whole((16, width)), whole((tokens, cols)),
                whole(momentum.shape), whole(momentum.shape),
            ],
            scratch_shapes=[pltpu.VMEM(gains.shape, F32)],
        ),
        out_shape=[spec((16, width), BF16), spec((tokens, cols), BF16)]
        + [spec(momentum.shape, F32)] * 2,
        cost_estimate=cost(2_000_000, 2_100_000), name="final",
    )(idx, keep, *got[1:], own_values, inputs, inv_scale, gains, grads, global_params, momentum)
    return (values, weight_grad, input_grad, new_global, new_momentum)


def solution(mesh):
    placed = (
        P(("replica", "shard"), None),
        P(),
        P("shard", "tensor"),
        P(("replica", "shard"), "tensor"),
        P("replica", ("shard", "tensor"), None),
        P(("shard", "tensor"), "replica"),
        P(("shard", "tensor"), "replica"),
    )
    return jax.shard_map(
        body,
        mesh=mesh,
        in_specs=placed,
        out_specs=(
            P(("replica", "shard"), "tensor"),
            P("replica", "shard", "tensor"),
            P(("replica", "shard", "tensor"), None),
            P(("shard", "tensor"), "replica"),
            P(("shard", "tensor"), "replica"),
        ),
        check_vma=False,
    )
```

time: 117 us -> 126 us (1.077)
  waiting for transfers between devices: 20.1 us -> 44.3 us
  starting transfers between devices: 56.1 us -> 49.8 us
  matrix products: 11.7 us -> 8.63 us
  Pallas kernels: 20.9 us -> 17.9 us
  local copies, waits for them, and re-layouts: 4.56 us -> 2.9 us
  other arithmetic: 1.98 us -> 0.56 us
    all_to_all x0 -> x1, waiting for transfers between devices: none -> 20.5 us  [body(): lax.all_to_all(sent, 'shard', 0, 0, tiled=True)]
    ppermute x3 -> x0, starting transfers between devices: 10.4 us -> none  [body(): normed[k] = lax.ppermute(sent[k], 'shard', shard_shift(k))]
    all_to_all x0 -> x1, starting transfers between devices: none -> 4.59 us  [body(): lax.all_to_all(sent, 'shard', 0, 0, tiled=True)]
    dot_general x5 -> x2, matrix products: 9.86 us -> 6.39 us  [the longest x1 3.32 us: body(): lax.dot_general(normed, own_cots.reshape(SHARDS * tokens, cols), (((0,),...]
    all_to_all x1, waiting for transfers between devices: 0.01 us -> 3.39 us  [body(): lax.all_to_all(spread, ('shard', 'tensor'), 0, 0, axis_index_groups=near,...]
    pallas_call x4 -> x2, Pallas kernels: 12.6 us -> 9.28 us  [the longest x1 6.93 us: body(): sent, inv_scale = packing(idx, inputs, gains)]
    squeeze x1, local copies, waits for them, and re-layouts: 1.65 us -> 0.03 us  [body(): lax.dynamic_index_in_dim(pairs, 1 - tensor % CORES, 1, keepdims=False)]
    reshape x1 -> x0, other arithmetic: 1.32 us -> none  [body(): gain_row = gain.astype(F32).reshape(1, width)]
  transfers between devices with their start and end apart: 12 -> 10, of which waited for: 3 -> 6; matrix products, arithmetic and copies ran while one was open for 14% -> 8% of each run, Pallas kernels for 14% -> 10%
where the time goes in v4:
time: 126 us; the launch traced here: 125 us
  starting transfers between devices  49.8 us (40%)
  waiting for transfers between devices  44.3 us (35%)
  Pallas kernels  17.9 us (14%)
  matrix products  8.63 us (7%)
  local copies, waits for them, and re-layouts  2.9 us (2%)
    all_to_all x1, waiting for transfers between devices, body(): lax.all_to_all(sent, 'shard', 0, 0, tiled=True)  20.5 us
    ppermute x3, waiting for transfers between devices, body(): hidden[j] = lax.ppermute(outs[j], 'tensor', chip_shift(j))  19.5 us
    all_to_all x1, starting transfers between devices, body(): grads = lax.all_to_all(packed, 'replica', 0, 0, tiled=True)  16.4 us
    ppermute x3, starting transfers between devices, body(): hidden[j] = lax.ppermute(outs[j], 'tensor', chip_shift(j))  12.2 us
    ppermute x3, starting transfers between devices, body(): got[k] = lax.ppermute(merged[k - 1], 'shard', shard_shift(k))  10.4 us
    pallas_call x1, Pallas kernels, body(): sent, inv_scale = packing(idx, inputs, gains)  6.93 us
    all_to_all x1, starting transfers between devices, body(): lax.all_to_all(sent, 'shard', 0, 0, tiled=True)  4.59 us
    all_to_all x1, starting transfers between devices, body(): lax.all_to_all(spread, ('shard', 'tensor'), 0, 0, axis_index_groups=near,...  4.31 us
  transfers between devices with their start and end apart: 10, of which 6 were waited for; matrix products, arithmetic and copies ran while one was open for 8% of the time, Pallas kernels for 10%

profile of v4, /device:TPU:16, one launch (start us, length us, event | category | flops | bytes accessed | tf_op | source)
XLA Modules:
  0.0 124.9 jit_solution(5288804961131808593)
XLA Ops:
  0.6 0.6 pad_add_fusion.idx
  1.2 2.4 %spread.1 = bf16[8,128,256]{2,1,0:T(8,128)(2,1)} custom-call(s32[4]{0:T(128)} %pad_add_fusion.idx, bf16[128,256]{1,0:T(8,128)(2,1)} %x_ref.4), custom_call_target="tpu_custom_call" | custom-call | bytes 600000 | tf_op jit(solution)/shard_map/spread/pallas_call | solution.py:164
  3.6 4.3 %all-to-all-start = ((bf16[8,128,256]{2,1,0:T(8,128)(2,1)}), bf16[8,128,256]{2,1,0:T(8,128)(2,1)S(1)}, u32[]{:S(2)}, u32[]{:S(2)}) async-start(bf16[8,128,256]{2,1,0:T(8,128)(2,1)} %spread.1), calls=%async_computation | async-start | bytes 1048576 | tf_op jit(solution)/shard_map/all_to_all | solution.py:175
  7.9 6.9 %pack.1 = (bf16[4,128,2048]{2,1,0:T(8,128)(2,1)}, f32[128,128]{1,0:T(8,128)}) custom-call(s32[4]{0:T(128)} %pad_add_fusion.idx, bf16[128,8192]{1,0:T(8,128)(2,1)} %x_ref.7, bf16[64,128]{1,0:T(8,128)(2,1)} %bitcast.46), custom_call_target="tpu_custom_call" | custom-call | flops 6000000 | bytes 4300000 | tf_op jit(solution)/shard_map/pack/pallas_call | solution.py:199
  14.8 3.4 %all-to-all-done = bf16[8,128,256]{2,1,0:T(8,128)(2,1)S(1)} async-done(((bf16[8,128,256]{2,1,0:T(8,128)(2,1)}), bf16[8,128,256]{2,1,0:T(8,128)(2,1)S(1)}, u32[]{:S(2)}, u32[]{:S(2)}) %all-to-all-start) | async-done | bytes 524320 | tf_op jit(solution)/shard_map/all_to_all | solution.py:175
  18.2 0.0 copy-start.1
  18.2 4.6 %all-to-all-start.1 = ((bf16[4,128,2048]{2,1,0:T(8,128)(2,1)}), bf16[4,128,2048]{2,1,0:T(8,128)(2,1)}, u32[]{:S(2)}, u32[]{:S(2)}) async-start(bf16[4,128,2048]{2,1,0:T(8,128)(2,1)} %get-tuple-element.16), calls=%async_computation.1 | async-start | bytes 4194304 | tf_op jit(solution)/shard_map/all_to_all | solution.py:200
  22.8 0.0 copy-done.1
  22.8 1.9 %collective-permute-start = (bf16[2048,256]{1,0:T(8,128)(2,1)S(1)}, bf16[2048,256]{1,0:T(8,128)(2,1)}, u32[]{:S(2)}, u32[]{:S(2)}) collective-permute-start(bf16[2048,256]{1,0:T(8,128)(2,1)S(1)} %copy-done.1), channel_id=1, source_target_pairs={{0,1},{1,0},{2,3},{3,2},{4,5},{5,4},{6,7},{7,6},{8,9},{9,8},{10,11... | collective-permute-start | bytes 3145736 | tf_op jit(solution)/shard_map/ppermute | solution.py:178
  24.8 2.7 %outerpack.1 = bf16[24,64,128]{2,1,0:T(8,128)(2,1)} custom-call(f32[1,64,3072]{2,1,0:T(8,128)} %x_ref.6), custom_call_target="tpu_custom_call" | custom-call | bytes 1200000 | tf_op jit(solution)/shard_map/outerpack/pallas_call | solution.py:226
  27.5 0.0 copy-start.2
  27.5 0.7 slice.25
  28.3 0.0 copy-done.2
  28.3 0.5 fusion.3
  28.7 20.5 %all-to-all-done.1 = bf16[4,128,2048]{2,1,0:T(8,128)(2,1)} async-done(((bf16[4,128,2048]{2,1,0:T(8,128)(2,1)}), bf16[4,128,2048]{2,1,0:T(8,128)(2,1)}, u32[]{:S(2)}, u32[]{:S(2)}) %all-to-all-start.1) | async-done | bytes 2097184 | tf_op jit(solution)/shard_map/all_to_all | solution.py:200
  49.2 16.4 %all-to-all-start.2 = ((bf16[24,64,128]{2,1,0:T(8,128)(2,1)}), bf16[24,64,128]{2,1,0:T(8,128)(2,1)S(1)}, u32[]{:S(2)}, u32[]{:S(2)}) async-start(bf16[24,64,128]{2,1,0:T(8,128)(2,1)} %outerpack.1), calls=%async_computation.2 | async-start | bytes 786432 | tf_op jit(solution)/shard_map/all_to_all | solution.py:227
  65.6 0.0 collective-permute-done
  65.6 1.8 %fusion = bf16[256,2048]{1,0:T(8,128)(2,1)S(1)} fusion(f32[256,2048]{1,0:T(8,128)S(1)} %fusion.3, bf16[256,256]{1,0:T(8,128)(2,1)} %bitcast.41, bf16[2048,256]{1,0:T(8,128)(2,1)} %collective-permute-done), kind=kOutput, calls=%fused_computation.2 | convolution fusion | flops 269484032 | bytes 4325376 | tf_op jit(solution)/shard_map/dot_general | solution.py:210
  67.4 0.8 fusion.2
  68.1 2.2 %collective-permute-start.1 = (bf16[64,2048]{1,0:T(8,128)(2,1)S(1)}, bf16[64,2048]{1,0:T(8,128)(2,1)S(1)}, u32[]{:S(2)}, u32[]{:S(2)}) collective-permute-start(bf16[64,2048]{1,0:T(8,128)(2,1)S(1)} %bitcast.45), channel_id=1, source_target_pairs={{0,2},{1,3},{2,0},{3,1},{4,6},{5,7},{6,4},{7,5},{8,10},{9,11},{10,... | collective-permute-start | bytes 786440 | tf_op jit(solution)/shard_map/ppermute | solution.py:215
  70.4 6.8 %collective-permute-start.2 = (bf16[64,2048]{1,0:T(8,128)(2,1)S(1)}, bf16[64,2048]{1,0:T(8,128)(2,1)S(1)}, u32[]{:S(2)}, u32[]{:S(2)}) collective-permute-start(bf16[64,2048]{1,0:T(8,128)(2,1)S(1)} %bitcast.44), channel_id=1, source_target_pairs={{0,4},{1,5},{2,6},{3,7},{4,0},{5,1},{6,2},{7,3},{8,12},{9,13},{10,... | collective-permute-start | bytes 786440 | tf_op jit(solution)/shard_map/ppermute | solution.py:215
  77.2 3.1 %collective-permute-start.3 = (bf16[64,2048]{1,0:T(8,128)(2,1)S(1)}, bf16[64,2048]{1,0:T(8,128)(2,1)S(1)}, u32[]{:S(2)}, u32[]{:S(2)}) collective-permute-start(bf16[64,2048]{1,0:T(8,128)(2,1)S(1)} %bitcast.43), channel_id=1, source_target_pairs={{0,6},{1,7},{2,4},{3,5},{4,2},{5,3},{6,0},{7,1},{8,14},{9,15},{10,... | collective-permute-start | bytes 786440 | tf_op jit(solution)/shard_map/ppermute | solution.py:215
  80.4 0.0 copy-start.3
  80.4 3.1 %convolution_convert_fusion.1.values = bf16[512,256]{1,0:T(8,128)(2,1)} fusion(bf16[512,2048]{1,0:T(8,128)(2,1)} %bitcast.15, bf16[2048,256]{1,0:T(8,128)(2,1)S(1)} %copy-done.1), kind=kOutput, calls=%fused_computation.4 | convolution fusion | flops 537001984 | bytes 3407872 | tf_op jit(solution)/shard_map/dot_general | solution.py:229
  83.4 6.5 %collective-permute-done.1.r1 = bf16[64,2048]{1,0:T(8,128)(2,1)S(1)} collective-permute-done((bf16[64,2048]{1,0:T(8,128)(2,1)S(1)}, bf16[64,2048]{1,0:T(8,128)(2,1)S(1)}, u32[]{:S(2)}, u32[]{:S(2)}) %collective-permute-start.1) | collective-permute-done | bytes 262176 | tf_op jit(solution)/shard_map/ppermute | solution.py:215
  90.0 0.0 copy-start.4
  90.0 3.3 %collective-permute-done.2.r2 = bf16[64,2048]{1,0:T(8,128)(2,1)S(1)} collective-permute-done((bf16[64,2048]{1,0:T(8,128)(2,1)S(1)}, bf16[64,2048]{1,0:T(8,128)(2,1)S(1)}, u32[]{:S(2)}, u32[]{:S(2)}) %collective-permute-start.2) | collective-permute-done | bytes 262176 | tf_op jit(solution)/shard_map/ppermute | solution.py:215
  93.3 9.7 %collective-permute-done.3.r3 = bf16[64,2048]{1,0:T(8,128)(2,1)S(1)} collective-permute-done((bf16[64,2048]{1,0:T(8,128)(2,1)S(1)}, bf16[64,2048]{1,0:T(8,128)(2,1)S(1)}, u32[]{:S(2)}, u32[]{:S(2)}) %collective-permute-start.3) | collective-permute-done | bytes 262176 | tf_op jit(solution)/shard_map/ppermute | solution.py:215
  103.0 0.0 copy-done.4
  103.0 0.0 copy-done.5
  103.0 0.7 copy-done.6
  103.7 2.8 %merge.1 = (f32[16,2048]{1,0:T(8,128)}, bf16[128,256]{1,0:T(8,128)(2,1)}, bf16[256,256]{1,0:T(8,128)(2,1)}, bf16[256,256]{1,0:T(8,128)(2,1)}, bf16[256,256]{1,0:T(8,128)(2,1)}) custom-call(s32[4]{0:T(128)} %pad_add_fusion.idx, bf16[64,2048]{1,0:T(8,128)(2,1)} %bitcast.38, bf16[64,2048]{1,0:T(8,128)(2,1)} %copy-done.4, bf16[64,2048]{1,0:T(8,128)(2,1)} %copy-done.5, ...), custom_call_target="tpu_custom_call" | custom-call | flops 1000000 | bytes 1700000 | tf_op jit(solution)/shard_map/merge/pallas_call | solution.py:235
  106.5 2.5 %collective-permute-start.4 = (bf16[256,256]{1,0:T(8,128)(2,1)}, bf16[256,256]{1,0:T(8,128)(2,1)S(1)}, u32[]{:S(2)}, u32[]{:S(2)}) collective-permute-start(bf16[256,256]{1,0:T(8,128)(2,1)} %get-tuple-element.18), channel_id=1, source_target_pairs={{0,8},{8,0},{16,24},{24,16},{1,9},{9,1},{17,25},{25,17},{2,10},{10... | collective-permute-start | bytes 393224 | tf_op jit(solution)/shard_map/ppermute | solution.py:248
  109.0 4.0 %collective-permute-start.5 = (bf16[256,256]{1,0:T(8,128)(2,1)}, bf16[256,256]{1,0:T(8,128)(2,1)S(1)}, u32[]{:S(2)}, u32[]{:S(2)}) collective-permute-start(bf16[256,256]{1,0:T(8,128)(2,1)} %get-tuple-element.19), channel_id=1, source_target_pairs={{0,16},{8,24},{16,0},{24,8},{1,17},{9,25},{17,1},{25,9},{2,18},{10... | collective-permute-start | bytes 393224 | tf_op jit(solution)/shard_map/ppermute | solution.py:248
  113.0 4.0 %collective-permute-start.6 = (bf16[256,256]{1,0:T(8,128)(2,1)}, bf16[256,256]{1,0:T(8,128)(2,1)S(1)}, u32[]{:S(2)}, u32[]{:S(2)}) collective-permute-start(bf16[256,256]{1,0:T(8,128)(2,1)} %get-tuple-element.20), channel_id=1, source_target_pairs={{0,24},{8,16},{16,8},{24,0},{1,25},{9,17},{17,9},{25,1},{2,26},{10... | collective-permute-start | bytes 393224 | tf_op jit(solution)/shard_map/ppermute | solution.py:248
  116.9 0.0 copy-done.3
  117.0 3.3 %fusion.1 = bf16[1,2048,256]{2,1,0:T(8,128)(2,1)} fusion(bf16[512,2048]{1,0:T(8,128)(2,1)} %bitcast.15, bf16[512,256]{1,0:T(8,128)(2,1)S(1)} %bitcast.40), kind=kOutput, calls=%fused_computation.3 | convolution fusion | flops 537395200 | bytes 3407872 | tf_op jit(solution)/shard_map/dot_general | solution.py:230
  120.3 0.0 all-to-all-done.2.grads
  120.3 0.0 collective-permute-done.4.m1
  120.3 0.0 copy-start.7
  120.3 0.0 collective-permute-done.5.m2
  120.3 0.0 copy-start.8
  120.3 0.9 collective-permute-done.6.m3
  121.2 0.0 copy-done
  121.3 0.0 copy-done.7
  121.3 0.0 copy-done.8
  121.3 0.6 copy-done.9
  121.9 3.1 %final.1 = (bf16[16,8192]{1,0:T(8,128)(2,1)}, bf16[128,256]{1,0:T(8,128)(2,1)}, f32[64,128]{1,0:T(8,128)}, f32[64,128]{1,0:T(8,128)}) custom-call(s32[4]{0:T(128)} %pad_add_fusion.idx, f32[16,2048]{1,0:T(8,128)} %get-tuple-element.17.keep, bf16[256,256]{1,0:T(8,128)(2,1)} %copy-done.7, bf16[256,256]{1,0:T(8,128)(2,1)} %copy-done.8, ...), custom_call_target="tpu_custom_call" | custom-call | flops 2000000 | bytes 2100000 | tf_op jit(solution)/shard_map/final/pallas_call | solution.py:250
  (6 shorter events, 0.1 us)
Async XLA Ops:
  3.6 14.6 %all-to-all-start = ((bf16[8,128,256]{2,1,0:T(8,128)(2,1)}), bf16[8,128,256]{2,1,0:T(8,128)(2,1)S(1)}, u32[]{:S(2)}, u32[]{:S(2)}) async-start(bf16[8,128,256]{2,1,0:T(8,128)(2,1)} %spread.1), calls=%async_computation | async-start | bytes 1048576 | tf_op jit(solution)/shard_map/all_to_all | solution.py:175
  18.2 4.6 %copy-start.1 = (bf16[2048,256]{1,0:T(8,128)(2,1)S(1)}, bf16[2048,256]{1,0:T(8,128)(2,1)}, u32[]{:S(2)}) copy-start(bf16[2048,256]{1,0:T(8,128)(2,1)} %param.9) | copy-start | bytes 3145732
  18.2 31.0 %all-to-all-start.1 = ((bf16[4,128,2048]{2,1,0:T(8,128)(2,1)}), bf16[4,128,2048]{2,1,0:T(8,128)(2,1)}, u32[]{:S(2)}, u32[]{:S(2)}) async-start(bf16[4,128,2048]{2,1,0:T(8,128)(2,1)} %get-tuple-element.16), calls=%async_computation.1 | async-start | bytes 4194304 | tf_op jit(solution)/shard_map/all_to_all | solution.py:200
  22.8 42.8 %collective-permute-start = (bf16[2048,256]{1,0:T(8,128)(2,1)S(1)}, bf16[2048,256]{1,0:T(8,128)(2,1)}, u32[]{:S(2)}, u32[]{:S(2)}) collective-permute-start(bf16[2048,256]{1,0:T(8,128)(2,1)S(1)} %copy-done.1), channel_id=1, source_target_pairs={{0,1},{1,0},{2,3},{3,2},{4,5},{5,4},{6,7},{7,6},{8,9},{9,8},{10,11... | collective-permute-start | bytes 3145736 | tf_op jit(solution)/shard_map/ppermute | solution.py:178
  27.5 0.7 copy-start.2
  49.2 71.1 %all-to-all-start.2 = ((bf16[24,64,128]{2,1,0:T(8,128)(2,1)}), bf16[24,64,128]{2,1,0:T(8,128)(2,1)S(1)}, u32[]{:S(2)}, u32[]{:S(2)}) async-start(bf16[24,64,128]{2,1,0:T(8,128)(2,1)} %outerpack.1), calls=%async_computation.2 | async-start | bytes 786432 | tf_op jit(solution)/shard_map/all_to_all | solution.py:227
  68.1 21.9 %collective-permute-start.1 = (bf16[64,2048]{1,0:T(8,128)(2,1)S(1)}, bf16[64,2048]{1,0:T(8,128)(2,1)S(1)}, u32[]{:S(2)}, u32[]{:S(2)}) collective-permute-start(bf16[64,2048]{1,0:T(8,128)(2,1)S(1)} %bitcast.45), channel_id=1, source_target_pairs={{0,2},{1,3},{2,0},{3,1},{4,6},{5,7},{6,4},{7,5},{8,10},{9,11},{10,... | collective-permute-start | bytes 786440 | tf_op jit(solution)/shard_map/ppermute | solution.py:215
  70.4 22.9 %collective-permute-start.2 = (bf16[64,2048]{1,0:T(8,128)(2,1)S(1)}, bf16[64,2048]{1,0:T(8,128)(2,1)S(1)}, u32[]{:S(2)}, u32[]{:S(2)}) collective-permute-start(bf16[64,2048]{1,0:T(8,128)(2,1)S(1)} %bitcast.44), channel_id=1, source_target_pairs={{0,4},{1,5},{2,6},{3,7},{4,0},{5,1},{6,2},{7,3},{8,12},{9,13},{10,... | collective-permute-start | bytes 786440 | tf_op jit(solution)/shard_map/ppermute | solution.py:215
  77.2 25.8 %collective-permute-start.3 = (bf16[64,2048]{1,0:T(8,128)(2,1)S(1)}, bf16[64,2048]{1,0:T(8,128)(2,1)S(1)}, u32[]{:S(2)}, u32[]{:S(2)}) collective-permute-start(bf16[64,2048]{1,0:T(8,128)(2,1)S(1)} %bitcast.43), channel_id=1, source_target_pairs={{0,6},{1,7},{2,4},{3,5},{4,2},{5,3},{6,0},{7,1},{8,14},{9,15},{10,... | collective-permute-start | bytes 786440 | tf_op jit(solution)/shard_map/ppermute | solution.py:215
  80.4 36.6 %copy-start.3 = (bf16[4,1,128,256]{3,2,1,0:T(8,128)(2,1)S(1)}, bf16[4,1,128,256]{3,2,1,0:T(8,128)(2,1)}, u32[]{:S(2)}) copy-start(bf16[4,1,128,256]{3,2,1,0:T(8,128)(2,1)} %copy-done.2) | copy-start | bytes 786436
  90.0 13.0 %copy-start.4 = (bf16[64,2048]{1,0:T(8,128)(2,1)}, bf16[64,2048]{1,0:T(8,128)(2,1)S(1)}, u32[]{:S(2)}) copy-start(bf16[64,2048]{1,0:T(8,128)(2,1)S(1)} %collective-permute-done.1.r1) | copy-start | bytes 786436
  93.3 9.7 %copy-start.5 = (bf16[64,2048]{1,0:T(8,128)(2,1)}, bf16[64,2048]{1,0:T(8,128)(2,1)S(1)}, u32[]{:S(2)}) copy-start(bf16[64,2048]{1,0:T(8,128)(2,1)S(1)} %collective-permute-done.2.r2) | copy-start | bytes 786436
  103.0 0.7 copy-start.6
  106.5 13.8 %collective-permute-start.4 = (bf16[256,256]{1,0:T(8,128)(2,1)}, bf16[256,256]{1,0:T(8,128)(2,1)S(1)}, u32[]{:S(2)}, u32[]{:S(2)}) collective-permute-start(bf16[256,256]{1,0:T(8,128)(2,1)} %get-tuple-element.18), channel_id=1, source_target_pairs={{0,8},{8,0},{16,24},{24,16},{1,9},{9,1},{17,25},{25,17},{2,10},{10... | collective-permute-start | bytes 393224 | tf_op jit(solution)/shard_map/ppermute | solution.py:248
  109.0 11.3 %collective-permute-start.5 = (bf16[256,256]{1,0:T(8,128)(2,1)}, bf16[256,256]{1,0:T(8,128)(2,1)S(1)}, u32[]{:S(2)}, u32[]{:S(2)}) collective-permute-start(bf16[256,256]{1,0:T(8,128)(2,1)} %get-tuple-element.19), channel_id=1, source_target_pairs={{0,16},{8,24},{16,0},{24,8},{1,17},{9,25},{17,1},{25,9},{2,18},{10... | collective-permute-start | bytes 393224 | tf_op jit(solution)/shard_map/ppermute | solution.py:248
  113.0 8.3 %collective-permute-start.6 = (bf16[256,256]{1,0:T(8,128)(2,1)}, bf16[256,256]{1,0:T(8,128)(2,1)S(1)}, u32[]{:S(2)}, u32[]{:S(2)}) collective-permute-start(bf16[256,256]{1,0:T(8,128)(2,1)} %get-tuple-element.20), channel_id=1, source_target_pairs={{0,24},{8,16},{16,8},{24,0},{1,25},{9,17},{17,9},{25,1},{2,26},{10... | collective-permute-start | bytes 393224 | tf_op jit(solution)/shard_map/ppermute | solution.py:248
  120.3 1.0 copy-start
  120.3 1.0 copy-start.7
  120.3 0.9 copy-start.8
  121.2 0.6 copy-start.9

commit v5 on v4

--- a/solution.py
+++ b/solution.py
@@ -24,43 +24,47 @@
     return pl.BlockSpec(shape, lambda *_: (0,) * len(shape))
 
 
-def block_of(idx, place, flip=0):
-    return CORES * (idx[1] ^ (place % CHIPS)) + (idx[0] ^ flip ^ (place // CHIPS))
-
-
-def spread_kernel(idx, x_ref, o_ref, both, sems):
-    fan = o_ref.shape[0]
-    copies = []
-    for core in range(CORES):
-        for place in range(2 * CHIPS):
-            block = CORES * (idx[1] ^ (place % CHIPS)) + (core ^ (place // CHIPS))
-            both[core, place * 16:(place + 1) * 16, :] = x_ref[pl.ds(pl.multiple_of(block * 16, 16), 16), :]
-        for s in range(fan // CORES):
-            at = CORES * s + core
-            copies.append(pltpu.make_async_copy(both.at[core], o_ref.at[at], sems.at[at]))
-            copies[-1].start()
+def block_of(idx, place):
+    return CORES * (idx[1] ^ (place % CHIPS)) + place // CHIPS
+
+
+def spread_kernel(idx, x_ref, o_ref, ordered, sems):
+    for place in range(2 * CHIPS):
+        at = pl.multiple_of(block_of(idx, place) * 16, 16)
+        ordered[place * 16:(place + 1) * 16, :] = x_ref[pl.ds(at, 16), :]
+    copies = [
+        pltpu.make_async_copy(ordered, o_ref.at[i], sems.at[i]) for i in range(o_ref.shape[0])
+    ]
+    for copy in copies:
+        copy.start()
     for copy in copies:
         copy.wait()
 
 
-def pack_kernel(idx, x_ref, g_ref, o_ref, inv_ref, gain):
-    @pl.when(pl.program_id(0) == 0)
-    def _():
-        gain[...] = g_ref[...].astype(F32)
-
+def inverse_scale(x_ref):
     rows, width = x_ref.shape
-    part = width // SHARDS
     total = jnp.zeros((rows, 512), F32)
     for q in range(width // 512):
         wide = x_ref[:, q * 512:(q + 1) * 512].astype(F32)
         total += wide * wide
     inv = lax.rsqrt(jnp.sum(total, axis=1, keepdims=True) / width + norm_epsilon)
-    inv = jnp.broadcast_to(inv, inv_ref.shape)
-    inv_ref[...] = inv
-    for q in range(width // 128):
-        wide = x_ref[:, q * 128:(q + 1) * 128].astype(F32)
-        d, at = q * 128 // part, q * 128 % part
-        o_ref[d, :, at:at + 128] = (wide * inv * gain[q:q + 1, :]).astype(BF16)
+    return jnp.broadcast_to(inv, (rows, 128))
+
+
+def pack_kernel(idx, x_ref, g_ref, o_ref, gain):
+    @pl.when(pl.program_id(0) == 0)
+    def _():
+        gain[...] = g_ref[...].astype(F32)
+
+    width = x_ref.shape[1]
+    part = width // SHARDS
+    inv = inverse_scale(x_ref)
+    half = part // CORES
+    for d in range(SHARDS):
+        for q in range(half // 128):
+            row = (d * CORES + idx[0]) * (half // 128) + q
+            wide = x_ref[:, pl.ds(pl.multiple_of(row * 128, 128), 128)].astype(F32)
+            o_ref[d, :, q * 128:(q + 1) * 128] = (wide * inv * gain[pl.ds(row, 1), :]).astype(BF16)
 
 
 def merge_kernel(idx, h0, r1, r2, r3, values, keep, v0, m1, m2, m3):
@@ -84,7 +88,7 @@
 
 
 def final_kernel(
-    idx, keep, m1, m2, m3, v0, x_ref, inv_ref, g_ref, grads, p_ref, q_ref,
+    idx, keep, m1, m2, m3, v0, x_ref, g_ref, grads, p_ref, q_ref,
     o_ref, val_ref, new_p, new_m, gain,
 ):
     gain[...] = g_ref[...].astype(F32)
@@ -92,7 +96,7 @@
     tokens, cols = v0.shape
     width = x_ref.shape[1]
     lanes = 128
-    inv = inv_ref[...]
+    inv = inverse_scale(x_ref)
     places = []
     for k, got in enumerate((keep, m1, m2, m3)):
         first = (idx[2] ^ k) * (part // lanes)
@@ -160,6 +164,7 @@
     fan = SHARDS * CORES
     spec = jax.ShapeDtypeStruct
     rest = (1, 3, 2)
+    small = pltpu.CompilerParams(vmem_limit_bytes=8 * 1024 * 1024)
 
     spread = pl.pallas_call(
         spread_kernel,
@@ -167,10 +172,10 @@
             num_scalar_prefetch=1, grid=(1,),
             in_specs=[whole((tokens, cols))],
             out_specs=pl.BlockSpec(memory_space=pl.ANY),
-            scratch_shapes=[pltpu.VMEM((CORES, tokens, cols), BF16), pltpu.SemaphoreType.DMA((fan,))],
+            scratch_shapes=[pltpu.VMEM((tokens, cols), BF16), pltpu.SemaphoreType.DMA((fan,))],
         ),
         out_shape=spec((fan, tokens, cols), BF16),
-        cost_estimate=cost(0, 600_000), name="spread",
+        cost_estimate=cost(0, 600_000), name="spread", compiler_params=small,
     )(idx, value_cot)
     cots = lax.all_to_all(
         spread, ("shard", "tensor"), 0, 0, axis_index_groups=near, tiled=True
@@ -186,25 +191,37 @@
             in_specs=[pl.BlockSpec((16, width), lambda i, _: (i, 0)), whole(gains.shape)],
             out_specs=[
                 pl.BlockSpec(
-                    (SHARDS, 16, part),
-                    lambda i, at: (0, ((i // CORES) ^ at[1]) + CHIPS * ((i % CORES) ^ at[0]), 0),
+                    (SHARDS, 16, part // CORES),
+                    lambda i, at: (0, ((i // CORES) ^ at[1]) + CHIPS * (i % CORES), 0),
                 ),
-                pl.BlockSpec((16, 128), lambda i, _: (i, 0)),
             ],
             scratch_shapes=[pltpu.VMEM(gains.shape, F32)],
         ),
-        out_shape=[spec((SHARDS, tokens, part), BF16), spec((tokens, 128), F32)],
-        cost_estimate=cost(6_000_000, 4_300_000), name="pack",
-    )
-    sent, inv_scale = packing(idx, inputs, gains)
-    normed = lax.all_to_all(sent, "shard", 0, 0, tiled=True).reshape(SHARDS * tokens, part)
+        out_shape=[spec((SHARDS, tokens, part // CORES), BF16)],
+        cost_estimate=cost(6_000_000, 4_300_000), name="pack", compiler_params=small,
+    )
+    (sent,) = packing(idx, inputs, gains)
+    mine = lax.all_to_all(sent, "shard", 0, 0, tiled=True)
+    mine = mine.reshape(SHARDS * tokens, part // CORES)
+    theirs = lax.ppermute(mine, "tensor", swap)
+    normed = jnp.where(
+        tensor % CORES == 0,
+        jnp.concatenate([mine, theirs], axis=1),
+        jnp.concatenate([theirs, mine], axis=1),
+    )
 
     pairs = cots.reshape(SHARDS, CORES, tokens, cols)
-    own_cots = lax.dynamic_index_in_dim(pairs, tensor % CORES, 1, keepdims=False)
-    other_cots = lax.dynamic_index_in_dim(pairs, 1 - tensor % CORES, 1, keepdims=False)
+    core = tensor % CORES
     share = tokens // CORES
-    own_rows = own_cots[:, :share].reshape(SHARDS * share, cols)
-    other_rows = other_cots[:, :share].reshape(SHARDS * share, cols)
+    own_cots = lax.dynamic_index_in_dim(pairs, core, 1, keepdims=False)
+
+    def half_of(source):
+        block = lax.dynamic_slice(
+            pairs, (0, source, core * share, 0), (SHARDS, 1, share, cols)
+        )
+        return block.reshape(SHARDS * share, cols)
+
+    own_rows, other_rows = half_of(core), half_of(1 - core)
     last_dims = (((1,), (1,)), ((), ()))
     product = lax.dot_general(own_rows, value_weight, last_dims, preferred_element_type=F32)
     product += lax.dot_general(other_rows, other_weight, last_dims, preferred_element_type=F32)
@@ -221,7 +238,7 @@
         in_specs=[pl.BlockSpec((1, frows, fcols // 3), lambda i: (0, 0, i))],
         out_specs=pl.BlockSpec((replicas // 3, frows, own_cols), lambda i: (i, 0, 0)),
         out_shape=spec((replicas, frows, own_cols), BF16),
-        cost_estimate=cost(0, 1_200_000), name="outerpack",
+        cost_estimate=cost(0, 1_200_000), name="outerpack", compiler_params=small,
     )
     packed = outer_packing(pseudo_grad)
     grads = lax.all_to_all(packed, "replica", 0, 0, tiled=True)
@@ -241,7 +258,7 @@
         ),
         out_shape=[spec((16, rows), F32), spec((tokens, cols), BF16)]
         + [spec((2 * tokens, cols), BF16)] * 3,
-        cost_estimate=cost(1_000_000, 1_700_000), name="merge",
+        cost_estimate=cost(1_000_000, 1_700_000), name="merge", compiler_params=small,
     )(idx, *hidden, partial_values)
     got = [None] * SHARDS
     for k in rest:
@@ -255,7 +272,6 @@
             + [
                 whole((tokens, cols)),
                 pl.BlockSpec((16, width), lambda i, at: (at[3], 0)),
-                pl.BlockSpec((16, 128), lambda i, at: (at[3], 0)),
                 whole(gains.shape),
                 whole(grads.shape),
                 whole(momentum.shape),
@@ -269,8 +285,8 @@
         ),
         out_shape=[spec((16, width), BF16), spec((tokens, cols), BF16)]
         + [spec(momentum.shape, F32)] * 2,
-        cost_estimate=cost(2_000_000, 2_100_000), name="final",
-    )(idx, keep, *got[1:], own_values, inputs, inv_scale, gains, grads, global_params, momentum)
+        cost_estimate=cost(2_000_000, 2_100_000), name="final", compiler_params=small,
+    )(idx, keep, *got[1:], own_values, inputs, gains, grads, global_params, momentum)
     return (values, weight_grad, input_grad, new_global, new_momentum)
 
 

time: 126 us -> 111 us (0.88)
  Pallas kernels: 17.9 us -> 9.8 us
  waiting for transfers between devices: 44.3 us -> 37.3 us
    all_to_all x1, waiting for transfers between devices: 20.5 us -> 10.9 us  [body(): mine = lax.all_to_all(sent, 'shard', 0, 0, tiled=True)]
    pallas_call x1, Pallas kernels: 6.93 us -> 3.97 us  [body(): sent, = packing(idx, inputs, gains)]
    ppermute x3, waiting for transfers between devices: 19.5 us -> 21.8 us  [body(): hidden[j] = lax.ppermute(outs[j], 'tensor', chip_shift(j))]
    ppermute x0 -> x1, starting transfers between devices: none -> 1.92 us  [body(): theirs = lax.ppermute(mine, 'tensor', swap)]
    unnamed x20, local copies, waits for them, and re-layouts: 1.37 us -> 3.18 us
    pallas_call x1, Pallas kernels: 2.81 us -> 1.27 us  [body(): pl.pallas_call(merge_kernel, grid_spec=pltpu.PrefetchScalarGridSpec(num_s...]
    pallas_call x1, Pallas kernels: 3.06 us -> 1.73 us  [body(): pl.pallas_call(final_kernel, grid_spec=pltpu.PrefetchScalarGridSpec(num_s...]
    pallas_call x1, Pallas kernels: 2.71 us -> 1.4 us  [body(): packed = outer_packing(pseudo_grad)]
  transfers between devices with their start and end apart: 10 -> 11, of which waited for: 6 -> 5; matrix products, arithmetic and copies ran while one was open for 8% -> 8% of each run, Pallas kernels for 10% -> 6%
where the time goes in v5:
time: 111 us
  starting transfers between devices  50.8 us (46%)
  waiting for transfers between devices  37.3 us (34%)
  Pallas kernels  9.8 us (9%)
  matrix products  7.62 us (7%)
  local copies, waits for them, and re-layouts  4.01 us (4%)
    ppermute x3, waiting for transfers between devices, body(): hidden[j] = lax.ppermute(outs[j], 'tensor', chip_shift(j))  21.8 us
    all_to_all x1, starting transfers between devices, body(): grads = lax.all_to_all(packed, 'replica', 0, 0, tiled=True)  16.4 us
    ppermute x3, starting transfers between devices, body(): hidden[j] = lax.ppermute(outs[j], 'tensor', chip_shift(j))  12.4 us
    all_to_all x1, waiting for transfers between devices, body(): mine = lax.all_to_all(sent, 'shard', 0, 0, tiled=True)  10.9 us
    ppermute x3, starting transfers between devices, body(): got[k] = lax.ppermute(merged[k - 1], 'shard', shard_shift(k))  10.4 us
    all_to_all x1, starting transfers between devices, body(): lax.all_to_all(spread, ('shard', 'tensor'), 0, 0, axis_index_groups=near,...  4.31 us
    all_to_all x1, waiting for transfers between devices, body(): lax.all_to_all(spread, ('shard', 'tensor'), 0, 0, axis_index_groups=near,...  4.03 us
    pallas_call x1, Pallas kernels, body(): sent, = packing(idx, inputs, gains)  3.97 us
  transfers between devices with their start and end apart: 11, of which 5 were waited for; matrix products, arithmetic and copies ran while one was open for 8% of the time, Pallas kernels for 6%

profile of v5, /device:TPU:16, one launch (start us, length us, event | category | flops | bytes accessed | tf_op | source)
XLA Modules:
  0.0 110.6 jit_solution(12744495006675875730)
XLA Ops:
  0.6 0.1 pad_add_fusion.idx
  0.7 0.8 copy-done.5
  1.6 1.4 %spread.1 = bf16[8,128,256]{2,1,0:T(8,128)(2,1)} custom-call(s32[4]{0:T(128)S(1)} %pad_add_fusion.idx, bf16[128,256]{1,0:T(8,128)(2,1)S(1)} %copy-done.5), custom_call_target="tpu_custom_call" | custom-call | bytes 600000 | tf_op jit(solution)/shard_map/spread/pallas_call | solution.py:169
  3.0 4.3 %all-to-all-start = ((bf16[8,128,256]{2,1,0:T(8,128)(2,1)}), bf16[8,128,256]{2,1,0:T(8,128)(2,1)S(1)}, u32[]{:S(2)}, u32[]{:S(2)}) async-start(bf16[8,128,256]{2,1,0:T(8,128)(2,1)} %spread.1), calls=%async_computation | async-start | bytes 1048576 | tf_op jit(solution)/shard_map/all_to_all | solution.py:180
  7.3 1.6 %copy-done = bf16[128,8192]{1,0:T(8,128)(2,1)S(1)} copy-done((bf16[128,8192]{1,0:T(8,128)(2,1)S(1)}, bf16[128,8192]{1,0:T(8,128)(2,1)}, u32[]{:S(2)}) %copy-start) | copy-done | bytes 2097176
  8.9 0.7 copy-done.3
  9.6 4.0 %pack.1 = bf16[4,128,1024]{2,1,0:T(8,128)(2,1)} custom-call(s32[4]{0:T(128)S(1)} %pad_add_fusion.idx, bf16[128,8192]{1,0:T(8,128)(2,1)S(1)} %copy-done, bf16[64,128]{1,0:T(8,128)(2,1)S(1)} %bitcast.32), custom_call_target="tpu_custom_call" | custom-call | flops 6000000 | bytes 4300000 | tf_op jit(solution)/shard_map/pack/pallas_call | solution.py:203
  13.6 4.0 %all-to-all-done = bf16[8,128,256]{2,1,0:T(8,128)(2,1)S(1)} async-done(((bf16[8,128,256]{2,1,0:T(8,128)(2,1)}), bf16[8,128,256]{2,1,0:T(8,128)(2,1)S(1)}, u32[]{:S(2)}, u32[]{:S(2)}) %all-to-all-start) | async-done | bytes 524320 | tf_op jit(solution)/shard_map/all_to_all | solution.py:180
  17.6 3.5 %all-to-all-start.1 = ((bf16[4,128,1024]{2,1,0:T(8,128)(2,1)}), bf16[4,128,1024]{2,1,0:T(8,128)(2,1)S(1)}, u32[]{:S(2)}, u32[]{:S(2)}) async-start(bf16[4,128,1024]{2,1,0:T(8,128)(2,1)} %pack.1), calls=%async_computation.1 | async-start | bytes 2097152 | tf_op jit(solution)/shard_map/all_to_all | solution.py:204
  21.2 1.9 %collective-permute-start = (bf16[2048,256]{1,0:T(8,128)(2,1)}, bf16[2048,256]{1,0:T(8,128)(2,1)S(1)}, u32[]{:S(2)}, u32[]{:S(2)}) collective-permute-start(bf16[2048,256]{1,0:T(8,128)(2,1)} %param.9), channel_id=1, source_target_pairs={{0,1},{1,0},{2,3},{3,2},{4,5},{5,4},{6,7},{7,6},{8,9},{9,8},{10,11... | collective-permute-start | bytes 3145736 | tf_op jit(solution)/shard_map/ppermute | solution.py:183
  23.1 0.0 copy-done.2
  23.1 1.4 %outerpack.1 = bf16[24,64,128]{2,1,0:T(8,128)(2,1)} custom-call(f32[1,64,3072]{2,1,0:T(8,128)S(1)} %copy-done.2), custom_call_target="tpu_custom_call" | custom-call | bytes 1200000 | tf_op jit(solution)/shard_map/outerpack/pallas_call | solution.py:243
  24.5 0.7 constant_dynamic-slice_fusion
  25.3 10.9 %all-to-all-done.1 = bf16[4,128,1024]{2,1,0:T(8,128)(2,1)S(1)} async-done(((bf16[4,128,1024]{2,1,0:T(8,128)(2,1)}), bf16[4,128,1024]{2,1,0:T(8,128)(2,1)S(1)}, u32[]{:S(2)}, u32[]{:S(2)}) %all-to-all-start.1) | async-done | bytes 1048608 | tf_op jit(solution)/shard_map/all_to_all | solution.py:204
  36.2 16.4 %all-to-all-start.2 = ((bf16[24,64,128]{2,1,0:T(8,128)(2,1)}), bf16[24,64,128]{2,1,0:T(8,128)(2,1)S(1)}, u32[]{:S(2)}, u32[]{:S(2)}) async-start(bf16[24,64,128]{2,1,0:T(8,128)(2,1)} %outerpack.1), calls=%async_computation.2 | async-start | bytes 786432 | tf_op jit(solution)/shard_map/all_to_all | solution.py:244
  52.6 1.9 %collective-permute-start.4 = (bf16[512,1024]{1,0:T(8,128)(2,1)S(1)}, bf16[512,1024]{1,0:T(8,128)(2,1)S(1)}, u32[]{:S(2)}, u32[]{:S(2)}) collective-permute-start(bf16[512,1024]{1,0:T(8,128)(2,1)S(1)} %bitcast.37), channel_id=1, source_target_pairs={{0,1},{1,0},{2,3},{3,2},{4,5},{5,4},{6,7},{7,6},{8,9},{9,8},{10,11... | collective-permute-start | bytes 3145736 | tf_op jit(solution)/shard_map/ppermute | solution.py:206
  54.5 1.7 %fusion.5 = f32[256,2048]{1,0:T(8,128)S(1)} fusion(bf16[256,256]{1,0:T(8,128)(2,1)S(1)} %bitcast.41, bf16[2048,256]{1,0:T(8,128)(2,1)} %param.9), kind=kOutput, calls=%fused_computation.13 | convolution fusion | flops 268435456 | bytes 3276800 | tf_op jit(solution)/shard_map/dot_general | solution.py:226
  56.2 0.0 collective-permute-done
  56.2 0.5 fusion
  56.7 0.1 fusion.4
  56.8 2.2 %collective-permute-start.1 = (bf16[64,2048]{1,0:T(8,128)(2,1)S(1)}, bf16[64,2048]{1,0:T(8,128)(2,1)S(1)}, u32[]{:S(2)}, u32[]{:S(2)}) collective-permute-start(bf16[64,2048]{1,0:T(8,128)(2,1)S(1)} %bitcast.45), channel_id=1, source_target_pairs={{0,2},{1,3},{2,0},{3,1},{4,6},{5,7},{6,4},{7,5},{8,10},{9,11},{10,... | collective-permute-start | bytes 786440 | tf_op jit(solution)/shard_map/ppermute | solution.py:232
  59.1 6.8 %collective-permute-start.2 = (bf16[64,2048]{1,0:T(8,128)(2,1)S(1)}, bf16[64,2048]{1,0:T(8,128)(2,1)S(1)}, u32[]{:S(2)}, u32[]{:S(2)}) collective-permute-start(bf16[64,2048]{1,0:T(8,128)(2,1)S(1)} %bitcast.44), channel_id=1, source_target_pairs={{0,4},{1,5},{2,6},{3,7},{4,0},{5,1},{6,2},{7,3},{8,12},{9,13},{10,... | collective-permute-start | bytes 786440 | tf_op jit(solution)/shard_map/ppermute | solution.py:232
  65.9 0.0 copy-start.9
  65.9 3.3 %collective-permute-start.3 = (bf16[64,2048]{1,0:T(8,128)(2,1)S(1)}, bf16[64,2048]{1,0:T(8,128)(2,1)S(1)}, u32[]{:S(2)}, u32[]{:S(2)}) collective-permute-start(bf16[64,2048]{1,0:T(8,128)(2,1)S(1)} %bitcast.43), channel_id=1, source_target_pairs={{0,6},{1,7},{2,4},{3,5},{4,2},{5,3},{6,0},{7,1},{8,14},{9,15},{10,... | collective-permute-start | bytes 786440 | tf_op jit(solution)/shard_map/ppermute | solution.py:232
  69.2 0.0 collective-permute-done.4
  69.2 2.0 %convolution_convert_fusion.1.values = bf16[512,256]{1,0:T(8,128)(2,1)S(1)} fusion(bf16[2048,256]{1,0:T(8,128)(2,1)} %param.9, bf16[512,1024]{1,0:T(8,128)(2,1)S(1)} %collective-permute-done.4, bf16[512,1024]{1,0:T(8,128)(2,1)S(1)} %bitcast.38, pred[]{:T(512)S(6)} %eq.7), kind=kOutput, calls=%fused_computation.5 | convolution fusion | flops 546439168 | bytes 3407873 | tf_op jit(solution)/shard_map/dot_general | solution.py:246
  71.2 0.0 copy-done.8
  71.2 10.6 %collective-permute-done.1.r1 = bf16[64,2048]{1,0:T(8,128)(2,1)S(1)} collective-permute-done((bf16[64,2048]{1,0:T(8,128)(2,1)S(1)}, bf16[64,2048]{1,0:T(8,128)(2,1)S(1)}, u32[]{:S(2)}, u32[]{:S(2)}) %collective-permute-start.1) | collective-permute-done | bytes 262176 | tf_op jit(solution)/shard_map/ppermute | solution.py:232
  81.8 0.0 collective-permute-done.2.r2
  81.8 11.2 %collective-permute-done.3.r3 = bf16[64,2048]{1,0:T(8,128)(2,1)S(1)} collective-permute-done((bf16[64,2048]{1,0:T(8,128)(2,1)S(1)}, bf16[64,2048]{1,0:T(8,128)(2,1)S(1)}, u32[]{:S(2)}, u32[]{:S(2)}) %collective-permute-start.3) | collective-permute-done | bytes 262176 | tf_op jit(solution)/shard_map/ppermute | solution.py:232
  93.0 1.3 %merge.1 = (f32[16,2048]{1,0:T(8,128)S(1)}, bf16[128,256]{1,0:T(8,128)(2,1)S(1)}, bf16[256,256]{1,0:T(8,128)(2,1)}, bf16[256,256]{1,0:T(8,128)(2,1)S(1)}, bf16[256,256]{1,0:T(8,128)(2,1)S(1)}) custom-call(s32[4]{0:T(128)S(1)} %pad_add_fusion.idx, bf16[64,2048]{1,0:T(8,128)(2,1)S(1)} %bitcast.31, bf16[64,2048]{1,0:T(8,128)(2,1)S(1)} %collective-permute-done.1.r1, ...), custom_call_target="tpu_custom_call" | custom-call | flops 1000000 | bytes 1700000 | tf_op jit(solution)/shard_map/merge/pallas_call | solution.py:252
  94.3 2.5 %collective-permute-start.5 = (bf16[256,256]{1,0:T(8,128)(2,1)}, bf16[256,256]{1,0:T(8,128)(2,1)S(1)}, u32[]{:S(2)}, u32[]{:S(2)}) collective-permute-start(bf16[256,256]{1,0:T(8,128)(2,1)} %get-tuple-element.15), channel_id=1, source_target_pairs={{0,8},{8,0},{16,24},{24,16},{1,9},{9,1},{17,25},{25,17},{2,10},{10... | collective-permute-start | bytes 393224 | tf_op jit(solution)/shard_map/ppermute | solution.py:265
  96.8 4.0 %collective-permute-start.6 = (bf16[256,256]{1,0:T(8,128)(2,1)S(1)}, bf16[256,256]{1,0:T(8,128)(2,1)S(1)}, u32[]{:S(2)}, u32[]{:S(2)}) collective-permute-start(bf16[256,256]{1,0:T(8,128)(2,1)S(1)} %get-tuple-element.16), channel_id=1, source_target_pairs={{0,16},{8,24},{16,0},{24,8},{1,17},{9,25},{17,1},{25,9},{2,18},{10... | collective-permute-start | bytes 393224 | tf_op jit(solution)/shard_map/ppermute | solution.py:265
  100.7 4.0 %collective-permute-start.7 = (bf16[256,256]{1,0:T(8,128)(2,1)S(1)}, bf16[256,256]{1,0:T(8,128)(2,1)S(1)}, u32[]{:S(2)}, u32[]{:S(2)}) collective-permute-start(bf16[256,256]{1,0:T(8,128)(2,1)S(1)} %get-tuple-element.17), channel_id=1, source_target_pairs={{0,24},{8,16},{16,8},{24,0},{1,25},{9,17},{17,9},{25,1},{2,26},{10... | collective-permute-start | bytes 393224 | tf_op jit(solution)/shard_map/ppermute | solution.py:265
  104.7 0.0 copy-done.9
  104.7 0.0 copy-start.1
  104.7 0.0 copy-start.4
  104.8 0.0 copy-start.6
  104.8 0.0 copy-start.7
  104.8 3.5 %fusion.1 = bf16[1,2048,256]{2,1,0:T(8,128)(2,1)} fusion(bf16[512,256]{1,0:T(8,128)(2,1)S(1)} %bitcast.42, bf16[512,1024]{1,0:T(8,128)(2,1)S(1)} %collective-permute-done.4, bf16[512,1024]{1,0:T(8,128)(2,1)} %bitcast.39, pred[]{:T(512)S(6)} %eq.7), kind=kOutput, calls=%fused_computation.3 | convolution fusion | flops 546832384 | bytes 3407873 | tf_op jit(solution)/shard_map/dot_general | solution.py:247
  108.3 0.0 all-to-all-done.2.grads
  108.3 0.0 collective-permute-done.5.m1
  108.3 0.0 collective-permute-done.6.m2
  108.3 0.5 collective-permute-done.7.m3
  108.8 0.0 copy-done.1
  108.8 0.0 copy-done.4
  108.8 0.0 copy-done.6
  108.8 1.7 %final.1 = (bf16[16,8192]{1,0:T(8,128)(2,1)}, bf16[128,256]{1,0:T(8,128)(2,1)}, f32[64,128]{1,0:T(8,128)}, f32[64,128]{1,0:T(8,128)}) custom-call(s32[4]{0:T(128)S(1)} %pad_add_fusion.idx, f32[16,2048]{1,0:T(8,128)S(1)} %get-tuple-element.14.keep, bf16[256,256]{1,0:T(8,128)(2,1)S(1)} %collective-permute-done.5.m1, ...), custom_call_target="tpu_custom_call" | custom-call | flops 2000000 | bytes 2100000 | tf_op jit(solution)/shard_map/final/pallas_call | solution.py:267
  (7 shorter events, 0.0 us)
Async XLA Ops:
  0.7 0.8 copy-start.5
  3.0 14.6 %all-to-all-start = ((bf16[8,128,256]{2,1,0:T(8,128)(2,1)}), bf16[8,128,256]{2,1,0:T(8,128)(2,1)S(1)}, u32[]{:S(2)}, u32[]{:S(2)}) async-start(bf16[8,128,256]{2,1,0:T(8,128)(2,1)} %spread.1), calls=%async_computation | async-start | bytes 1048576 | tf_op jit(solution)/shard_map/all_to_all | solution.py:180
  7.3 1.6 %copy-start = (bf16[128,8192]{1,0:T(8,128)(2,1)S(1)}, bf16[128,8192]{1,0:T(8,128)(2,1)}, u32[]{:S(2)}) copy-start(bf16[128,8192]{1,0:T(8,128)(2,1)} %x_ref.7) | copy-start | bytes 6291460
  8.9 0.7 copy-start.3
  9.6 13.5 %copy-start.2 = (f32[1,64,3072]{2,1,0:T(8,128)S(1)}, f32[1,64,3072]{2,1,0:T(8,128)}, u32[]{:S(2)}) copy-start(f32[1,64,3072]{2,1,0:T(8,128)} %x_ref.6) | copy-start | bytes 2359300
  17.6 18.6 %all-to-all-start.1 = ((bf16[4,128,1024]{2,1,0:T(8,128)(2,1)}), bf16[4,128,1024]{2,1,0:T(8,128)(2,1)S(1)}, u32[]{:S(2)}, u32[]{:S(2)}) async-start(bf16[4,128,1024]{2,1,0:T(8,128)(2,1)} %pack.1), calls=%async_computation.1 | async-start | bytes 2097152 | tf_op jit(solution)/shard_map/all_to_all | solution.py:204
  21.2 35.1 %collective-permute-start = (bf16[2048,256]{1,0:T(8,128)(2,1)}, bf16[2048,256]{1,0:T(8,128)(2,1)S(1)}, u32[]{:S(2)}, u32[]{:S(2)}) collective-permute-start(bf16[2048,256]{1,0:T(8,128)(2,1)} %param.9), channel_id=1, source_target_pairs={{0,1},{1,0},{2,3},{3,2},{4,5},{5,4},{6,7},{7,6},{8,9},{9,8},{10,11... | collective-permute-start | bytes 3145736 | tf_op jit(solution)/shard_map/ppermute | solution.py:183
  36.2 35.0 %copy-start.8 = (bf16[4,128,1024]{2,1,0:T(8,128)(2,1)}, bf16[4,128,1024]{2,1,0:T(8,128)(2,1)S(1)}, u32[]{:S(2)}) copy-start(bf16[4,128,1024]{2,1,0:T(8,128)(2,1)S(1)} %all-to-all-done.1) | copy-start | bytes 3145732
  36.2 72.1 %all-to-all-start.2 = ((bf16[24,64,128]{2,1,0:T(8,128)(2,1)}), bf16[24,64,128]{2,1,0:T(8,128)(2,1)S(1)}, u32[]{:S(2)}, u32[]{:S(2)}) async-start(bf16[24,64,128]{2,1,0:T(8,128)(2,1)} %outerpack.1), calls=%async_computation.2 | async-start | bytes 786432 | tf_op jit(solution)/shard_map/all_to_all | solution.py:244
  52.6 16.6 %collective-permute-start.4 = (bf16[512,1024]{1,0:T(8,128)(2,1)S(1)}, bf16[512,1024]{1,0:T(8,128)(2,1)S(1)}, u32[]{:S(2)}, u32[]{:S(2)}) collective-permute-start(bf16[512,1024]{1,0:T(8,128)(2,1)S(1)} %bitcast.37), channel_id=1, source_target_pairs={{0,1},{1,0},{2,3},{3,2},{4,5},{5,4},{6,7},{7,6},{8,9},{9,8},{10,11... | collective-permute-start | bytes 3145736 | tf_op jit(solution)/shard_map/ppermute | solution.py:206
  56.8 25.0 %collective-permute-start.1 = (bf16[64,2048]{1,0:T(8,128)(2,1)S(1)}, bf16[64,2048]{1,0:T(8,128)(2,1)S(1)}, u32[]{:S(2)}, u32[]{:S(2)}) collective-permute-start(bf16[64,2048]{1,0:T(8,128)(2,1)S(1)} %bitcast.45), channel_id=1, source_target_pairs={{0,2},{1,3},{2,0},{3,1},{4,6},{5,7},{6,4},{7,5},{8,10},{9,11},{10,... | collective-permute-start | bytes 786440 | tf_op jit(solution)/shard_map/ppermute | solution.py:232
  59.1 22.7 %collective-permute-start.2 = (bf16[64,2048]{1,0:T(8,128)(2,1)S(1)}, bf16[64,2048]{1,0:T(8,128)(2,1)S(1)}, u32[]{:S(2)}, u32[]{:S(2)}) collective-permute-start(bf16[64,2048]{1,0:T(8,128)(2,1)S(1)} %bitcast.44), channel_id=1, source_target_pairs={{0,4},{1,5},{2,6},{3,7},{4,0},{5,1},{6,2},{7,3},{8,12},{9,13},{10,... | collective-permute-start | bytes 786440 | tf_op jit(solution)/shard_map/ppermute | solution.py:232
  65.9 38.8 %copy-start.9 = (bf16[4,1,128,256]{3,2,1,0:T(8,128)(2,1)S(1)}, bf16[4,1,128,256]{3,2,1,0:T(8,128)(2,1)}, u32[]{:S(2)}) copy-start(bf16[4,1,128,256]{3,2,1,0:T(8,128)(2,1)} %constant_dynamic-slice_fusion) | copy-start | bytes 786436
  65.9 27.1 %collective-permute-start.3 = (bf16[64,2048]{1,0:T(8,128)(2,1)S(1)}, bf16[64,2048]{1,0:T(8,128)(2,1)S(1)}, u32[]{:S(2)}, u32[]{:S(2)}) collective-permute-start(bf16[64,2048]{1,0:T(8,128)(2,1)S(1)} %bitcast.43), channel_id=1, source_target_pairs={{0,6},{1,7},{2,4},{3,5},{4,2},{5,3},{6,0},{7,1},{8,14},{9,15},{10,... | collective-permute-start | bytes 786440 | tf_op jit(solution)/shard_map/ppermute | solution.py:232
  94.3 14.0 %collective-permute-start.5 = (bf16[256,256]{1,0:T(8,128)(2,1)}, bf16[256,256]{1,0:T(8,128)(2,1)S(1)}, u32[]{:S(2)}, u32[]{:S(2)}) collective-permute-start(bf16[256,256]{1,0:T(8,128)(2,1)} %get-tuple-element.15), channel_id=1, source_target_pairs={{0,8},{8,0},{16,24},{24,16},{1,9},{9,1},{17,25},{25,17},{2,10},{10... | collective-permute-start | bytes 393224 | tf_op jit(solution)/shard_map/ppermute | solution.py:265
  96.8 11.5 %collective-permute-start.6 = (bf16[256,256]{1,0:T(8,128)(2,1)S(1)}, bf16[256,256]{1,0:T(8,128)(2,1)S(1)}, u32[]{:S(2)}, u32[]{:S(2)}) collective-permute-start(bf16[256,256]{1,0:T(8,128)(2,1)S(1)} %get-tuple-element.16), channel_id=1, source_target_pairs={{0,16},{8,24},{16,0},{24,8},{1,17},{9,25},{17,1},{25,9},{2,18},{10... | collective-permute-start | bytes 393224 | tf_op jit(solution)/shard_map/ppermute | solution.py:265
  100.7 8.1 %collective-permute-start.7 = (bf16[256,256]{1,0:T(8,128)(2,1)S(1)}, bf16[256,256]{1,0:T(8,128)(2,1)S(1)}, u32[]{:S(2)}, u32[]{:S(2)}) collective-permute-start(bf16[256,256]{1,0:T(8,128)(2,1)S(1)} %get-tuple-element.17), channel_id=1, source_target_pairs={{0,24},{8,16},{16,8},{24,0},{1,25},{9,17},{17,9},{25,1},{2,26},{10... | collective-permute-start | bytes 393224 | tf_op jit(solution)/shard_map/ppermute | solution.py:265
  104.7 4.1 %copy-start.1 = (bf16[128,8192]{1,0:T(8,128)(2,1)S(1)}, bf16[128,8192]{1,0:T(8,128)(2,1)}, u32[]{:S(2)}) copy-start(bf16[128,8192]{1,0:T(8,128)(2,1)} %x_ref.7) | copy-start | bytes 6291460
  104.7 4.1 %copy-start.4 = (bf16[8192]{0:T(1024)(128)(2,1)S(1)}, bf16[8192]{0:T(1024)(128)(2,1)}, u32[]{:S(2)}) copy-start(bf16[8192]{0:T(1024)(128)(2,1)} %param.8) | copy-start | bytes 49156
  104.8 4.1 %copy-start.6 = (f32[64,128]{1,0:T(8,128)S(1)}, f32[64,128]{1,0:T(8,128)}, u32[]{:S(2)}) copy-start(f32[64,128]{1,0:T(8,128)} %p_ref.1) | copy-start | bytes 98308
  104.8 4.1 %copy-start.7 = (f32[64,128]{1,0:T(8,128)S(1)}, f32[64,128]{1,0:T(8,128)}, u32[]{:S(2)}) copy-start(f32[64,128]{1,0:T(8,128)} %q_ref.1) | copy-start | bytes 98308

commit v6 on v5

--- a/solution.py
+++ b/solution.py
@@ -67,64 +67,54 @@
             o_ref[d, :, q * 128:(q + 1) * 128] = (wide * inv * gain[pl.ds(row, 1), :]).astype(BF16)
 
 
-def merge_kernel(idx, h0, r1, r2, r3, values, keep, v0, m1, m2, m3):
-    tokens, cols = v0.shape
-    for k, out in enumerate((keep, m1, m2, m3)):
+def merge_kernel(idx, h0, r1, r2, r3, values, m0, m1, m2, m3):
+    cols = m0.shape[1]
+    tokens = m0.shape[0] // 2
+    for k, out in enumerate((m0, m1, m2, m3)):
         at = pl.ds(pl.multiple_of((idx[2] ^ k) * 16, 16), 16)
         for q in range(h0.shape[1] // cols):
             lanes = slice(q * cols, (q + 1) * cols)
             total = h0[at, lanes].astype(F32) + r1[at, lanes].astype(F32)
             total += r2[at, lanes].astype(F32) + r3[at, lanes].astype(F32)
-            if k == 0:
-                out[:, lanes] = total
-            else:
-                out[q * 16:(q + 1) * 16, :] = total.astype(BF16)
-    for k, out in enumerate((v0, m1, m2, m3)):
-        val = values[pl.ds(pl.multiple_of((idx[2] ^ k) * tokens, tokens), tokens), :]
-        if k == 0:
-            out[...] = val
-        else:
-            out[tokens:, :] = val
+            out[q * 16:(q + 1) * 16, :] = total.astype(BF16)
+        out[tokens:, :] = values[pl.ds(pl.multiple_of((idx[2] ^ k) * tokens, tokens), tokens), :]
 
 
 def final_kernel(
-    idx, keep, m1, m2, m3, v0, x_ref, g_ref, grads, p_ref, q_ref,
+    idx, m0, m1, m2, m3, x_ref, g_ref, grads, p_ref, q_ref,
     o_ref, val_ref, new_p, new_m, gain,
 ):
     gain[...] = g_ref[...].astype(F32)
-    part = keep.shape[1]
-    tokens, cols = v0.shape
+    tokens = val_ref.shape[0]
+    cols = m0.shape[1]
     width = x_ref.shape[1]
+    part = width // SHARDS
     lanes = 128
     inv = inverse_scale(x_ref)
     places = []
-    for k, got in enumerate((keep, m1, m2, m3)):
+    for k, got in enumerate((m0, m1, m2, m3)):
         first = (idx[2] ^ k) * (part // lanes)
         for q in range(part // lanes):
             at = pl.ds(pl.multiple_of((first + q) * lanes, lanes), lanes)
-            places.append((k, got, q, first + q, at))
-
-    def scaled(k, got, q, row, at):
-        if k == 0:
-            term = got[:, q * lanes:(q + 1) * lanes]
-        else:
-            r, l = q * lanes // cols * 16, q * lanes % cols
-            term = got[r:r + 16, l:l + lanes].astype(F32)
-        return gain[pl.ds(row, 1), :] * term
+            places.append((got, q, first + q, at))
+
+    def scaled(got, q, row, at):
+        r, l = q * lanes // cols * 16, q * lanes % cols
+        return gain[pl.ds(row, 1), :] * got[r:r + 16, l:l + lanes].astype(F32)
 
     total = jnp.zeros((16, lanes), F32)
     for place in places:
-        total += x_ref[:, place[4]].astype(F32) * scaled(*place)
+        total += x_ref[:, place[3]].astype(F32) * scaled(*place)
     mean = jnp.sum(total, axis=1, keepdims=True) / width
     factor = inv * inv * inv * mean
     for place in places:
-        at = place[4]
+        at = place[3]
         o_ref[:, at] = (inv * scaled(*place) - x_ref[:, at].astype(F32) * factor).astype(BF16)
     for place in range(2 * CHIPS):
-        rows = slice(place * 16, (place + 1) * 16)
-        summed = v0[rows, :].astype(F32)
+        rows = slice(tokens + place * 16, tokens + (place + 1) * 16)
+        summed = m0[rows, :].astype(F32)
         for got in (m1, m2, m3):
-            summed += got[tokens + place * 16:tokens + (place + 1) * 16, :].astype(F32)
+            summed += got[rows, :].astype(F32)
         to = pl.ds(pl.multiple_of(block_of(idx, place) * 16, 16), 16)
         val_ref[to, :] = summed.astype(BF16)
 
@@ -249,28 +239,26 @@
         (((0,), (0,)), ((), ())), preferred_element_type=F32,
     ).astype(BF16)[None]
 
-    keep, own_values, *merged = pl.pallas_call(
+    merged = pl.pallas_call(
         merge_kernel,
         grid_spec=pltpu.PrefetchScalarGridSpec(
             num_scalar_prefetch=1, grid=(1,),
             in_specs=[whole((64, rows))] * CHIPS + [whole((SHARDS * tokens, cols))],
-            out_specs=[whole((16, rows)), whole((tokens, cols))] + [whole((2 * tokens, cols))] * 3,
-        ),
-        out_shape=[spec((16, rows), F32), spec((tokens, cols), BF16)]
-        + [spec((2 * tokens, cols), BF16)] * 3,
+            out_specs=[whole((2 * tokens, cols))] * SHARDS,
+        ),
+        out_shape=[spec((2 * tokens, cols), BF16)] * SHARDS,
         cost_estimate=cost(1_000_000, 1_700_000), name="merge", compiler_params=small,
     )(idx, *hidden, partial_values)
-    got = [None] * SHARDS
+    got = [merged[0], None, None, None]
     for k in rest:
-        got[k] = lax.ppermute(merged[k - 1], "shard", shard_shift(k))
+        got[k] = lax.ppermute(merged[k], "shard", shard_shift(k))
 
     input_grad, values, new_global, new_momentum = pl.pallas_call(
         final_kernel,
         grid_spec=pltpu.PrefetchScalarGridSpec(
             num_scalar_prefetch=1, grid=(1,),
-            in_specs=[whole((16, rows))] + [whole((2 * tokens, cols))] * 3
+            in_specs=[whole((2 * tokens, cols))] * SHARDS
             + [
-                whole((tokens, cols)),
                 pl.BlockSpec((16, width), lambda i, at: (at[3], 0)),
                 whole(gains.shape),
                 whole(grads.shape),
@@ -286,7 +274,7 @@
         out_shape=[spec((16, width), BF16), spec((tokens, cols), BF16)]
         + [spec(momentum.shape, F32)] * 2,
         cost_estimate=cost(2_000_000, 2_100_000), name="final", compiler_params=small,
-    )(idx, keep, *got[1:], own_values, inputs, gains, grads, global_params, momentum)
+    )(idx, *got, inputs, gains, grads, global_params, momentum)
     return (values, weight_grad, input_grad, new_global, new_momentum)
 
 

time: 111 us -> 111 us (level)
  no operation moved by 1% of the time
where the time goes in v6:
time: 111 us; the launch traced here: 110 us
  starting transfers between devices  50.8 us (46%)
  waiting for transfers between devices  37.3 us (34%)
  Pallas kernels  9.22 us (8%)
  matrix products  7.62 us (7%)
  local copies, waits for them, and re-layouts  4.01 us (4%)
    ppermute x3, waiting for transfers between devices, body(): hidden[j] = lax.ppermute(outs[j], 'tensor', chip_shift(j))  21.8 us
    all_to_all x1, starting transfers between devices, body(): grads = lax.all_to_all(packed, 'replica', 0, 0, tiled=True)  16.4 us
    ppermute x3, starting transfers between devices, body(): hidden[j] = lax.ppermute(outs[j], 'tensor', chip_shift(j))  12.4 us
    all_to_all x1, waiting for transfers between devices, body(): mine = lax.all_to_all(sent, 'shard', 0, 0, tiled=True)  10.9 us
    ppermute x3, starting transfers between devices, body(): got[k] = lax.ppermute(merged[k], 'shard', shard_shift(k))  10.4 us
    all_to_all x1, starting transfers between devices, body(): lax.all_to_all(spread, ('shard', 'tensor'), 0, 0, axis_index_groups=near,...  4.31 us
    all_to_all x1, waiting for transfers between devices, body(): lax.all_to_all(spread, ('shard', 'tensor'), 0, 0, axis_index_groups=near,...  4.03 us
    pallas_call x1, Pallas kernels, body(): sent, = packing(idx, inputs, gains)  3.97 us
  transfers between devices with their start and end apart: 11, of which 5 were waited for; matrix products, arithmetic and copies ran while one was open for 8% of the time, Pallas kernels for 6%

profile of v6, /device:TPU:16, one launch (start us, length us, event | category | flops | bytes accessed | tf_op | source)
XLA Modules:
  0.0 110.0 jit_solution(1346946643837985595)
XLA Ops:
  0.6 0.1 pad_add_fusion.idx
  0.7 0.8 copy-done.5
  1.6 1.4 %spread.1 = bf16[8,128,256]{2,1,0:T(8,128)(2,1)} custom-call(s32[4]{0:T(128)S(1)} %pad_add_fusion.idx, bf16[128,256]{1,0:T(8,128)(2,1)S(1)} %copy-done.5), custom_call_target="tpu_custom_call" | custom-call | bytes 600000 | tf_op jit(solution)/shard_map/spread/pallas_call | solution.py:159
  3.0 4.3 %all-to-all-start = ((bf16[8,128,256]{2,1,0:T(8,128)(2,1)}), bf16[8,128,256]{2,1,0:T(8,128)(2,1)S(1)}, u32[]{:S(2)}, u32[]{:S(2)}) async-start(bf16[8,128,256]{2,1,0:T(8,128)(2,1)} %spread.1), calls=%async_computation | async-start | bytes 1048576 | tf_op jit(solution)/shard_map/all_to_all | solution.py:170
  7.3 1.6 %copy-done = bf16[128,8192]{1,0:T(8,128)(2,1)S(1)} copy-done((bf16[128,8192]{1,0:T(8,128)(2,1)S(1)}, bf16[128,8192]{1,0:T(8,128)(2,1)}, u32[]{:S(2)}) %copy-start) | copy-done | bytes 2097176
  8.9 0.7 copy-done.3
  9.6 4.0 %pack.1 = bf16[4,128,1024]{2,1,0:T(8,128)(2,1)} custom-call(s32[4]{0:T(128)S(1)} %pad_add_fusion.idx, bf16[128,8192]{1,0:T(8,128)(2,1)S(1)} %copy-done, bf16[64,128]{1,0:T(8,128)(2,1)S(1)} %bitcast.32), custom_call_target="tpu_custom_call" | custom-call | flops 6000000 | bytes 4300000 | tf_op jit(solution)/shard_map/pack/pallas_call | solution.py:193
  13.6 4.0 %all-to-all-done = bf16[8,128,256]{2,1,0:T(8,128)(2,1)S(1)} async-done(((bf16[8,128,256]{2,1,0:T(8,128)(2,1)}), bf16[8,128,256]{2,1,0:T(8,128)(2,1)S(1)}, u32[]{:S(2)}, u32[]{:S(2)}) %all-to-all-start) | async-done | bytes 524320 | tf_op jit(solution)/shard_map/all_to_all | solution.py:170
  17.6 3.5 %all-to-all-start.1 = ((bf16[4,128,1024]{2,1,0:T(8,128)(2,1)}), bf16[4,128,1024]{2,1,0:T(8,128)(2,1)S(1)}, u32[]{:S(2)}, u32[]{:S(2)}) async-start(bf16[4,128,1024]{2,1,0:T(8,128)(2,1)} %pack.1), calls=%async_computation.1 | async-start | bytes 2097152 | tf_op jit(solution)/shard_map/all_to_all | solution.py:194
  21.2 1.9 %collective-permute-start = (bf16[2048,256]{1,0:T(8,128)(2,1)}, bf16[2048,256]{1,0:T(8,128)(2,1)S(1)}, u32[]{:S(2)}, u32[]{:S(2)}) collective-permute-start(bf16[2048,256]{1,0:T(8,128)(2,1)} %param.9), channel_id=1, source_target_pairs={{0,1},{1,0},{2,3},{3,2},{4,5},{5,4},{6,7},{7,6},{8,9},{9,8},{10,11... | collective-permute-start | bytes 3145736 | tf_op jit(solution)/shard_map/ppermute | solution.py:173
  23.1 0.0 copy-done.2
  23.1 1.4 %outerpack.1 = bf16[24,64,128]{2,1,0:T(8,128)(2,1)} custom-call(f32[1,64,3072]{2,1,0:T(8,128)S(1)} %copy-done.2), custom_call_target="tpu_custom_call" | custom-call | bytes 1200000 | tf_op jit(solution)/shard_map/outerpack/pallas_call | solution.py:233
  24.5 0.7 constant_dynamic-slice_fusion
  25.3 10.9 %all-to-all-done.1 = bf16[4,128,1024]{2,1,0:T(8,128)(2,1)S(1)} async-done(((bf16[4,128,1024]{2,1,0:T(8,128)(2,1)}), bf16[4,128,1024]{2,1,0:T(8,128)(2,1)S(1)}, u32[]{:S(2)}, u32[]{:S(2)}) %all-to-all-start.1) | async-done | bytes 1048608 | tf_op jit(solution)/shard_map/all_to_all | solution.py:194
  36.2 16.4 %all-to-all-start.2 = ((bf16[24,64,128]{2,1,0:T(8,128)(2,1)}), bf16[24,64,128]{2,1,0:T(8,128)(2,1)S(1)}, u32[]{:S(2)}, u32[]{:S(2)}) async-start(bf16[24,64,128]{2,1,0:T(8,128)(2,1)} %outerpack.1), calls=%async_computation.2 | async-start | bytes 786432 | tf_op jit(solution)/shard_map/all_to_all | solution.py:234
  52.6 1.9 %collective-permute-start.4 = (bf16[512,1024]{1,0:T(8,128)(2,1)S(1)}, bf16[512,1024]{1,0:T(8,128)(2,1)S(1)}, u32[]{:S(2)}, u32[]{:S(2)}) collective-permute-start(bf16[512,1024]{1,0:T(8,128)(2,1)S(1)} %bitcast.37), channel_id=1, source_target_pairs={{0,1},{1,0},{2,3},{3,2},{4,5},{5,4},{6,7},{7,6},{8,9},{9,8},{10,11... | collective-permute-start | bytes 3145736 | tf_op jit(solution)/shard_map/ppermute | solution.py:196
  54.5 1.7 %fusion.5 = f32[256,2048]{1,0:T(8,128)S(1)} fusion(bf16[256,256]{1,0:T(8,128)(2,1)S(1)} %bitcast.41, bf16[2048,256]{1,0:T(8,128)(2,1)} %param.9), kind=kOutput, calls=%fused_computation.13 | convolution fusion | flops 268435456 | bytes 3276800 | tf_op jit(solution)/shard_map/dot_general | solution.py:216
  56.2 0.0 collective-permute-done
  56.2 0.5 fusion
  56.7 0.1 fusion.4
  56.8 2.2 %collective-permute-start.1 = (bf16[64,2048]{1,0:T(8,128)(2,1)S(1)}, bf16[64,2048]{1,0:T(8,128)(2,1)S(1)}, u32[]{:S(2)}, u32[]{:S(2)}) collective-permute-start(bf16[64,2048]{1,0:T(8,128)(2,1)S(1)} %bitcast.45), channel_id=1, source_target_pairs={{0,2},{1,3},{2,0},{3,1},{4,6},{5,7},{6,4},{7,5},{8,10},{9,11},{10,... | collective-permute-start | bytes 786440 | tf_op jit(solution)/shard_map/ppermute | solution.py:222
  59.1 6.8 %collective-permute-start.2 = (bf16[64,2048]{1,0:T(8,128)(2,1)S(1)}, bf16[64,2048]{1,0:T(8,128)(2,1)S(1)}, u32[]{:S(2)}, u32[]{:S(2)}) collective-permute-start(bf16[64,2048]{1,0:T(8,128)(2,1)S(1)} %bitcast.44), channel_id=1, source_target_pairs={{0,4},{1,5},{2,6},{3,7},{4,0},{5,1},{6,2},{7,3},{8,12},{9,13},{10,... | collective-permute-start | bytes 786440 | tf_op jit(solution)/shard_map/ppermute | solution.py:222
  65.9 0.0 copy-start.9
  65.9 3.3 %collective-permute-start.3 = (bf16[64,2048]{1,0:T(8,128)(2,1)S(1)}, bf16[64,2048]{1,0:T(8,128)(2,1)S(1)}, u32[]{:S(2)}, u32[]{:S(2)}) collective-permute-start(bf16[64,2048]{1,0:T(8,128)(2,1)S(1)} %bitcast.43), channel_id=1, source_target_pairs={{0,6},{1,7},{2,4},{3,5},{4,2},{5,3},{6,0},{7,1},{8,14},{9,15},{10,... | collective-permute-start | bytes 786440 | tf_op jit(solution)/shard_map/ppermute | solution.py:222
  69.2 0.0 collective-permute-done.4
  69.2 2.0 %convolution_convert_fusion.1.values = bf16[512,256]{1,0:T(8,128)(2,1)S(1)} fusion(bf16[2048,256]{1,0:T(8,128)(2,1)} %param.9, bf16[512,1024]{1,0:T(8,128)(2,1)S(1)} %collective-permute-done.4, bf16[512,1024]{1,0:T(8,128)(2,1)S(1)} %bitcast.38, pred[]{:T(512)S(6)} %eq.7), kind=kOutput, calls=%fused_computation.5 | convolution fusion | flops 546439168 | bytes 3407873 | tf_op jit(solution)/shard_map/dot_general | solution.py:236
  71.2 0.0 copy-done.8
  71.2 10.6 %collective-permute-done.1.r1 = bf16[64,2048]{1,0:T(8,128)(2,1)S(1)} collective-permute-done((bf16[64,2048]{1,0:T(8,128)(2,1)S(1)}, bf16[64,2048]{1,0:T(8,128)(2,1)S(1)}, u32[]{:S(2)}, u32[]{:S(2)}) %collective-permute-start.1) | collective-permute-done | bytes 262176 | tf_op jit(solution)/shard_map/ppermute | solution.py:222
  81.8 0.0 collective-permute-done.2.r2
  81.8 11.2 %collective-permute-done.3.r3 = bf16[64,2048]{1,0:T(8,128)(2,1)S(1)} collective-permute-done((bf16[64,2048]{1,0:T(8,128)(2,1)S(1)}, bf16[64,2048]{1,0:T(8,128)(2,1)S(1)}, u32[]{:S(2)}, u32[]{:S(2)}) %collective-permute-start.3) | collective-permute-done | bytes 262176 | tf_op jit(solution)/shard_map/ppermute | solution.py:222
  93.0 0.7 merge.1
  93.7 2.5 %collective-permute-start.5 = (bf16[256,256]{1,0:T(8,128)(2,1)S(1)}, bf16[256,256]{1,0:T(8,128)(2,1)S(1)}, u32[]{:S(2)}, u32[]{:S(2)}) collective-permute-start(bf16[256,256]{1,0:T(8,128)(2,1)S(1)} %get-tuple-element.14), channel_id=1, source_target_pairs={{0,8},{8,0},{16,24},{24,16},{1,9},{9,1},{17,25},{25,17},{2,10},{10... | collective-permute-start | bytes 393224 | tf_op jit(solution)/shard_map/ppermute | solution.py:254
  96.2 4.0 %collective-permute-start.6 = (bf16[256,256]{1,0:T(8,128)(2,1)S(1)}, bf16[256,256]{1,0:T(8,128)(2,1)S(1)}, u32[]{:S(2)}, u32[]{:S(2)}) collective-permute-start(bf16[256,256]{1,0:T(8,128)(2,1)S(1)} %get-tuple-element.15), channel_id=1, source_target_pairs={{0,16},{8,24},{16,0},{24,8},{1,17},{9,25},{17,1},{25,9},{2,18},{10... | collective-permute-start | bytes 393224 | tf_op jit(solution)/shard_map/ppermute | solution.py:254
  100.2 4.0 %collective-permute-start.7 = (bf16[256,256]{1,0:T(8,128)(2,1)S(1)}, bf16[256,256]{1,0:T(8,128)(2,1)S(1)}, u32[]{:S(2)}, u32[]{:S(2)}) collective-permute-start(bf16[256,256]{1,0:T(8,128)(2,1)S(1)} %get-tuple-element.16), channel_id=1, source_target_pairs={{0,24},{8,16},{16,8},{24,0},{1,25},{9,17},{17,9},{25,1},{2,26},{10... | collective-permute-start | bytes 393224 | tf_op jit(solution)/shard_map/ppermute | solution.py:254
  104.2 0.0 copy-done.9
  104.2 0.0 copy-start.1
  104.2 0.0 copy-start.4
  104.2 0.0 copy-start.6
  104.2 0.0 copy-start.7
  104.2 3.5 %fusion.1 = bf16[1,2048,256]{2,1,0:T(8,128)(2,1)} fusion(bf16[512,256]{1,0:T(8,128)(2,1)S(1)} %bitcast.42, bf16[512,1024]{1,0:T(8,128)(2,1)S(1)} %collective-permute-done.4, bf16[512,1024]{1,0:T(8,128)(2,1)} %bitcast.39, pred[]{:T(512)S(6)} %eq.7), kind=kOutput, calls=%fused_computation.3 | convolution fusion | flops 546832384 | bytes 3407873 | tf_op jit(solution)/shard_map/dot_general | solution.py:237
  107.7 0.0 all-to-all-done.2.grads
  107.7 0.0 collective-permute-done.5.m1
  107.7 0.0 collective-permute-done.6.m2
  107.7 0.5 collective-permute-done.7.m3
  108.2 0.0 copy-done.1
  108.2 0.0 copy-done.4
  108.2 0.0 copy-done.6
  108.3 1.7 %final.1 = (bf16[16,8192]{1,0:T(8,128)(2,1)}, bf16[128,256]{1,0:T(8,128)(2,1)}, f32[64,128]{1,0:T(8,128)}, f32[64,128]{1,0:T(8,128)}) custom-call(s32[4]{0:T(128)S(1)} %pad_add_fusion.idx, bf16[256,256]{1,0:T(8,128)(2,1)S(1)} %get-tuple-element.13.m0, bf16[256,256]{1,0:T(8,128)(2,1)S(1)} %collective-permute-done.5.m1, ...), custom_call_target="tpu_custom_call" | custom-call | flops 2000000 | bytes 2100000 | tf_op jit(solution)/shard_map/final/pallas_call | solution.py:256
  (7 shorter events, 0.0 us)
Async XLA Ops:
  0.7 0.8 copy-start.5
  3.0 14.6 %all-to-all-start = ((bf16[8,128,256]{2,1,0:T(8,128)(2,1)}), bf16[8,128,256]{2,1,0:T(8,128)(2,1)S(1)}, u32[]{:S(2)}, u32[]{:S(2)}) async-start(bf16[8,128,256]{2,1,0:T(8,128)(2,1)} %spread.1), calls=%async_computation | async-start | bytes 1048576 | tf_op jit(solution)/shard_map/all_to_all | solution.py:170
  7.3 1.6 %copy-start = (bf16[128,8192]{1,0:T(8,128)(2,1)S(1)}, bf16[128,8192]{1,0:T(8,128)(2,1)}, u32[]{:S(2)}) copy-start(bf16[128,8192]{1,0:T(8,128)(2,1)} %x_ref.7) | copy-start | bytes 6291460
  8.9 0.7 copy-start.3
  9.6 13.5 %copy-start.2 = (f32[1,64,3072]{2,1,0:T(8,128)S(1)}, f32[1,64,3072]{2,1,0:T(8,128)}, u32[]{:S(2)}) copy-start(f32[1,64,3072]{2,1,0:T(8,128)} %x_ref.6) | copy-start | bytes 2359300
  17.6 18.6 %all-to-all-start.1 = ((bf16[4,128,1024]{2,1,0:T(8,128)(2,1)}), bf16[4,128,1024]{2,1,0:T(8,128)(2,1)S(1)}, u32[]{:S(2)}, u32[]{:S(2)}) async-start(bf16[4,128,1024]{2,1,0:T(8,128)(2,1)} %pack.1), calls=%async_computation.1 | async-start | bytes 2097152 | tf_op jit(solution)/shard_map/all_to_all | solution.py:194
  21.2 35.1 %collective-permute-start = (bf16[2048,256]{1,0:T(8,128)(2,1)}, bf16[2048,256]{1,0:T(8,128)(2,1)S(1)}, u32[]{:S(2)}, u32[]{:S(2)}) collective-permute-start(bf16[2048,256]{1,0:T(8,128)(2,1)} %param.9), channel_id=1, source_target_pairs={{0,1},{1,0},{2,3},{3,2},{4,5},{5,4},{6,7},{7,6},{8,9},{9,8},{10,11... | collective-permute-start | bytes 3145736 | tf_op jit(solution)/shard_map/ppermute | solution.py:173
  36.2 35.0 %copy-start.8 = (bf16[4,128,1024]{2,1,0:T(8,128)(2,1)}, bf16[4,128,1024]{2,1,0:T(8,128)(2,1)S(1)}, u32[]{:S(2)}) copy-start(bf16[4,128,1024]{2,1,0:T(8,128)(2,1)S(1)} %all-to-all-done.1) | copy-start | bytes 3145732
  36.2 71.5 %all-to-all-start.2 = ((bf16[24,64,128]{2,1,0:T(8,128)(2,1)}), bf16[24,64,128]{2,1,0:T(8,128)(2,1)S(1)}, u32[]{:S(2)}, u32[]{:S(2)}) async-start(bf16[24,64,128]{2,1,0:T(8,128)(2,1)} %outerpack.1), calls=%async_computation.2 | async-start | bytes 786432 | tf_op jit(solution)/shard_map/all_to_all | solution.py:234
  52.6 16.6 %collective-permute-start.4 = (bf16[512,1024]{1,0:T(8,128)(2,1)S(1)}, bf16[512,1024]{1,0:T(8,128)(2,1)S(1)}, u32[]{:S(2)}, u32[]{:S(2)}) collective-permute-start(bf16[512,1024]{1,0:T(8,128)(2,1)S(1)} %bitcast.37), channel_id=1, source_target_pairs={{0,1},{1,0},{2,3},{3,2},{4,5},{5,4},{6,7},{7,6},{8,9},{9,8},{10,11... | collective-permute-start | bytes 3145736 | tf_op jit(solution)/shard_map/ppermute | solution.py:196
  56.8 25.0 %collective-permute-start.1 = (bf16[64,2048]{1,0:T(8,128)(2,1)S(1)}, bf16[64,2048]{1,0:T(8,128)(2,1)S(1)}, u32[]{:S(2)}, u32[]{:S(2)}) collective-permute-start(bf16[64,2048]{1,0:T(8,128)(2,1)S(1)} %bitcast.45), channel_id=1, source_target_pairs={{0,2},{1,3},{2,0},{3,1},{4,6},{5,7},{6,4},{7,5},{8,10},{9,11},{10,... | collective-permute-start | bytes 786440 | tf_op jit(solution)/shard_map/ppermute | solution.py:222
  59.1 22.7 %collective-permute-start.2 = (bf16[64,2048]{1,0:T(8,128)(2,1)S(1)}, bf16[64,2048]{1,0:T(8,128)(2,1)S(1)}, u32[]{:S(2)}, u32[]{:S(2)}) collective-permute-start(bf16[64,2048]{1,0:T(8,128)(2,1)S(1)} %bitcast.44), channel_id=1, source_target_pairs={{0,4},{1,5},{2,6},{3,7},{4,0},{5,1},{6,2},{7,3},{8,12},{9,13},{10,... | collective-permute-start | bytes 786440 | tf_op jit(solution)/shard_map/ppermute | solution.py:222
  65.9 38.2 %copy-start.9 = (bf16[4,1,128,256]{3,2,1,0:T(8,128)(2,1)S(1)}, bf16[4,1,128,256]{3,2,1,0:T(8,128)(2,1)}, u32[]{:S(2)}) copy-start(bf16[4,1,128,256]{3,2,1,0:T(8,128)(2,1)} %constant_dynamic-slice_fusion) | copy-start | bytes 786436
  65.9 27.1 %collective-permute-start.3 = (bf16[64,2048]{1,0:T(8,128)(2,1)S(1)}, bf16[64,2048]{1,0:T(8,128)(2,1)S(1)}, u32[]{:S(2)}, u32[]{:S(2)}) collective-permute-start(bf16[64,2048]{1,0:T(8,128)(2,1)S(1)} %bitcast.43), channel_id=1, source_target_pairs={{0,6},{1,7},{2,4},{3,5},{4,2},{5,3},{6,0},{7,1},{8,14},{9,15},{10,... | collective-permute-start | bytes 786440 | tf_op jit(solution)/shard_map/ppermute | solution.py:222
  93.7 14.0 %collective-permute-start.5 = (bf16[256,256]{1,0:T(8,128)(2,1)S(1)}, bf16[256,256]{1,0:T(8,128)(2,1)S(1)}, u32[]{:S(2)}, u32[]{:S(2)}) collective-permute-start(bf16[256,256]{1,0:T(8,128)(2,1)S(1)} %get-tuple-element.14), channel_id=1, source_target_pairs={{0,8},{8,0},{16,24},{24,16},{1,9},{9,1},{17,25},{25,17},{2,10},{10... | collective-permute-start | bytes 393224 | tf_op jit(solution)/shard_map/ppermute | solution.py:254
  96.2 11.5 %collective-permute-start.6 = (bf16[256,256]{1,0:T(8,128)(2,1)S(1)}, bf16[256,256]{1,0:T(8,128)(2,1)S(1)}, u32[]{:S(2)}, u32[]{:S(2)}) collective-permute-start(bf16[256,256]{1,0:T(8,128)(2,1)S(1)} %get-tuple-element.15), channel_id=1, source_target_pairs={{0,16},{8,24},{16,0},{24,8},{1,17},{9,25},{17,1},{25,9},{2,18},{10... | collective-permute-start | bytes 393224 | tf_op jit(solution)/shard_map/ppermute | solution.py:254
  100.2 8.1 %collective-permute-start.7 = (bf16[256,256]{1,0:T(8,128)(2,1)S(1)}, bf16[256,256]{1,0:T(8,128)(2,1)S(1)}, u32[]{:S(2)}, u32[]{:S(2)}) collective-permute-start(bf16[256,256]{1,0:T(8,128)(2,1)S(1)} %get-tuple-element.16), channel_id=1, source_target_pairs={{0,24},{8,16},{16,8},{24,0},{1,25},{9,17},{17,9},{25,1},{2,26},{10... | collective-permute-start | bytes 393224 | tf_op jit(solution)/shard_map/ppermute | solution.py:254
  104.2 4.1 %copy-start.1 = (bf16[128,8192]{1,0:T(8,128)(2,1)S(1)}, bf16[128,8192]{1,0:T(8,128)(2,1)}, u32[]{:S(2)}) copy-start(bf16[128,8192]{1,0:T(8,128)(2,1)} %x_ref.7) | copy-start | bytes 6291460
  104.2 4.1 %copy-start.4 = (bf16[8192]{0:T(1024)(128)(2,1)S(1)}, bf16[8192]{0:T(1024)(128)(2,1)}, u32[]{:S(2)}) copy-start(bf16[8192]{0:T(1024)(128)(2,1)} %param.8) | copy-start | bytes 49156
  104.2 4.1 %copy-start.6 = (f32[64,128]{1,0:T(8,128)S(1)}, f32[64,128]{1,0:T(8,128)}, u32[]{:S(2)}) copy-start(f32[64,128]{1,0:T(8,128)} %p_ref.1) | copy-start | bytes 98308
  104.2 4.1 %copy-start.7 = (f32[64,128]{1,0:T(8,128)S(1)}, f32[64,128]{1,0:T(8,128)}, u32[]{:S(2)}) copy-start(f32[64,128]{1,0:T(8,128)} %q_ref.1) | copy-start | bytes 98308

commit v7 on v6

--- a/solution.py
+++ b/solution.py
@@ -213,8 +213,11 @@
 
     own_rows, other_rows = half_of(core), half_of(1 - core)
     last_dims = (((1,), (1,)), ((), ()))
-    product = lax.dot_general(own_rows, value_weight, last_dims, preferred_element_type=F32)
-    product += lax.dot_general(other_rows, other_weight, last_dims, preferred_element_type=F32)
+    product = lax.dot_general(
+        jnp.concatenate([own_rows, other_rows], axis=1),
+        jnp.concatenate([value_weight, other_weight], axis=1),
+        last_dims, preferred_element_type=F32,
+    )
     product = product.astype(BF16).reshape(SHARDS, CHIPS, 16, rows)
     outs = [product[:, j].reshape(SHARDS * 16, rows) for j in range(CHIPS)]
     hidden = [outs[0], None, None, None]
@@ -233,7 +236,15 @@
     packed = outer_packing(pseudo_grad)
     grads = lax.all_to_all(packed, "replica", 0, 0, tiled=True)
 
-    partial_values = jnp.dot(normed, value_weight, preferred_element_type=F32).astype(BF16)
+    halves = value_weight.reshape(CORES, rows // CORES, cols)
+    partial_values = jnp.dot(
+        mine, lax.dynamic_index_in_dim(halves, core, 0, keepdims=False), preferred_element_type=F32
+    )
+    partial_values += jnp.dot(
+        theirs, lax.dynamic_index_in_dim(halves, 1 - core, 0, keepdims=False),
+        preferred_element_type=F32,
+    )
+    partial_values = partial_values.astype(BF16)
     weight_grad = lax.dot_general(
         normed, own_cots.reshape(SHARDS * tokens, cols),
         (((0,), (0,)), ((), ())), preferred_element_type=F32,

time: 111 us -> 114 us (1.027)
  waiting for transfers between devices: 37.3 us -> 40.2 us
  matrix products: 7.62 us -> 9.33 us
  local copies, waits for them, and re-layouts: 4.01 us -> 2.48 us
    all_to_all x1, waiting for transfers between devices: 4.03 us -> 6.55 us  [body(): lax.all_to_all(spread, ('shard', 'tensor'), 0, 0, axis_index_groups=near,...]
    dot_general x3, matrix products: 4.13 us -> 5.57 us  [the longest x1 2.28 us: body(): lax.dot_general(jnp.concatenate([own_rows, other_rows], axis=1), jnp.conc...]
  transfers between devices with their start and end apart: 11 -> 11, of which waited for: 5 -> 5; matrix products, arithmetic and copies ran while one was open for 8% -> 8% of each run, Pallas kernels for 6% -> 3%
where the time goes in v7:
time: 114 us; the launch traced here: 113 us
  starting transfers between devices  51.3 us (45%)
  waiting for transfers between devices  40.2 us (35%)
  matrix products  9.33 us (8%)
  Pallas kernels  9.18 us (8%)
  local copies, waits for them, and re-layouts  2.48 us (2%)
    ppermute x3, waiting for transfers between devices, body(): hidden[j] = lax.ppermute(outs[j], 'tensor', chip_shift(j))  21.7 us
    all_to_all x1, starting transfers between devices, body(): grads = lax.all_to_all(packed, 'replica', 0, 0, tiled=True)  16.4 us
    ppermute x3, starting transfers between devices, body(): hidden[j] = lax.ppermute(outs[j], 'tensor', chip_shift(j))  12.4 us
    all_to_all x1, waiting for transfers between devices, body(): mine = lax.all_to_all(sent, 'shard', 0, 0, tiled=True)  11.7 us
    ppermute x3, starting transfers between devices, body(): got[k] = lax.ppermute(merged[k], 'shard', shard_shift(k))  10.4 us
    all_to_all x1, waiting for transfers between devices, body(): lax.all_to_all(spread, ('shard', 'tensor'), 0, 0, axis_index_groups=near,...  6.55 us
    all_to_all x1, starting transfers between devices, body(): mine = lax.all_to_all(sent, 'shard', 0, 0, tiled=True)  4.42 us
    pallas_call x1, Pallas kernels, body(): sent, = packing(idx, inputs, gains)  3.97 us
  transfers between devices with their start and end apart: 11, of which 5 were waited for; matrix products, arithmetic and copies ran while one was open for 8% of the time, Pallas kernels for 3%

profile of v7, /device:TPU:16, one launch (start us, length us, event | category | flops | bytes accessed | tf_op | source)
XLA Modules:
  0.0 113.5 jit_solution(9002022469843565268)
XLA Ops:
  0.7 0.1 pad_add_fusion.idx
  0.7 1.6 %copy-done = bf16[128,8192]{1,0:T(8,128)(2,1)S(1)} copy-done((bf16[128,8192]{1,0:T(8,128)(2,1)S(1)}, bf16[128,8192]{1,0:T(8,128)(2,1)}, u32[]{:S(2)}) %copy-start) | copy-done | bytes 2097176
  2.3 0.7 copy-done.3
  3.0 4.0 %pack.1 = bf16[4,128,1024]{2,1,0:T(8,128)(2,1)} custom-call(s32[4]{0:T(128)S(1)} %pad_add_fusion.idx, bf16[128,8192]{1,0:T(8,128)(2,1)S(1)} %copy-done, bf16[64,128]{1,0:T(8,128)(2,1)S(1)} %bitcast.36), custom_call_target="tpu_custom_call" | custom-call | flops 6000000 | bytes 4300000 | tf_op jit(solution)/shard_map/pack/pallas_call | solution.py:193
  7.0 4.4 %all-to-all-start.1 = ((bf16[4,128,1024]{2,1,0:T(8,128)(2,1)}), bf16[4,128,1024]{2,1,0:T(8,128)(2,1)S(1)}, u32[]{:S(2)}, u32[]{:S(2)}) async-start(bf16[4,128,1024]{2,1,0:T(8,128)(2,1)} %pack.1), calls=%async_computation.1 | async-start | bytes 2097152 | tf_op jit(solution)/shard_map/all_to_all | solution.py:194
  11.4 1.9 %collective-permute-start = (bf16[2048,256]{1,0:T(8,128)(2,1)}, bf16[2048,256]{1,0:T(8,128)(2,1)}, u32[]{:S(2)}, u32[]{:S(2)}) collective-permute-start(bf16[2048,256]{1,0:T(8,128)(2,1)} %param.9), channel_id=1, source_target_pairs={{0,1},{1,0},{2,3},{3,2},{4,5},{5,4},{6,7},{7,6},{8,9},{9,8},{10,11... | collective-permute-start | bytes 3145736 | tf_op jit(solution)/shard_map/ppermute | solution.py:173
  13.4 0.0 copy-done.5
  13.4 1.4 %spread.1 = bf16[8,128,256]{2,1,0:T(8,128)(2,1)} custom-call(s32[4]{0:T(128)S(1)} %pad_add_fusion.idx, bf16[128,256]{1,0:T(8,128)(2,1)S(1)} %copy-done.5), custom_call_target="tpu_custom_call" | custom-call | bytes 600000 | tf_op jit(solution)/shard_map/spread/pallas_call | solution.py:159
  14.8 11.7 %all-to-all-done.1 = bf16[4,128,1024]{2,1,0:T(8,128)(2,1)S(1)} async-done(((bf16[4,128,1024]{2,1,0:T(8,128)(2,1)}), bf16[4,128,1024]{2,1,0:T(8,128)(2,1)S(1)}, u32[]{:S(2)}, u32[]{:S(2)}) %all-to-all-start.1) | async-done | bytes 1048608 | tf_op jit(solution)/shard_map/all_to_all | solution.py:194
  26.5 3.5 %all-to-all-start = ((bf16[8,128,256]{2,1,0:T(8,128)(2,1)}), bf16[8,128,256]{2,1,0:T(8,128)(2,1)S(1)}, u32[]{:S(2)}, u32[]{:S(2)}) async-start(bf16[8,128,256]{2,1,0:T(8,128)(2,1)} %spread.1), calls=%async_computation | async-start | bytes 1048576 | tf_op jit(solution)/shard_map/all_to_all | solution.py:170
  30.1 0.0 copy-done.2
  30.1 1.4 %outerpack.1 = bf16[24,64,128]{2,1,0:T(8,128)(2,1)} custom-call(f32[1,64,3072]{2,1,0:T(8,128)S(1)} %copy-done.2), custom_call_target="tpu_custom_call" | custom-call | bytes 1200000 | tf_op jit(solution)/shard_map/outerpack/pallas_call | solution.py:236
  31.5 2.3 %collective-permute-start.4 = (bf16[512,1024]{1,0:T(8,128)(2,1)S(1)}, bf16[512,1024]{1,0:T(8,128)(2,1)}, u32[]{:S(2)}, u32[]{:S(2)}) collective-permute-start(bf16[512,1024]{1,0:T(8,128)(2,1)S(1)} %bitcast.38), channel_id=1, source_target_pairs={{0,1},{1,0},{2,3},{3,2},{4,5},{5,4},{6,7},{7,6},{8,9},{9,8},{10,11... | collective-permute-start | bytes 3145736 | tf_op jit(solution)/shard_map/ppermute | solution.py:196
  33.7 6.6 %all-to-all-done = bf16[8,128,256]{2,1,0:T(8,128)(2,1)S(1)} async-done(((bf16[8,128,256]{2,1,0:T(8,128)(2,1)}), bf16[8,128,256]{2,1,0:T(8,128)(2,1)S(1)}, u32[]{:S(2)}, u32[]{:S(2)}) %all-to-all-start) | async-done | bytes 524320 | tf_op jit(solution)/shard_map/all_to_all | solution.py:170
  40.3 16.4 %all-to-all-start.2 = ((bf16[24,64,128]{2,1,0:T(8,128)(2,1)}), bf16[24,64,128]{2,1,0:T(8,128)(2,1)S(1)}, u32[]{:S(2)}, u32[]{:S(2)}) async-start(bf16[24,64,128]{2,1,0:T(8,128)(2,1)} %outerpack.1), calls=%async_computation.2 | async-start | bytes 786432 | tf_op jit(solution)/shard_map/all_to_all | solution.py:237
  56.7 1.5 %fusion.12 = f32[512,256]{1,0:T(8,128)S(1)} fusion(bf16[512,1024]{1,0:T(8,128)(2,1)S(1)} %bitcast.39, bf16[2,1024,256]{2,1,0:T(8,128)(2,1)} %bitcast.14, s32[]{:T(128)S(6)} %select_n.40), kind=kOutput, calls=%fused_computation.16 | convolution fusion | flops 268435456 | bytes 2097156 | tf_op jit(solution)/shard_map/dot_general | solution.py:240
  58.2 0.0 copy-done.8
  58.3 0.0 collective-permute-done
  58.3 2.3 %convolution_convert_fusion.1 = bf16[256,2048]{1,0:T(8,128)(2,1)S(1)} fusion(bf16[2048,256]{1,0:T(8,128)(2,1)} %collective-permute-done, bf16[2048,256]{1,0:T(8,128)(2,1)} %param.9, bf16[256,256]{1,0:T(8,128)(2,1)S(1)} %bitcast.49, bf16[256,256]{1,0:T(8,128)(2,1)S(1)} %bitcast.48), kind=kOutput, calls=%fused_computation.1 | convolution fusion | flops 542113792 | bytes 3407872 | tf_op jit(solution)/shard_map/dot_general | solution.py:216
  60.6 0.1 fusion.23
  60.6 0.0 copy-start.9
  60.6 2.4 %collective-permute-start.1 = (bf16[64,2048]{1,0:T(8,128)(2,1)S(1)}, bf16[64,2048]{1,0:T(8,128)(2,1)S(1)}, u32[]{:S(2)}, u32[]{:S(2)}) collective-permute-start(bf16[64,2048]{1,0:T(8,128)(2,1)S(1)} %bitcast.47), channel_id=1, source_target_pairs={{0,2},{1,3},{2,0},{3,1},{4,6},{5,7},{6,4},{7,5},{8,10},{9,11},{10,... | collective-permute-start | bytes 786440 | tf_op jit(solution)/shard_map/ppermute | solution.py:225
  63.0 6.8 %collective-permute-start.2 = (bf16[64,2048]{1,0:T(8,128)(2,1)S(1)}, bf16[64,2048]{1,0:T(8,128)(2,1)S(1)}, u32[]{:S(2)}, u32[]{:S(2)}) collective-permute-start(bf16[64,2048]{1,0:T(8,128)(2,1)S(1)} %bitcast.46), channel_id=1, source_target_pairs={{0,4},{1,5},{2,6},{3,7},{4,0},{5,1},{6,2},{7,3},{8,12},{9,13},{10,... | collective-permute-start | bytes 786440 | tf_op jit(solution)/shard_map/ppermute | solution.py:225
  69.9 3.1 %collective-permute-start.3 = (bf16[64,2048]{1,0:T(8,128)(2,1)S(1)}, bf16[64,2048]{1,0:T(8,128)(2,1)S(1)}, u32[]{:S(2)}, u32[]{:S(2)}) collective-permute-start(bf16[64,2048]{1,0:T(8,128)(2,1)S(1)} %bitcast.45), channel_id=1, source_target_pairs={{0,6},{1,7},{2,4},{3,5},{4,2},{5,3},{6,0},{7,1},{8,14},{9,15},{10,... | collective-permute-start | bytes 786440 | tf_op jit(solution)/shard_map/ppermute | solution.py:225
  73.0 0.0 collective-permute-done.4
  73.0 1.8 %fusion.10.values = bf16[512,256]{1,0:T(8,128)(2,1)S(1)} fusion(f32[512,256]{1,0:T(8,128)S(1)} %fusion.12, bf16[512,1024]{1,0:T(8,128)(2,1)} %collective-permute-done.4, bf16[2,1024,256]{2,1,0:T(8,128)(2,1)} %bitcast.14, s32[]{:T(128)S(6)} %select_n.42), kind=kOutput, calls=%fused_computation.14 | convolution fusion | flops 268697600 | bytes 2359300 | tf_op jit(solution)/shard_map/dot_general | solution.py:243
  74.8 7.4 %collective-permute-done.1.r1 = bf16[64,2048]{1,0:T(8,128)(2,1)S(1)} collective-permute-done((bf16[64,2048]{1,0:T(8,128)(2,1)S(1)}, bf16[64,2048]{1,0:T(8,128)(2,1)S(1)}, u32[]{:S(2)}, u32[]{:S(2)}) %collective-permute-start.1) | collective-permute-done | bytes 262176 | tf_op jit(solution)/shard_map/ppermute | solution.py:225
  82.2 0.0 collective-permute-done.2.r2
  82.2 14.3 %collective-permute-done.3.r3 = bf16[64,2048]{1,0:T(8,128)(2,1)S(1)} collective-permute-done((bf16[64,2048]{1,0:T(8,128)(2,1)S(1)}, bf16[64,2048]{1,0:T(8,128)(2,1)S(1)}, u32[]{:S(2)}, u32[]{:S(2)}) %collective-permute-start.3) | collective-permute-done | bytes 262176 | tf_op jit(solution)/shard_map/ppermute | solution.py:225
  96.5 0.7 merge.1
  97.2 2.5 %collective-permute-start.5 = (bf16[256,256]{1,0:T(8,128)(2,1)S(1)}, bf16[256,256]{1,0:T(8,128)(2,1)S(1)}, u32[]{:S(2)}, u32[]{:S(2)}) collective-permute-start(bf16[256,256]{1,0:T(8,128)(2,1)S(1)} %get-tuple-element.14), channel_id=1, source_target_pairs={{0,8},{8,0},{16,24},{24,16},{1,9},{9,1},{17,25},{25,17},{2,10},{10... | collective-permute-start | bytes 393224 | tf_op jit(solution)/shard_map/ppermute | solution.py:265
  99.7 4.0 %collective-permute-start.6 = (bf16[256,256]{1,0:T(8,128)(2,1)S(1)}, bf16[256,256]{1,0:T(8,128)(2,1)S(1)}, u32[]{:S(2)}, u32[]{:S(2)}) collective-permute-start(bf16[256,256]{1,0:T(8,128)(2,1)S(1)} %get-tuple-element.15), channel_id=1, source_target_pairs={{0,16},{8,24},{16,0},{24,8},{1,17},{9,25},{17,1},{25,9},{2,18},{10... | collective-permute-start | bytes 393224 | tf_op jit(solution)/shard_map/ppermute | solution.py:265
  103.7 4.0 %collective-permute-start.7 = (bf16[256,256]{1,0:T(8,128)(2,1)S(1)}, bf16[256,256]{1,0:T(8,128)(2,1)S(1)}, u32[]{:S(2)}, u32[]{:S(2)}) collective-permute-start(bf16[256,256]{1,0:T(8,128)(2,1)S(1)} %get-tuple-element.16), channel_id=1, source_target_pairs={{0,24},{8,16},{16,8},{24,0},{1,25},{9,17},{17,9},{25,1},{2,26},{10... | collective-permute-start | bytes 393224 | tf_op jit(solution)/shard_map/ppermute | solution.py:265
  107.7 0.0 copy-done.9
  107.7 0.0 copy-start.1
  107.7 0.0 copy-start.4
  107.7 0.0 copy-start.6
  107.7 0.0 copy-start.7
  107.7 3.8 %fusion = bf16[1,2048,256]{2,1,0:T(8,128)(2,1)} fusion(bf16[512,256]{1,0:T(8,128)(2,1)S(1)} %bitcast.44, bf16[512,1024]{1,0:T(8,128)(2,1)} %collective-permute-done.4, bf16[512,1024]{1,0:T(8,128)(2,1)S(1)} %bitcast.40, pred[]{:T(512)S(6)} %eq.7), kind=kOutput, calls=%fused_computation.2 | convolution fusion | flops 546832384 | bytes 3407873 | tf_op jit(solution)/shard_map/dot_general | solution.py:248
  111.5 0.0 all-to-all-done.2.grads
  111.5 0.0 collective-permute-done.5.m1
  111.5 0.0 collective-permute-done.6.m2
  111.5 0.2 collective-permute-done.7.m3
  111.7 0.0 copy-done.1
  111.7 0.0 copy-done.4
  111.7 0.0 copy-done.6
  111.7 0.0 copy-done.7
  111.8 1.7 %final.1 = (bf16[16,8192]{1,0:T(8,128)(2,1)}, bf16[128,256]{1,0:T(8,128)(2,1)}, f32[64,128]{1,0:T(8,128)}, f32[64,128]{1,0:T(8,128)}) custom-call(s32[4]{0:T(128)S(1)} %pad_add_fusion.idx, bf16[256,256]{1,0:T(8,128)(2,1)S(1)} %get-tuple-element.13.m0, bf16[256,256]{1,0:T(8,128)(2,1)S(1)} %collective-permute-done.5.m1, ...), custom_call_target="tpu_custom_call" | custom-call | flops 2000000 | bytes 2100000 | tf_op jit(solution)/shard_map/final/pallas_call | solution.py:267
  (7 shorter events, 0.1 us)
Async XLA Ops:
  0.7 1.6 %copy-start = (bf16[128,8192]{1,0:T(8,128)(2,1)S(1)}, bf16[128,8192]{1,0:T(8,128)(2,1)}, u32[]{:S(2)}) copy-start(bf16[128,8192]{1,0:T(8,128)(2,1)} %x_ref.7) | copy-start | bytes 6291460
  2.3 0.7 copy-start.3
  3.0 10.3 %copy-start.5 = (bf16[128,256]{1,0:T(8,128)(2,1)S(1)}, bf16[128,256]{1,0:T(8,128)(2,1)}, u32[]{:S(2)}) copy-start(bf16[128,256]{1,0:T(8,128)(2,1)} %x_ref.4) | copy-start | bytes 196612
  7.0 23.0 %copy-start.2 = (f32[1,64,3072]{2,1,0:T(8,128)S(1)}, f32[1,64,3072]{2,1,0:T(8,128)}, u32[]{:S(2)}) copy-start(f32[1,64,3072]{2,1,0:T(8,128)} %x_ref.6) | copy-start | bytes 2359300
  7.0 19.5 %all-to-all-start.1 = ((bf16[4,128,1024]{2,1,0:T(8,128)(2,1)}), bf16[4,128,1024]{2,1,0:T(8,128)(2,1)S(1)}, u32[]{:S(2)}, u32[]{:S(2)}) async-start(bf16[4,128,1024]{2,1,0:T(8,128)(2,1)} %pack.1), calls=%async_computation.1 | async-start | bytes 2097152 | tf_op jit(solution)/shard_map/all_to_all | solution.py:194
  11.4 46.8 %collective-permute-start = (bf16[2048,256]{1,0:T(8,128)(2,1)}, bf16[2048,256]{1,0:T(8,128)(2,1)}, u32[]{:S(2)}, u32[]{:S(2)}) collective-permute-start(bf16[2048,256]{1,0:T(8,128)(2,1)} %param.9), channel_id=1, source_target_pairs={{0,1},{1,0},{2,3},{3,2},{4,5},{5,4},{6,7},{7,6},{8,9},{9,8},{10,11... | collective-permute-start | bytes 3145736 | tf_op jit(solution)/shard_map/ppermute | solution.py:173
  26.5 31.7 %copy-start.8 = (bf16[4,128,1024]{2,1,0:T(8,128)(2,1)}, bf16[4,128,1024]{2,1,0:T(8,128)(2,1)S(1)}, u32[]{:S(2)}) copy-start(bf16[4,128,1024]{2,1,0:T(8,128)(2,1)S(1)} %all-to-all-done.1) | copy-start | bytes 3145732
  26.5 13.7 %all-to-all-start = ((bf16[8,128,256]{2,1,0:T(8,128)(2,1)}), bf16[8,128,256]{2,1,0:T(8,128)(2,1)S(1)}, u32[]{:S(2)}, u32[]{:S(2)}) async-start(bf16[8,128,256]{2,1,0:T(8,128)(2,1)} %spread.1), calls=%async_computation | async-start | bytes 1048576 | tf_op jit(solution)/shard_map/all_to_all | solution.py:170
  31.5 41.6 %collective-permute-start.4 = (bf16[512,1024]{1,0:T(8,128)(2,1)S(1)}, bf16[512,1024]{1,0:T(8,128)(2,1)}, u32[]{:S(2)}, u32[]{:S(2)}) collective-permute-start(bf16[512,1024]{1,0:T(8,128)(2,1)S(1)} %bitcast.38), channel_id=1, source_target_pairs={{0,1},{1,0},{2,3},{3,2},{4,5},{5,4},{6,7},{7,6},{8,9},{9,8},{10,11... | collective-permute-start | bytes 3145736 | tf_op jit(solution)/shard_map/ppermute | solution.py:196
  40.3 71.2 %all-to-all-start.2 = ((bf16[24,64,128]{2,1,0:T(8,128)(2,1)}), bf16[24,64,128]{2,1,0:T(8,128)(2,1)S(1)}, u32[]{:S(2)}, u32[]{:S(2)}) async-start(bf16[24,64,128]{2,1,0:T(8,128)(2,1)} %outerpack.1), calls=%async_computation.2 | async-start | bytes 786432 | tf_op jit(solution)/shard_map/all_to_all | solution.py:237
  60.6 47.0 %copy-start.9 = (bf16[4,128,1024]{2,1,0:T(8,128)(2,1)S(1)}, bf16[4,128,1024]{2,1,0:T(8,128)(2,1)}, u32[]{:S(2)}) copy-start(bf16[4,128,1024]{2,1,0:T(8,128)(2,1)} %copy-done.8) | copy-start | bytes 3145732
  60.6 21.6 %collective-permute-start.1 = (bf16[64,2048]{1,0:T(8,128)(2,1)S(1)}, bf16[64,2048]{1,0:T(8,128)(2,1)S(1)}, u32[]{:S(2)}, u32[]{:S(2)}) collective-permute-start(bf16[64,2048]{1,0:T(8,128)(2,1)S(1)} %bitcast.47), channel_id=1, source_target_pairs={{0,2},{1,3},{2,0},{3,1},{4,6},{5,7},{6,4},{7,5},{8,10},{9,11},{10,... | collective-permute-start | bytes 786440 | tf_op jit(solution)/shard_map/ppermute | solution.py:225
  63.0 19.2 %collective-permute-start.2 = (bf16[64,2048]{1,0:T(8,128)(2,1)S(1)}, bf16[64,2048]{1,0:T(8,128)(2,1)S(1)}, u32[]{:S(2)}, u32[]{:S(2)}) collective-permute-start(bf16[64,2048]{1,0:T(8,128)(2,1)S(1)} %bitcast.46), channel_id=1, source_target_pairs={{0,4},{1,5},{2,6},{3,7},{4,0},{5,1},{6,2},{7,3},{8,12},{9,13},{10,... | collective-permute-start | bytes 786440 | tf_op jit(solution)/shard_map/ppermute | solution.py:225
  69.9 26.7 %collective-permute-start.3 = (bf16[64,2048]{1,0:T(8,128)(2,1)S(1)}, bf16[64,2048]{1,0:T(8,128)(2,1)S(1)}, u32[]{:S(2)}, u32[]{:S(2)}) collective-permute-start(bf16[64,2048]{1,0:T(8,128)(2,1)S(1)} %bitcast.45), channel_id=1, source_target_pairs={{0,6},{1,7},{2,4},{3,5},{4,2},{5,3},{6,0},{7,1},{8,14},{9,15},{10,... | collective-permute-start | bytes 786440 | tf_op jit(solution)/shard_map/ppermute | solution.py:225
  97.2 14.3 %collective-permute-start.5 = (bf16[256,256]{1,0:T(8,128)(2,1)S(1)}, bf16[256,256]{1,0:T(8,128)(2,1)S(1)}, u32[]{:S(2)}, u32[]{:S(2)}) collective-permute-start(bf16[256,256]{1,0:T(8,128)(2,1)S(1)} %get-tuple-element.14), channel_id=1, source_target_pairs={{0,8},{8,0},{16,24},{24,16},{1,9},{9,1},{17,25},{25,17},{2,10},{10... | collective-permute-start | bytes 393224 | tf_op jit(solution)/shard_map/ppermute | solution.py:265
  99.7 11.8 %collective-permute-start.6 = (bf16[256,256]{1,0:T(8,128)(2,1)S(1)}, bf16[256,256]{1,0:T(8,128)(2,1)S(1)}, u32[]{:S(2)}, u32[]{:S(2)}) collective-permute-start(bf16[256,256]{1,0:T(8,128)(2,1)S(1)} %get-tuple-element.15), channel_id=1, source_target_pairs={{0,16},{8,24},{16,0},{24,8},{1,17},{9,25},{17,1},{25,9},{2,18},{10... | collective-permute-start | bytes 393224 | tf_op jit(solution)/shard_map/ppermute | solution.py:265
  103.7 8.1 %collective-permute-start.7 = (bf16[256,256]{1,0:T(8,128)(2,1)S(1)}, bf16[256,256]{1,0:T(8,128)(2,1)S(1)}, u32[]{:S(2)}, u32[]{:S(2)}) collective-permute-start(bf16[256,256]{1,0:T(8,128)(2,1)S(1)} %get-tuple-element.16), channel_id=1, source_target_pairs={{0,24},{8,16},{16,8},{24,0},{1,25},{9,17},{17,9},{25,1},{2,26},{10... | collective-permute-start | bytes 393224 | tf_op jit(solution)/shard_map/ppermute | solution.py:265
  107.7 4.1 %copy-start.1 = (bf16[128,8192]{1,0:T(8,128)(2,1)S(1)}, bf16[128,8192]{1,0:T(8,128)(2,1)}, u32[]{:S(2)}) copy-start(bf16[128,8192]{1,0:T(8,128)(2,1)} %x_ref.7) | copy-start | bytes 6291460
  107.7 4.1 %copy-start.4 = (bf16[8192]{0:T(1024)(128)(2,1)S(1)}, bf16[8192]{0:T(1024)(128)(2,1)}, u32[]{:S(2)}) copy-start(bf16[8192]{0:T(1024)(128)(2,1)} %param.8) | copy-start | bytes 49156
  107.7 4.0 %copy-start.6 = (f32[64,128]{1,0:T(8,128)S(1)}, f32[64,128]{1,0:T(8,128)}, u32[]{:S(2)}) copy-start(f32[64,128]{1,0:T(8,128)} %p_ref.1) | copy-start | bytes 98308
  107.7 4.0 %copy-start.7 = (f32[64,128]{1,0:T(8,128)S(1)}, f32[64,128]{1,0:T(8,128)}, u32[]{:S(2)}) copy-start(f32[64,128]{1,0:T(8,128)} %q_ref.1) | copy-start | bytes 98308
